TPU v7x, 256 devices: a whole 4x4x8 slice. The times are simulated.
256 devices in a mesh: expert: 64 (over z, x, core), tensor: 4 (over y).
Axes of the slice: x: 4, y: 4, z: 8, core: 2. Of those that a mesh axis runs over, the one named last changes fastest.
Arguments:
- tokens: bfloat16 [2048, 4096], P('expert', 'tensor'), may hold values from -6 to 6
- cotangent: bfloat16 [2048, 4096], P('expert', 'tensor'), may hold values from -6 to 6
- routing: int32 [2048, 8], P('expert'), may hold values from 0 to 63, as said below
- gates: float32 [2048, 8], P('expert'), may hold values from 0.1 to 0.4
- w_in: bfloat16 [64, 4096, 1536], P('expert', None, 'tensor'), may hold values from -0.09375 to 0.09375
- w_out: bfloat16 [64, 1536, 4096], P('expert', 'tensor'), may hold values from -0.15625 to 0.15625
Outputs:
- mixed: bfloat16 [2048, 4096], P('expert', 'tensor')
- d_tokens: bfloat16 [2048, 4096], P('expert', 'tensor')
- d_w_in: bfloat16 [64, 4096, 1536], P('expert', None, 'tensor')
- d_w_out: bfloat16 [64, 1536, 4096], P('expert', 'tensor')
Inputs may be any that keep to these rules, and one draw needn't show every extreme that they name: `routing`: each row names 8 different experts. In each aligned block of 32 rows (the tokens of one index of the expert axis) no expert is named by more than 8 rows, and one expert is named by exactly 8 rows of every block.
All inputs are finite; a program needn't handle non-finite values.
Results may differ from a plain program's by a relative error of at most 0.0058.
Values may be sent and summed in bfloat16 or wider, within the bound.
A program may use at most 128 MiB of HBM per device.

v0:
```python
import jax
import jax.numpy as jnp
from jax import lax
from jax.sharding import PartitionSpec as P


def shards(tokens, cotangent, routing, gates, w_in, w_out):
    devices = lax.axis_size("expert")
    local_experts = w_in.shape[0]
    experts = devices * local_experts
    tok_rows = routing.shape[0]
    capacity = tok_rows // 4
    buffer_rows = experts * capacity
    highest = lax.Precision.HIGHEST
    matches = (routing[:, :, None] == jnp.arange(experts, dtype=jnp.int32)[None, None, :]).astype(
        jnp.int32
    )
    per_token = jnp.sum(matches, axis=1)
    earlier = jnp.cumsum(per_token, axis=0) - per_token
    destination = routing * capacity + jnp.take_along_axis(earlier, routing, axis=1)
    placed = (
        destination[:, :, None] == jnp.arange(buffer_rows, dtype=jnp.int32)[None, None, :]
    ).astype(jnp.float32)
    membership = jnp.sum(placed, axis=1)
    weighting = jnp.sum(placed * gates[:, :, None], axis=1)
    whole_tokens, whole_cot = (
        lax.all_gather(tokens, "tensor", axis=1, tiled=True),
        lax.all_gather(cotangent, "tensor", axis=1, tiled=True),
    )
    width = whole_tokens.shape[1]
    rows = jnp.einsum(
        "tr,td->rd",
        membership.astype(jnp.bfloat16),
        whole_tokens,
        preferred_element_type=jnp.float32,
    ).astype(jnp.bfloat16)
    scaled = jnp.einsum(
        "tr,td->rd", weighting, whole_cot.astype(jnp.float32), precision=highest
    ).astype(jnp.bfloat16)
    send_rows = rows.reshape(devices, local_experts, capacity, width)
    send_scaled = scaled.reshape(devices, local_experts, capacity, width)
    expert_rows, expert_scaled = (
        lax.all_to_all(send_rows, "expert", split_axis=0, concat_axis=0, tiled=True),
        lax.all_to_all(send_scaled, "expert", split_axis=0, concat_axis=0, tiled=True),
    )
    preact = jnp.einsum("nesd,edh->nesh", expert_rows, w_in, preferred_element_type=jnp.float32)
    sigmoid_val = jax.nn.sigmoid(preact)
    hidden = (preact * sigmoid_val).astype(jnp.bfloat16)
    out_part = jnp.einsum("nesh,ehd->nesd", hidden, w_out, preferred_element_type=jnp.float32)
    grad_hidden = jnp.einsum(
        "nesd,ehd->nesh", expert_scaled, w_out, preferred_element_type=jnp.float32
    )
    grad_preact = (grad_hidden * sigmoid_val * (1.0 + preact * (1.0 - sigmoid_val))).astype(
        jnp.bfloat16
    )
    d_w_out = jnp.einsum(
        "nesh,nesd->ehd", hidden, expert_scaled, preferred_element_type=jnp.float32
    ).astype(jnp.bfloat16)
    d_w_in = jnp.einsum(
        "nesd,nesh->edh", expert_rows, grad_preact, preferred_element_type=jnp.float32
    ).astype(jnp.bfloat16)
    grad_part = jnp.einsum("nesh,edh->nesd", grad_preact, w_in, preferred_element_type=jnp.float32)
    out_sums, grad_sums = (
        lax.psum_scatter(out_part, "tensor", scatter_dimension=3, tiled=True),
        lax.psum_scatter(grad_part, "tensor", scatter_dimension=3, tiled=True),
    )
    back_out, back_grad = (
        lax.all_to_all(out_sums, "expert", split_axis=0, concat_axis=0, tiled=True),
        lax.all_to_all(grad_sums, "expert", split_axis=0, concat_axis=0, tiled=True),
    )
    width_q = back_out.shape[3]
    mixed = jnp.einsum(
        "tr,rd->td", weighting, back_out.reshape(buffer_rows, width_q), precision=highest
    ).astype(jnp.bfloat16)
    d_tokens = jnp.einsum(
        "tr,rd->td", membership, back_grad.reshape(buffer_rows, width_q), precision=highest
    ).astype(jnp.bfloat16)
    return (mixed, d_tokens, d_w_in, d_w_out)


def solution(mesh):
    placed = (
        P("expert", "tensor"),
        P("expert", "tensor"),
        P("expert", None),
        P("expert", None),
        P("expert", None, "tensor"),
        P("expert", "tensor", None),
    )
    return jax.shard_map(
        shards,
        mesh=mesh,
        in_specs=placed,
        out_specs=(
            P("expert", "tensor"),
            P("expert", "tensor"),
            P("expert", None, "tensor"),
            P("expert", "tensor", None),
        ),
        check_vma=False,
    )
```

profile of v0, /device:TPU:7, one launch (start us, length us, event | category | flops | bytes accessed | tf_op | source)
XLA Modules:
  0.0 421.8 jit_solution(5423124009950122582)
XLA Ops:
  7.2 0.8 bitcast_or_fusion
  8.1 0.8 copy.47
  9.1 0.8 copy.51
  10.0 1.9 gather_fusion
  12.2 10.4 %all_gather.6 = bf16[32,4096]{1,0:T(8,128)(2,1)S(1)} all-gather(bf16[32,1024]{1,0:T(8,128)(2,1)S(1)} %copy-done.8), channel_id=1, replica_groups=mesh['expert'=64,'tensor'=4] {'tensor'}, dimensions={1}, use_global_device_ids=true | all-gather | bytes 327680 | tf_op jit(solution)/shard_map/all_gather | solution.py:27
  23.0 1.3 fusion
  24.3 109.3 %all_to_all.20 = bf16[64,1,8,4096]{3,2,1,0:T(8,128)(2,1)S(1)} all-to-all(bf16[64,1,8,4096]{3,2,1,0:T(8,128)(2,1)S(1)} %fusion), channel_id=1, replica_groups=mesh['expert'=64,'tensor'=4] {'expert'}, dimensions={0} | all-to-all | bytes 8388608 | tf_op jit(solution)/shard_map/all_to_all | solution.py:43
  133.6 2.3 fusion.18
  136.0 0.9 copy-done.5
  136.8 5.6 %convolution_bitcast_fusion.1 = f32[64,1,8,4096]{3,2,0,1:T(8,128)} fusion(bf16[1,384,4096]{2,1,0:T(8,128)(2,1)S(1)} %copy-done, f32[64,1,8,384]{3,2,0,1:T(8,128)S(1)} %fusion.18), kind=kOutput, calls=%fused_computation.2 | convolution fusion | flops 1611595776 | bytes 12320768 | tf_op jit(solution)/shard_map/nesh,ehd->nesd/dot_general | solution.py:49
  142.5 0.8 copy-done.9
  143.2 9.4 %all_gather.7 = bf16[32,4096]{1,0:T(8,128)(2,1)S(1)} all-gather(bf16[32,1024]{1,0:T(8,128)(2,1)S(1)} %copy-done.9), channel_id=1, replica_groups=mesh['expert'=64,'tensor'=4] {'tensor'}, dimensions={1}, use_global_device_ids=true | all-gather | bytes 327680 | tf_op jit(solution)/shard_map/all_gather | solution.py:28
  152.6 3.7 fusion.1
  156.3 105.4 %all_to_all.21 = bf16[64,1,8,4096]{3,2,1,0:T(8,128)(2,1)S(1)} all-to-all(bf16[64,1,8,4096]{3,2,1,0:T(8,128)(2,1)S(1)} %fusion.1), channel_id=1, replica_groups=mesh['expert'=64,'tensor'=4] {'expert'}, dimensions={0} | all-to-all | bytes 8388608 | tf_op jit(solution)/shard_map/all_to_all | solution.py:44
  261.7 2.4 fusion.43
  265.1 5.6 %convolution_bitcast_fusion = f32[64,1,8,4096]{3,2,0,1:T(8,128)} fusion(bf16[64,8,384]{2,1,0:T(8,128)(2,1)S(1)} %fusion.43, bf16[1,4096,384]{2,1,0:T(8,128)(2,1)S(1)} %copy-done.4), kind=kOutput, calls=%fused_computation.1 | convolution fusion | flops 1610612736 | bytes 11927552 | tf_op jit(solution)/shard_map/nesh,edh->nesd/dot_general | solution.py:62
  270.8 7.3 %all-to-all-start.1 = ((f32[64,1,8,1024]{3,2,1,0:T(8,128)}), f32[64,1,8,1024]{3,2,1,0:T(8,128)}, u32[]{:S(2)}, u32[]{:S(2)}) async-start(f32[64,1,8,1024]{3,2,1,0:T(8,128)} %bitcast.128), calls=%async_computation.2 | async-start | bytes 4194304 | tf_op jit(solution)/shard_map/all_to_all | solution.py:68
  278.0 6.8 %fusion.3 = bf16[1,384,4096]{2,1,0:T(8,128)(2,1)} fusion(bf16[64,1,8,4096]{3,2,1,0:T(8,128)(2,1)} %copy-done.2, f32[64,1,8,384]{3,2,0,1:T(8,128)} %copy-done.5), kind=kOutput, calls=%fused_computation.10 | convolution fusion | flops 1613168640 | bytes 8126464 | tf_op jit(solution)/shard_map/nesh,nesd->ehd/dot_general | solution.py:56
  284.8 66.1 %reduce-scatter.5.cloned.1.call-done = f32[64,1,8,1024]{3,2,0,1:T(8,128)} async-done(((f32[64,1,8,4096]{3,2,0,1:T(8,128)}), f32[64,1,8,1024]{3,2,0,1:T(8,128)}) %reduce-scatter.5.cloned.1.call-update) | async-done | bytes 2097168 | tf_op jit(solution)/shard_map/reduce_scatter | solution.py:65
  350.9 11.0 %all-to-all-start.3 = ((f32[64,1,8,1024]{3,2,1,0:T(8,128)}), f32[64,1,8,1024]{3,2,1,0:T(8,128)}, u32[]{:S(2)}, u32[]{:S(2)}) async-start(f32[64,1,8,1024]{3,2,1,0:T(8,128)} %bitcast.129), calls=%async_computation.5 | async-start | bytes 4194304 | tf_op jit(solution)/shard_map/all_to_all | solution.py:69
  361.9 6.3 %fusion.2 = bf16[1,4096,384]{2,1,0:T(8,128)(2,1)} fusion(bf16[64,8,384]{2,1,0:T(8,128)(2,1)} %copy-done.7, bf16[64,1,8,4096]{3,2,1,0:T(8,128)(2,1)} %copy-done.1), kind=kOutput, calls=%fused_computation.9 | convolution fusion | flops 1612185600 | bytes 7733248 | tf_op jit(solution)/shard_map/nesd,nesh->edh/dot_general | solution.py:59
  368.2 3.5 fusion.48
  371.7 39.7 %all-to-all-done.3 = f32[64,1,8,1024]{3,2,1,0:T(8,128)} async-done(((f32[64,1,8,1024]{3,2,1,0:T(8,128)}), f32[64,1,8,1024]{3,2,1,0:T(8,128)}, u32[]{:S(2)}, u32[]{:S(2)}) %all-to-all-start.3) | async-done | bytes 2097184 | tf_op jit(solution)/shard_map/all_to_all | solution.py:69
  411.4 3.5 fusion.51
  (36 shorter events, 2.1 us)
Async XLA Ops:
  7.2 129.7 %copy-start = (bf16[1,384,4096]{2,1,0:T(8,128)(2,1)S(1)}, bf16[1,384,4096]{2,1,0:T(8,128)(2,1)}, u32[]{:S(2)}) copy-start(bf16[1,384,4096]{2,1,0:T(8,128)(2,1)} %param.11) | copy-start | bytes 9437188
  7.2 263.6 %reduce-scatter.3.cloned.1.call-start = ((), (), s32[]{:S(2)}) async-start(), calls=%async_computation.6 | async-start | bytes 10485760 | tf_op jit(solution)/shard_map/reduce_scatter | solution.py:64
  10.0 2.1 copy-start.10
  10.0 2.2 copy-start.8
  24.3 109.3 %copy-start.3 = (bf16[1,4096,384]{2,1,0:T(8,128)(2,1)S(1)}, bf16[1,4096,384]{2,1,0:T(8,128)(2,1)}, u32[]{:S(2)}) copy-start(bf16[1,4096,384]{2,1,0:T(8,128)(2,1)} %param.10) | copy-start | bytes 9437188
  133.6 2.3 copy-start.1
  136.0 0.9 copy-start.5
  142.4 0.8 copy-start.9
  142.4 208.4 %reduce-scatter.5.cloned.1.call-start = ((), (), s32[]{:S(2)}) async-start(), calls=%async_computation.7 | async-start | bytes 10485760 | tf_op jit(solution)/shard_map/reduce_scatter | solution.py:65
  156.3 105.4 %copy-start.6 = (f32[64,1,8,384]{3,2,0,1:T(8,128)S(1)}, f32[64,1,8,384]{3,2,0,1:T(8,128)}, u32[]{:S(2)}) copy-start(f32[64,1,8,384]{3,2,0,1:T(8,128)} %copy-done.5) | copy-start | bytes 2359300
  261.7 2.5 copy-start.2
  261.7 3.4 copy-start.4
  264.2 0.7 copy-start.7
  270.8 80.1 %all-to-all-start.1 = ((f32[64,1,8,1024]{3,2,1,0:T(8,128)}), f32[64,1,8,1024]{3,2,1,0:T(8,128)}, u32[]{:S(2)}, u32[]{:S(2)}) async-start(f32[64,1,8,1024]{3,2,1,0:T(8,128)} %bitcast.128), calls=%async_computation.2 | async-start | bytes 4194304 | tf_op jit(solution)/shard_map/all_to_all | solution.py:68
  350.9 60.5 %all-to-all-start.3 = ((f32[64,1,8,1024]{3,2,1,0:T(8,128)}), f32[64,1,8,1024]{3,2,1,0:T(8,128)}, u32[]{:S(2)}, u32[]{:S(2)}) async-start(f32[64,1,8,1024]{3,2,1,0:T(8,128)} %bitcast.129), calls=%async_computation.5 | async-start | bytes 4194304 | tf_op jit(solution)/shard_map/all_to_all | solution.py:69
Sparse Core Ops, SparseCore 0:
  142.6 81.0 reduce-scatter.2
  270.8 79.9 reduce-scatter.4
where the time goes:
time: 424 us; the launch traced here: 422 us
  blocking collectives  234 us (55%)
  waiting for transfers between devices  106 us (25%)
  matrix products  41 us (10%)
  starting transfers between devices  18.3 us (4%)
  between operations  14.2 us (3%)
  local copies, waits for them, and re-layouts  6.55 us (2%)
    all_to_all x1, blocking collectives, shards(): lax.all_to_all(send_rows, 'expert', split_axis=0, concat_axis=0, tiled=True)  109 us
    all_to_all x1, blocking collectives, shards(): lax.all_to_all(send_scaled, 'expert', split_axis=0, concat_axis=0, tiled=...  105 us
    reduce_scatter x1, waiting for transfers between devices, shards(): lax.psum_scatter(grad_part, 'tensor', scatter_dimension=3, tiled=True)  66.1 us
    all_to_all x1, waiting for transfers between devices, shards(): lax.all_to_all(grad_sums, 'expert', split_axis=0, concat_axis=0, tiled=True)  39.7 us
    all_to_all x1, starting transfers between devices, shards(): lax.all_to_all(grad_sums, 'expert', split_axis=0, concat_axis=0, tiled=True)  11 us
    all_gather x1, blocking collectives, shards(): lax.all_gather(tokens, 'tensor', axis=1, tiled=True)  10.4 us
    all_gather x1, blocking collectives, shards(): lax.all_gather(cotangent, 'tensor', axis=1, tiled=True)  9.36 us
  transfers between devices with their start and end apart: 4, of which 2 were waited for; matrix products, arithmetic and copies ran while one was open for 7% of the time, Pallas kernels for 0%

commit v1 on v0

--- a/solution.py
+++ b/solution.py
@@ -23,26 +23,27 @@
     ).astype(jnp.float32)
     membership = jnp.sum(placed, axis=1)
     weighting = jnp.sum(placed * gates[:, :, None], axis=1)
-    whole_tokens, whole_cot = (
-        lax.all_gather(tokens, "tensor", axis=1, tiled=True),
-        lax.all_gather(cotangent, "tensor", axis=1, tiled=True),
-    )
-    width = whole_tokens.shape[1]
+    quarter = tokens.shape[1]
     rows = jnp.einsum(
         "tr,td->rd",
         membership.astype(jnp.bfloat16),
-        whole_tokens,
+        tokens,
         preferred_element_type=jnp.float32,
     ).astype(jnp.bfloat16)
     scaled = jnp.einsum(
-        "tr,td->rd", weighting, whole_cot.astype(jnp.float32), precision=highest
+        "tr,td->rd", weighting, cotangent.astype(jnp.float32), precision=highest
     ).astype(jnp.bfloat16)
-    send_rows = rows.reshape(devices, local_experts, capacity, width)
-    send_scaled = scaled.reshape(devices, local_experts, capacity, width)
-    expert_rows, expert_scaled = (
-        lax.all_to_all(send_rows, "expert", split_axis=0, concat_axis=0, tiled=True),
-        lax.all_to_all(send_scaled, "expert", split_axis=0, concat_axis=0, tiled=True),
+    send = jnp.concatenate(
+        [
+            rows.reshape(devices, local_experts, capacity, quarter),
+            scaled.reshape(devices, local_experts, capacity, quarter),
+        ],
+        axis=2,
     )
+    arrived = lax.all_to_all(send, "expert", split_axis=0, concat_axis=0, tiled=True)
+    whole = lax.all_gather(arrived, "tensor", axis=3, tiled=True)
+    expert_rows = whole[:, :, :capacity]
+    expert_scaled = whole[:, :, capacity:]
     preact = jnp.einsum("nesd,edh->nesh", expert_rows, w_in, preferred_element_type=jnp.float32)
     sigmoid_val = jax.nn.sigmoid(preact)
     hidden = (preact * sigmoid_val).astype(jnp.bfloat16)
@@ -60,21 +61,17 @@
         "nesd,nesh->edh", expert_rows, grad_preact, preferred_element_type=jnp.float32
     ).astype(jnp.bfloat16)
     grad_part = jnp.einsum("nesh,edh->nesd", grad_preact, w_in, preferred_element_type=jnp.float32)
-    out_sums, grad_sums = (
-        lax.psum_scatter(out_part, "tensor", scatter_dimension=3, tiled=True),
-        lax.psum_scatter(grad_part, "tensor", scatter_dimension=3, tiled=True),
+    parts = jnp.concatenate(
+        [out_part.astype(jnp.bfloat16), grad_part.astype(jnp.bfloat16)], axis=2
     )
-    back_out, back_grad = (
-        lax.all_to_all(out_sums, "expert", split_axis=0, concat_axis=0, tiled=True),
-        lax.all_to_all(grad_sums, "expert", split_axis=0, concat_axis=0, tiled=True),
+    sums = lax.psum_scatter(parts, "tensor", scatter_dimension=3, tiled=True)
+    back = lax.all_to_all(sums, "expert", split_axis=0, concat_axis=0, tiled=True)
+    back_out = back[:, :, :capacity].reshape(buffer_rows, quarter).astype(jnp.float32)
+    back_grad = back[:, :, capacity:].reshape(buffer_rows, quarter).astype(jnp.float32)
+    mixed = jnp.einsum("tr,rd->td", weighting, back_out, precision=highest).astype(jnp.bfloat16)
+    d_tokens = jnp.einsum("tr,rd->td", membership, back_grad, precision=highest).astype(
+        jnp.bfloat16
     )
-    width_q = back_out.shape[3]
-    mixed = jnp.einsum(
-        "tr,rd->td", weighting, back_out.reshape(buffer_rows, width_q), precision=highest
-    ).astype(jnp.bfloat16)
-    d_tokens = jnp.einsum(
-        "tr,rd->td", membership, back_grad.reshape(buffer_rows, width_q), precision=highest
-    ).astype(jnp.bfloat16)
     return (mixed, d_tokens, d_w_in, d_w_out)
 
 

time: 424 us -> 343 us (0.81)
  blocking collectives: 234 us -> 61.8 us
  waiting for transfers between devices: 106 us -> 205 us
  other arithmetic: 1.41 us -> 9.46 us
  starting transfers between devices: 18.3 us -> 11.2 us
  matrix products: 41 us -> 35.2 us
    all_to_all x2 -> x1, blocking collectives: 215 us -> 61.8 us  [shards(): lax.all_to_all(send, 'expert', split_axis=0, concat_axis=0, tiled=True)]
    all_gather x0 -> x1, waiting for transfers between devices: none -> 83.3 us  [shards(): whole = lax.all_gather(arrived, 'tensor', axis=3, tiled=True)]
    all_gather x2 -> x0, blocking collectives: 19.8 us -> none  [the longest x1 10.4 us: shards(): lax.all_gather(tokens, 'tensor', axis=1, tiled=True)]
    reduce_scatter x2 -> x1, waiting for transfers between devices: 66.1 us -> 78.3 us  [shards(): sums = lax.psum_scatter(parts, 'tensor', scatter_dimension=3, tiled=True)]
    concatenate x0 -> x2, other arithmetic: none -> 8.04 us  [the longest x1 7.8 us: shards(): jnp.concatenate([out_part.astype(jnp.bfloat16), grad_part.astype(jnp.bflo...]
    all_to_all x2 -> x1, starting transfers between devices: 18.2 us -> 11 us  [shards(): lax.all_to_all(sums, 'expert', split_axis=0, concat_axis=0, tiled=True)]
    dot_general x4, matrix products: 12 us -> 6.4 us  [the longest x1 2.46 us: shards(): jnp.einsum('tr,rd->td', membership, back_grad, precision=highest)]
    all_to_all x2 -> x1, waiting for transfers between devices: 39.7 us -> 43.2 us  [shards(): lax.all_to_all(sums, 'expert', split_axis=0, concat_axis=0, tiled=True)]
  transfers between devices with their start and end apart: 4 -> 3, of which waited for: 2 -> 3; matrix products, arithmetic and copies ran while one was open for 7% -> 4% of each run, Pallas kernels for 0% -> 0%
where the time goes in v1:
time: 343 us; the launch traced here: 342 us
  waiting for transfers between devices  205 us (60%)
  blocking collectives  61.8 us (18%)
  matrix products  35.2 us (10%)
  between operations  14.2 us (4%)
  starting transfers between devices  11.2 us (3%)
  other arithmetic  9.46 us (3%)
  local copies, waits for them, and re-layouts  4.89 us (1%)
    all_gather x1, waiting for transfers between devices, shards(): whole = lax.all_gather(arrived, 'tensor', axis=3, tiled=True)  83.3 us
    reduce_scatter x1, waiting for transfers between devices, shards(): sums = lax.psum_scatter(parts, 'tensor', scatter_dimension=3, tiled=True)  78.3 us
    all_to_all x1, blocking collectives, shards(): lax.all_to_all(send, 'expert', split_axis=0, concat_axis=0, tiled=True)  61.8 us
    all_to_all x1, waiting for transfers between devices, shards(): lax.all_to_all(sums, 'expert', split_axis=0, concat_axis=0, tiled=True)  43.2 us
    all_to_all x1, starting transfers between devices, shards(): lax.all_to_all(sums, 'expert', split_axis=0, concat_axis=0, tiled=True)  11 us
    concatenate x1, other arithmetic, shards(): jnp.concatenate([out_part.astype(jnp.bfloat16), grad_part.astype(jnp.bflo...  7.8 us
  transfers between devices with their start and end apart: 3, of which 3 were waited for; matrix products, arithmetic and copies ran while one was open for 4% of the time, Pallas kernels for 0%

profile of v1, /device:TPU:7, one launch (start us, length us, event | category | flops | bytes accessed | tf_op | source)
XLA Modules:
  0.0 341.7 jit_solution(5815221899172722763)
XLA Ops:
  7.2 0.8 bitcast_or_fusion
  8.1 0.8 copy.47
  9.1 0.8 copy.51
  10.0 1.9 gather_fusion
  12.2 0.4 convert_reduce_fusion
  12.6 0.5 fusion.10
  13.1 1.0 fusion.11
  14.2 0.2 pad_maximum_fusion.1
  14.4 61.8 %all_to_all.10 = bf16[64,1,16,1024]{3,2,1,0:T(8,128)(2,1)} all-to-all(bf16[64,1,16,1024]{3,2,1,0:T(8,128)(2,1)S(1)} %pad_maximum_fusion.1), channel_id=1, replica_groups=mesh['expert'=64,'tensor'=4] {'expert'}, dimensions={0} | all-to-all | bytes 4194304 | tf_op jit(solution)/shard_map/all_to_all | solution.py:43
  76.2 0.2 reduce-scatter.2.cloned.1.call-start
  76.5 83.3 %all-gather.2.cloned.1.call-done = bf16[64,1,16,4096]{3,2,0,1:T(8,128)(2,1)} async-done(((bf16[64,1,16,1024]{3,2,0,1:T(8,128)(2,1)}), bf16[64,1,16,4096]{3,2,0,1:T(8,128)(2,1)}) %all-gather.2.cloned.1.call-update) | async-done | bytes 8388624 | tf_op jit(solution)/shard_map/all_gather | solution.py:44
  159.7 5.5 %fusion.18 = f32[64,1,8,384]{3,2,0,1:T(8,128)S(1)} fusion(bf16[1,4096,384]{2,1,0:T(8,128)(2,1)} %param.10, bf16[64,1,16,4096]{3,2,0,1:T(8,128)(2,1)} %all-gather.2.cloned.1.call-done), kind=kOutput, calls=%fused_computation.25 | convolution fusion | flops 1610612736 | bytes 8126464 | tf_op jit(solution)/shard_map/nesd,edh->nesh/dot_general | solution.py:47
  165.3 4.3 %fusion = bf16[64,1,8,4096]{3,2,0,1:T(8,128)(2,1)} fusion(bf16[1,384,4096]{2,1,0:T(8,128)(2,1)S(1)} %copy-done, f32[64,1,8,384]{3,2,0,1:T(8,128)S(1)} %fusion.18), kind=kOutput, calls=%fused_computation.6 | convolution fusion | flops 1613692928 | bytes 8126464 | tf_op jit(solution)/shard_map/nesh,ehd->nesd/dot_general | solution.py:50
  169.7 2.4 fusion.27
  172.1 0.8 copy-done.6
  172.9 4.3 %fusion.1 = bf16[64,1,8,4096]{3,2,0,1:T(8,128)(2,1)} fusion(bf16[64,8,384]{2,1,0:T(8,128)(2,1)S(1)} %fusion.27, bf16[1,4096,384]{2,1,0:T(8,128)(2,1)S(1)} %copy-done.5), kind=kOutput, calls=%fused_computation.7 | convolution fusion | flops 1612709888 | bytes 7733248 | tf_op jit(solution)/shard_map/nesh,edh->nesd/dot_general | solution.py:63
  177.3 7.8 %pad_maximum_fusion = bf16[64,1,16,4096]{3,2,0,1:T(8,128)(2,1)} fusion(bf16[64,1,8,4096]{3,2,0,1:T(8,128)(2,1)} %fusion.1, bf16[64,1,8,4096]{3,2,0,1:T(8,128)(2,1)} %fusion), kind=kLoop, calls=%fused_computation.1 | loop fusion | flops 16777216 | bytes 16777216 | tf_op jit(solution)/shard_map/concatenate | solution.py:64
  185.1 6.0 %fusion.3 = bf16[1,384,4096]{2,1,0:T(8,128)(2,1)} fusion(bf16[64,1,16,4096]{3,2,0,1:T(8,128)(2,1)} %all-gather.2.cloned.1.call-done, f32[64,1,8,384]{3,2,0,1:T(8,128)} %copy-done.7), kind=kOutput, calls=%fused_computation.9 | convolution fusion | flops 1613168640 | bytes 8126464 | tf_op jit(solution)/shard_map/nesh,nesd->ehd/dot_general | solution.py:57
  191.1 78.3 %reduce-scatter.2.cloned.1.call-done = bf16[64,1,16,1024]{3,2,0,1:T(8,128)(2,1)} async-done(((bf16[64,1,16,4096]{3,2,0,1:T(8,128)(2,1)}), bf16[64,1,16,1024]{3,2,0,1:T(8,128)(2,1)}) %reduce-scatter.2.cloned.1.call-update) | async-done | bytes 2097168 | tf_op jit(solution)/shard_map/reduce_scatter | solution.py:67
  269.4 11.0 %all-to-all-start.1 = ((bf16[64,1,16,1024]{3,2,1,0:T(8,128)(2,1)}), bf16[64,1,16,1024]{3,2,1,0:T(8,128)(2,1)}, u32[]{:S(2)}, u32[]{:S(2)}) async-start(bf16[64,1,16,1024]{3,2,1,0:T(8,128)(2,1)} %bitcast.123), calls=%async_computation.2 | async-start | bytes 4194304 | tf_op jit(solution)/shard_map/all_to_all | solution.py:68
  280.4 6.3 %fusion.2 = bf16[1,4096,384]{2,1,0:T(8,128)(2,1)} fusion(bf16[64,8,384]{2,1,0:T(8,128)(2,1)} %copy-done.6, bf16[64,1,16,4096]{3,2,0,1:T(8,128)(2,1)} %all-gather.2.cloned.1.call-done), kind=kOutput, calls=%fused_computation.8 | convolution fusion | flops 1612185600 | bytes 7733248 | tf_op jit(solution)/shard_map/nesd,nesh->edh/dot_general | solution.py:60
  286.7 43.2 %all-to-all-done.1 = bf16[64,1,16,1024]{3,2,1,0:T(8,128)(2,1)} async-done(((bf16[64,1,16,1024]{3,2,1,0:T(8,128)(2,1)}), bf16[64,1,16,1024]{3,2,1,0:T(8,128)(2,1)}, u32[]{:S(2)}, u32[]{:S(2)}) %all-to-all-start.1) | async-done | bytes 2097184 | tf_op jit(solution)/shard_map/all_to_all | solution.py:68
  330.0 2.5 convolution_convert_fusion.4
  332.4 2.5 convolution_convert_fusion.5
  (27 shorter events, 0.8 us)
Async XLA Ops:
  7.2 158.1 %copy-start = (bf16[1,384,4096]{2,1,0:T(8,128)(2,1)S(1)}, bf16[1,384,4096]{2,1,0:T(8,128)(2,1)}, u32[]{:S(2)}) copy-start(bf16[1,384,4096]{2,1,0:T(8,128)(2,1)} %param.11) | copy-start | bytes 9437188
  7.2 152.6 %all-gather.2.cloned.1.call-start = ((), (), s32[]{:S(2)}) async-start(), calls=%async_computation.3 | async-start | bytes 10485760 | tf_op jit(solution)/shard_map/all_gather | solution.py:44
  10.0 2.1 copy-start.3
  10.0 2.6 copy-start.1
  10.0 3.1 copy-start.2
  76.2 193.2 %reduce-scatter.2.cloned.1.call-start = ((), (), s32[]{:S(2)}) async-start(), calls=%async_computation.4 | async-start | bytes 10485760 | tf_op jit(solution)/shard_map/reduce_scatter | solution.py:67
  165.3 4.3 %copy-start.7 = (f32[64,1,8,384]{3,2,0,1:T(8,128)}, f32[64,1,8,384]{3,2,0,1:T(8,128)S(1)}, u32[]{:S(2)}) copy-start(f32[64,1,8,384]{3,2,0,1:T(8,128)S(1)} %fusion.18) | copy-start | bytes 2359300
  165.3 4.4 %copy-start.4 = (bf16[64,1,16,4096]{3,2,0,1:T(8,128)(2,1)S(1)}, bf16[64,1,16,4096]{3,2,0,1:T(8,128)(2,1)}, u32[]{:S(2)}) copy-start(bf16[64,1,16,4096]{3,2,0,1:T(8,128)(2,1)} %all-gather.2.cloned.1.call-done) | copy-start | bytes 25165828
  169.7 3.3 copy-start.5
  172.1 0.8 copy-start.6
  269.4 60.5 %all-to-all-start.1 = ((bf16[64,1,16,1024]{3,2,1,0:T(8,128)(2,1)}), bf16[64,1,16,1024]{3,2,1,0:T(8,128)(2,1)}, u32[]{:S(2)}, u32[]{:S(2)}) async-start(bf16[64,1,16,1024]{3,2,1,0:T(8,128)(2,1)} %bitcast.123), calls=%async_computation.2 | async-start | bytes 4194304 | tf_op jit(solution)/shard_map/all_to_all | solution.py:68
Sparse Core Ops, SparseCore 0:
  76.4 83.3 all-gather.1
  185.2 84.1 reduce-scatter.1

commit v2 on v1

v2 whole, which is shorter than its diff:
```python
import jax
import jax.numpy as jnp
from jax import lax
from jax.sharding import PartitionSpec as P

CHUNKS = 2


def expert_chunk(rows, scaled, w_in, w_out, quarter):
    slots = rows.shape[2]
    send = jnp.concatenate([rows, scaled], axis=2)
    arrived = lax.all_to_all(send, "expert", split_axis=0, concat_axis=0, tiled=True)
    whole = lax.all_gather(arrived, "tensor", axis=3, tiled=True)
    expert_rows = whole[:, :, :slots]
    expert_scaled = whole[:, :, slots:]
    preact = jnp.einsum("nesd,edh->nesh", expert_rows, w_in, preferred_element_type=jnp.float32)
    sigmoid_val = jax.nn.sigmoid(preact)
    hidden = (preact * sigmoid_val).astype(jnp.bfloat16)
    out_part = jnp.einsum("nesh,ehd->nesd", hidden, w_out, preferred_element_type=jnp.float32)
    grad_hidden = jnp.einsum(
        "nesd,ehd->nesh", expert_scaled, w_out, preferred_element_type=jnp.float32
    )
    grad_preact = (grad_hidden * sigmoid_val * (1.0 + preact * (1.0 - sigmoid_val))).astype(
        jnp.bfloat16
    )
    d_w_out = jnp.einsum(
        "nesh,nesd->ehd", hidden, expert_scaled, preferred_element_type=jnp.float32
    )
    d_w_in = jnp.einsum(
        "nesd,nesh->edh", expert_rows, grad_preact, preferred_element_type=jnp.float32
    )
    grad_part = jnp.einsum("nesh,edh->nesd", grad_preact, w_in, preferred_element_type=jnp.float32)
    parts = jnp.concatenate(
        [out_part.astype(jnp.bfloat16), grad_part.astype(jnp.bfloat16)], axis=2
    )
    sums = lax.psum_scatter(parts, "tensor", scatter_dimension=3, tiled=True)
    back = lax.all_to_all(sums, "expert", split_axis=0, concat_axis=0, tiled=True)
    return back[:, :, :slots], back[:, :, slots:], d_w_in, d_w_out


def shards(tokens, cotangent, routing, gates, w_in, w_out):
    devices = lax.axis_size("expert")
    local_experts = w_in.shape[0]
    experts = devices * local_experts
    tok_rows = routing.shape[0]
    capacity = tok_rows // 4
    buffer_rows = experts * capacity
    highest = lax.Precision.HIGHEST
    matches = (routing[:, :, None] == jnp.arange(experts, dtype=jnp.int32)[None, None, :]).astype(
        jnp.int32
    )
    per_token = jnp.sum(matches, axis=1)
    earlier = jnp.cumsum(per_token, axis=0) - per_token
    destination = routing * capacity + jnp.take_along_axis(earlier, routing, axis=1)
    placed = (
        destination[:, :, None] == jnp.arange(buffer_rows, dtype=jnp.int32)[None, None, :]
    ).astype(jnp.float32)
    membership = jnp.sum(placed, axis=1)
    weighting = jnp.sum(placed * gates[:, :, None], axis=1)
    quarter = tokens.shape[1]
    rows = jnp.einsum(
        "tr,td->rd",
        membership.astype(jnp.bfloat16),
        tokens,
        preferred_element_type=jnp.float32,
    ).astype(jnp.bfloat16)
    scaled = jnp.einsum(
        "tr,td->rd", weighting, cotangent.astype(jnp.float32), precision=highest
    ).astype(jnp.bfloat16)
    rows = rows.reshape(devices, local_experts, capacity, quarter)
    scaled = scaled.reshape(devices, local_experts, capacity, quarter)
    step = capacity // CHUNKS
    back_out, back_grad, d_w_in, d_w_out = [], [], None, None
    for c in range(CHUNKS):
        window = slice(c * step, (c + 1) * step)
        with jax.named_scope(f"slot_chunk{c}"):
            b_out, b_grad, g_in, g_out = expert_chunk(
                rows[:, :, window], scaled[:, :, window], w_in, w_out, quarter
            )
        back_out.append(b_out)
        back_grad.append(b_grad)
        d_w_in = g_in if d_w_in is None else d_w_in + g_in
        d_w_out = g_out if d_w_out is None else d_w_out + g_out
    back_out = jnp.concatenate(back_out, axis=2).reshape(buffer_rows, quarter).astype(jnp.float32)
    back_grad = jnp.concatenate(back_grad, axis=2).reshape(buffer_rows, quarter).astype(jnp.float32)
    mixed = jnp.einsum("tr,rd->td", weighting, back_out, precision=highest).astype(jnp.bfloat16)
    d_tokens = jnp.einsum("tr,rd->td", membership, back_grad, precision=highest).astype(
        jnp.bfloat16
    )
    return (mixed, d_tokens, d_w_in.astype(jnp.bfloat16), d_w_out.astype(jnp.bfloat16))


def solution(mesh):
    placed = (
        P("expert", "tensor"),
        P("expert", "tensor"),
        P("expert", None),
        P("expert", None),
        P("expert", None, "tensor"),
        P("expert", "tensor", None),
    )
    return jax.shard_map(
        shards,
        mesh=mesh,
        in_specs=placed,
        out_specs=(
            P("expert", "tensor"),
            P("expert", "tensor"),
            P("expert", None, "tensor"),
            P("expert", "tensor", None),
        ),
        check_vma=False,
    )
```

time: 343 us -> 319 us (0.930)
  waiting for transfers between devices: 205 us -> 145 us
  local copies, waits for them, and re-layouts: 4.89 us -> 21.2 us
  blocking collectives: 61.8 us -> 73.3 us
  starting transfers between devices: 11.2 us -> 22.2 us
    all_gather x1 -> x2, waiting for transfers between devices: 83.3 us -> 52.3 us  [expert_chunk(): whole = lax.all_gather(arrived, 'tensor', axis=3, tiled=True)]
    all_to_all x1 -> x2, waiting for transfers between devices: 43.2 us -> 14.4 us  [expert_chunk(): lax.all_to_all(sums, 'expert', split_axis=0, concat_axis=0, tiled=True)]
    all_to_all x1 -> x2, blocking collectives: 61.8 us -> 73.3 us  [expert_chunk(): lax.all_to_all(send, 'expert', split_axis=0, concat_axis=0, tiled=True)]
    all_to_all x1 -> x2, starting transfers between devices: 11 us -> 21.9 us  [expert_chunk(): lax.all_to_all(sums, 'expert', split_axis=0, concat_axis=0, tiled=True)]
    reduce_scatter x0 -> x2, local copies, waits for them, and re-layouts: none -> 5.64 us  [expert_chunk(): sums = lax.psum_scatter(parts, 'tensor', scatter_dimension=3, tiled=True)]
    slice x0 -> x3, local copies, waits for them, and re-layouts: none -> 5.1 us  [the longest x2 3.42 us: expert_chunk(): return (back[:, :, :slots], back[:, :, slots:], d_w_in, d_w_out)]
    dot_general x6 -> x12, matrix products: 28.8 us -> 27.4 us  [the longest x2 6.53 us: expert_chunk(): jnp.einsum('nesd,ehd->nesh', expert_scaled, w_out, preferred_element_type...]
    concatenate x2 -> x4, other arithmetic: 8.04 us -> 6.88 us  [the longest x2 4.65 us: expert_chunk(): jnp.concatenate([out_part.astype(jnp.bfloat16), grad_part.astype(jnp.bflo...]
  transfers between devices with their start and end apart: 3 -> 6, of which waited for: 3 -> 5; matrix products, arithmetic and copies ran while one was open for 4% -> 13% of each run, Pallas kernels for 0% -> 0%
where the time goes in v2:
time: 319 us; the launch traced here: 317 us
  waiting for transfers between devices  145 us (45%)
  blocking collectives  73.3 us (23%)
  matrix products  33.2 us (10%)
  starting transfers between devices  22.2 us (7%)
  local copies, waits for them, and re-layouts  21.2 us (7%)
  between operations  14.1 us (4%)
  other arithmetic  8.15 us (3%)
    reduce_scatter x2, waiting for transfers between devices, expert_chunk(): sums = lax.psum_scatter(parts, 'tensor', scatter_dimension=3, tiled=True)  77.9 us
    all_to_all x2, blocking collectives, expert_chunk(): lax.all_to_all(send, 'expert', split_axis=0, concat_axis=0, tiled=True)  73.3 us
    all_gather x2, waiting for transfers between devices, expert_chunk(): whole = lax.all_gather(arrived, 'tensor', axis=3, tiled=True)  52.3 us
    all_to_all x2, starting transfers between devices, expert_chunk(): lax.all_to_all(sums, 'expert', split_axis=0, concat_axis=0, tiled=True)  21.9 us
    all_to_all x2, waiting for transfers between devices, expert_chunk(): lax.all_to_all(sums, 'expert', split_axis=0, concat_axis=0, tiled=True)  14.4 us
    dot_general x2, matrix products, expert_chunk(): jnp.einsum('nesd,ehd->nesh', expert_scaled, w_out, preferred_element_type...  6.53 us
  transfers between devices with their start and end apart: 6, of which 5 were waited for; matrix products, arithmetic and copies ran while one was open for 13% of the time, Pallas kernels for 0%

profile of v2, /device:TPU:7, one launch (start us, length us, event | category | flops | bytes accessed | tf_op | source)
XLA Modules:
  0.0 316.9 jit_solution(12674950334931430944)
XLA Ops:
  9.2 1.9 gather_fusion
  15.8 39.1 %all_to_all.20 = bf16[64,1,8,1024]{3,2,1,0:T(8,128)(2,1)S(1)} all-to-all(bf16[64,1,8,1024]{3,2,1,0:T(8,128)(2,1)S(1)} %pad_maximum_fusion.2), channel_id=1, replica_groups=mesh['expert'=64,'tensor'=4] {'expert'}, dimensions={0} | all-to-all | bytes 2097152 | tf_op jit(solution)/shard_map/slot_chunk0/all_to_all | solution.py:12
  56.5 1.7 pad_maximum_fusion.3
  58.2 34.2 %all_to_all.21 = bf16[64,1,8,1024]{3,2,1,0:T(8,128)(2,1)S(1)} all-to-all(bf16[64,1,8,1024]{3,2,1,0:T(8,128)(2,1)S(1)} %pad_maximum_fusion.3), channel_id=1, replica_groups=mesh['expert'=64,'tensor'=4] {'expert'}, dimensions={0} | all-to-all | bytes 2097152 | tf_op jit(solution)/shard_map/slot_chunk1/all_to_all | solution.py:12
  94.3 11.2 %all-gather.3.cloned.1.call-done = bf16[64,1,8,4096]{3,0,2,1:T(8,128)(2,1)} async-done(((bf16[64,1,8,1024]{3,0,2,1:T(8,128)(2,1)}), bf16[64,1,8,4096]{3,0,2,1:T(8,128)(2,1)}) %all-gather.3.cloned.1.call-update) | async-done | bytes 4194320 | tf_op jit(solution)/shard_map/slot_chunk0/all_gather | solution.py:13
  105.5 3.0 fusion.24
  108.5 3.2 %fusion.57 = bf16[64,4,384]{2,0,1:T(8,128)(2,1)S(1)} fusion(bf16[1,384,4096]{2,1,0:T(8,128)(2,1)} %param.11, bf16[64,1,8,4096]{3,0,2,1:T(8,128)(2,1)S(1)} %copy-done.4, f32[64,1,4,384]{3,0,2,1:T(8,128)S(1)} %fusion.24), kind=kOutput, calls=%fused_computation.50 | convolution fusion | flops 806191104 | bytes 5832704 | tf_op jit(solution)/shard_map/slot_chunk0/nesd,ehd->nesh/dot_general | solution.py:20
  115.6 2.3 pad_maximum_fusion
  118.0 41.1 %all-gather.5.cloned.1.call-done = bf16[64,1,8,4096]{3,0,2,1:T(8,128)(2,1)} async-done(((bf16[64,1,8,1024]{3,0,2,1:T(8,128)(2,1)}), bf16[64,1,8,4096]{3,0,2,1:T(8,128)(2,1)}) %all-gather.5.cloned.1.call-update) | async-done | bytes 4194320 | tf_op jit(solution)/shard_map/slot_chunk1/all_gather | solution.py:13
  159.1 3.0 fusion.27
  162.1 3.3 %fusion.54 = bf16[64,4,384]{2,0,1:T(8,128)(2,1)S(1)} fusion(bf16[1,384,4096]{2,1,0:T(8,128)(2,1)} %param.11, bf16[64,1,8,4096]{3,0,2,1:T(8,128)(2,1)S(1)} %copy-done.19, f32[64,1,4,384]{3,0,2,1:T(8,128)S(1)} %fusion.27), kind=kOutput, calls=%fused_computation.49 | convolution fusion | flops 806191104 | bytes 5832704 | tf_op jit(solution)/shard_map/slot_chunk1/nesd,ehd->nesh/dot_general | solution.py:20
  169.3 2.3 pad_maximum_fusion.1
  171.6 39.9 %reduce-scatter.3.cloned.1.call-done = bf16[64,1,8,1024]{3,0,2,1:T(8,128)(2,1)} async-done(((bf16[64,1,8,4096]{3,0,2,1:T(8,128)(2,1)}), bf16[64,1,8,1024]{3,0,2,1:T(8,128)(2,1)}) %reduce-scatter.3.cloned.1.call-update) | async-done | bytes 1048592 | tf_op jit(solution)/shard_map/slot_chunk0/reduce_scatter | solution.py:36
  211.5 2.8 copy.73
  214.3 10.9 %all-to-all-start.1 = ((bf16[64,1,8,1024]{3,2,1,0:T(8,128)(2,1)}), bf16[64,1,8,1024]{3,2,1,0:T(8,128)(2,1)S(1)}, u32[]{:S(2)}, u32[]{:S(2)}) async-start(bf16[64,1,8,1024]{3,2,1,0:T(8,128)(2,1)} %copy.73), calls=%async_computation.2 | async-start | bytes 2097152 | tf_op jit(solution)/shard_map/slot_chunk0/all_to_all | solution.py:37
  225.2 38.0 %reduce-scatter.5.cloned.1.call-done = bf16[64,1,8,1024]{3,0,2,1:T(8,128)(2,1)} async-done(((bf16[64,1,8,4096]{3,0,2,1:T(8,128)(2,1)}), bf16[64,1,8,1024]{3,0,2,1:T(8,128)(2,1)}) %reduce-scatter.5.cloned.1.call-update) | async-done | bytes 1048592 | tf_op jit(solution)/shard_map/slot_chunk1/reduce_scatter | solution.py:36
  263.2 2.9 copy.78
  266.1 11.0 %all-to-all-start.3 = ((bf16[64,1,8,1024]{3,2,1,0:T(8,128)(2,1)}), bf16[64,1,8,1024]{3,2,1,0:T(8,128)(2,1)}, u32[]{:S(2)}, u32[]{:S(2)}) async-start(bf16[64,1,8,1024]{3,2,1,0:T(8,128)(2,1)} %copy.78), calls=%async_computation.5 | async-start | bytes 2097152 | tf_op jit(solution)/shard_map/slot_chunk1/all_to_all | solution.py:37
  277.1 3.0 fusion.20
  282.5 3.0 fusion.2
  285.5 2.7 fusion.3
  289.6 14.4 %all-to-all-done.3 = bf16[64,1,8,1024]{3,2,1,0:T(8,128)(2,1)} async-done(((bf16[64,1,8,1024]{3,2,1,0:T(8,128)(2,1)}), bf16[64,1,8,1024]{3,2,1,0:T(8,128)(2,1)}, u32[]{:S(2)}, u32[]{:S(2)}) %all-to-all-start.3) | async-done | bytes 1048608 | tf_op jit(solution)/shard_map/slot_chunk1/all_to_all | solution.py:37
  304.0 2.0 fusion.72
  306.1 2.7 convolution_convert_fusion.6
  (85 shorter events, 23.0 us)
Async XLA Ops:
  7.2 98.3 %copy-start = (bf16[1,4096,384]{2,1,0:T(8,128)(2,1)S(1)}, bf16[1,4096,384]{2,1,0:T(8,128)(2,1)}, u32[]{:S(2)}) copy-start(bf16[1,4096,384]{2,1,0:T(8,128)(2,1)} %param.10) | copy-start | bytes 9437188
  7.2 98.3 %all-gather.3.cloned.1.call-start = ((), (), s32[]{:S(2)}) async-start(), calls=%async_computation.6 | async-start | bytes 5242880 | tf_op jit(solution)/shard_map/slot_chunk0/all_gather | solution.py:13
  9.2 2.2 copy-start.17
  9.2 2.2 copy-start.18
  9.2 2.7 copy-start.15
  9.2 3.3 %copy-start.16 = (bf16[32,1024]{1,0:T(8,128)(2,1)S(1)}, bf16[32,1024]{1,0:T(8,128)(2,1)}, u32[]{:S(2)}) copy-start(bf16[32,1024]{1,0:T(8,128)(2,1)} %param.7) | copy-start | bytes 196612
  56.4 102.6 %all-gather.5.cloned.1.call-start = ((), (), s32[]{:S(2)}) async-start(), calls=%async_computation.8 | async-start | bytes 5242880 | tf_op jit(solution)/shard_map/slot_chunk1/all_gather | solution.py:13
  94.0 117.5 %reduce-scatter.3.cloned.1.call-start = ((), (), s32[]{:S(2)}) async-start(), calls=%async_computation.7 | async-start | bytes 5242880 | tf_op jit(solution)/shard_map/slot_chunk0/reduce_scatter | solution.py:36
  105.5 3.0 copy-start.4
  118.0 145.3 %reduce-scatter.5.cloned.1.call-start = ((), (), s32[]{:S(2)}) async-start(), calls=%async_computation.9 | async-start | bytes 5242880 | tf_op jit(solution)/shard_map/slot_chunk1/reduce_scatter | solution.py:36
  159.1 3.0 copy-start.19
  162.1 5.3 %copy-start.23 = (f32[64,1,4,384]{3,0,2,1:T(8,128)}, f32[64,1,4,384]{3,0,2,1:T(8,128)S(1)}, u32[]{:S(2)}) copy-start(f32[64,1,4,384]{3,0,2,1:T(8,128)S(1)} %fusion.27) | copy-start | bytes 1179652
  214.3 62.8 %copy-start.12 = (bf16[64,4,384]{2,0,1:T(8,128)(2,1)S(1)}, bf16[64,4,384]{2,0,1:T(8,128)(2,1)}, u32[]{:S(2)}) copy-start(bf16[64,4,384]{2,0,1:T(8,128)(2,1)} %copy-done.11) | copy-start | bytes 589828
  214.3 51.8 %all-to-all-start.1 = ((bf16[64,1,8,1024]{3,2,1,0:T(8,128)(2,1)}), bf16[64,1,8,1024]{3,2,1,0:T(8,128)(2,1)S(1)}, u32[]{:S(2)}, u32[]{:S(2)}) async-start(bf16[64,1,8,1024]{3,2,1,0:T(8,128)(2,1)} %copy.73), calls=%async_computation.2 | async-start | bytes 2097152 | tf_op jit(solution)/shard_map/slot_chunk0/all_to_all | solution.py:37
  266.1 14.1 %copy-start.2 = (bf16[64,1,8,1024]{3,2,1,0:T(8,128)(2,1)}, bf16[64,1,8,1024]{3,2,1,0:T(8,128)(2,1)S(1)}, u32[]{:S(2)}) copy-start(bf16[64,1,8,1024]{3,2,1,0:T(8,128)(2,1)S(1)} %all-to-all-done.1) | copy-start | bytes 3145732
  266.1 37.9 %all-to-all-start.3 = ((bf16[64,1,8,1024]{3,2,1,0:T(8,128)(2,1)}), bf16[64,1,8,1024]{3,2,1,0:T(8,128)(2,1)}, u32[]{:S(2)}, u32[]{:S(2)}) async-start(bf16[64,1,8,1024]{3,2,1,0:T(8,128)(2,1)} %copy.78), calls=%async_computation.5 | async-start | bytes 2097152 | tf_op jit(solution)/shard_map/slot_chunk1/all_to_all | solution.py:37
  277.1 3.1 copy-start.5
  280.2 2.3 copy-start.20
  282.5 3.0 copy-start.24
  285.5 2.7 copy-start.3
  288.2 17.9 %copy-start.10 = (f32[32,512]{1,0:T(8,128)S(1)}, f32[32,512]{1,0:T(8,128)}, u32[]{:S(2)}) copy-start(f32[32,512]{1,0:T(8,128)} %copy-done.9) | copy-start | bytes 196612
  288.2 20.5 %copy-start.8 = (f32[32,512]{1,0:T(8,128)S(1)}, f32[32,512]{1,0:T(8,128)}, u32[]{:S(2)}) copy-start(f32[32,512]{1,0:T(8,128)} %copy-done.7) | copy-start | bytes 196612
  288.2 22.1 %copy-start.1 = (bf16[1,4096,384]{2,1,0:T(8,128)(2,1)S(1)}, bf16[1,4096,384]{2,1,0:T(8,128)(2,1)}, u32[]{:S(2)}) copy-start(bf16[1,4096,384]{2,1,0:T(8,128)(2,1)} %param.10) | copy-start | bytes 9437188
  304.0 4.7 %copy-start.6 = (bf16[64,1,4,1024]{3,2,0,1:T(4,128)(2,1)S(1)}, bf16[64,1,4,1024]{3,2,0,1:T(4,128)(2,1)}, u32[]{:S(2)}) copy-start(bf16[64,1,4,1024]{3,2,0,1:T(4,128)(2,1)} %get-tuple-element.7) | copy-start | bytes 1572868
  (7 other events, 7.5 us)
Sparse Core Ops, SparseCore 0:
  56.6 48.8 all-gather.2
  107.9 51.1 all-gather.4
  161.6 49.8 reduce-scatter.2
  214.1 49.1 reduce-scatter.4

commit v3 on v2

--- a/solution.py
+++ b/solution.py
@@ -1,15 +1,86 @@
 import jax
 import jax.numpy as jnp
 from jax import lax
+from jax.experimental import pallas as pl
+from jax.experimental.pallas import tpu as pltpu
 from jax.sharding import PartitionSpec as P
 
 CHUNKS = 2
 
 
-def expert_chunk(rows, scaled, w_in, w_out, quarter):
+def _a2a_kernel(x_ref, o_ref, send_sem, recv_sem, local_sem):
+    n = x_ref.shape[0]
+    me = lax.axis_index("expert")
+    tau = lax.axis_index("tensor")
+    barrier = pltpu.get_barrier_semaphore()
+
+    def greet(k, carry):
+        peer = lax.rem(me + k, n)
+        pl.semaphore_signal(
+            barrier, inc=1, device_id=(peer, tau), device_id_type=pl.DeviceIdType.MESH
+        )
+        return carry
+
+    lax.fori_loop(1, n, greet, 0)
+    pl.semaphore_wait(barrier, n - 1)
+
+    local = pltpu.make_async_copy(x_ref.at[me], o_ref.at[me], local_sem)
+    local.start()
+
+    def push(k, carry):
+        peer = lax.rem(me + k, n)
+        pltpu.make_async_remote_copy(
+            src_ref=x_ref.at[peer],
+            dst_ref=o_ref.at[me],
+            send_sem=send_sem.at[k],
+            recv_sem=recv_sem.at[k],
+            device_id=(peer, tau),
+            device_id_type=pl.DeviceIdType.MESH,
+        ).start()
+        return carry
+
+    lax.fori_loop(1, n, push, 0)
+
+    def settle(k, carry):
+        peer = lax.rem(me + k, n)
+        source = lax.rem(me + n - k, n)
+        pltpu.make_async_remote_copy(
+            src_ref=x_ref.at[peer],
+            dst_ref=o_ref.at[source],
+            send_sem=send_sem.at[k],
+            recv_sem=recv_sem.at[k],
+            device_id=(peer, tau),
+            device_id_type=pl.DeviceIdType.MESH,
+        ).wait()
+        return carry
+
+    lax.fori_loop(1, n, settle, 0)
+    local.wait()
+
+
+def expert_all_to_all(x, collective_id):
+    n = x.shape[0]
+    return pl.pallas_call(
+        _a2a_kernel,
+        out_shape=jax.ShapeDtypeStruct(x.shape, x.dtype),
+        in_specs=[pl.BlockSpec(memory_space=pl.ANY)],
+        out_specs=pl.BlockSpec(memory_space=pl.ANY),
+        scratch_shapes=[
+            pltpu.SemaphoreType.DMA((n,)),
+            pltpu.SemaphoreType.DMA((n,)),
+            pltpu.SemaphoreType.DMA(()),
+        ],
+        compiler_params=pltpu.CompilerParams(collective_id=collective_id, has_side_effects=True),
+        cost_estimate=pl.CostEstimate(
+            flops=0, transcendentals=0, bytes_accessed=2 * x.size * x.dtype.itemsize
+        ),
+    )(x)
+
+
+def expert_chunk(rows, scaled, w_in, w_out, quarter, ids):
     slots = rows.shape[2]
     send = jnp.concatenate([rows, scaled], axis=2)
-    arrived = lax.all_to_all(send, "expert", split_axis=0, concat_axis=0, tiled=True)
+    arrived = expert_all_to_all(send.reshape(send.shape[0], -1, quarter), ids[0]).reshape(send.shape)
     whole = lax.all_gather(arrived, "tensor", axis=3, tiled=True)
     expert_rows = whole[:, :, :slots]
     expert_scaled = whole[:, :, slots:]
@@ -34,7 +105,7 @@
         [out_part.astype(jnp.bfloat16), grad_part.astype(jnp.bfloat16)], axis=2
     )
     sums = lax.psum_scatter(parts, "tensor", scatter_dimension=3, tiled=True)
-    back = lax.all_to_all(sums, "expert", split_axis=0, concat_axis=0, tiled=True)
+    back = expert_all_to_all(sums.reshape(sums.shape[0], -1, quarter), ids[1]).reshape(sums.shape)
     return back[:, :, :slots], back[:, :, slots:], d_w_in, d_w_out
 
 
@@ -75,7 +146,7 @@
         window = slice(c * step, (c + 1) * step)
         with jax.named_scope(f"slot_chunk{c}"):
             b_out, b_grad, g_in, g_out = expert_chunk(
-                rows[:, :, window], scaled[:, :, window], w_in, w_out, quarter
+                rows[:, :, window], scaled[:, :, window], w_in, w_out, quarter, (2 * c, 2 * c + 1)
             )
         back_out.append(b_out)
         back_grad.append(b_grad)

time: 319 us -> 313 us (0.981)
  Pallas kernels: 0 us -> 139 us
  blocking collectives: 73.3 us -> 0 us
  waiting for transfers between devices: 145 us -> 76.4 us
  starting transfers between devices: 22.2 us -> 0.86 us
  local copies, waits for them, and re-layouts: 21.2 us -> 32.7 us
  other arithmetic: 8.15 us -> 12.7 us
    pallas_call x0 -> x4, Pallas kernels: none -> 139 us  [expert_all_to_all(): pl.pallas_call(_a2a_kernel, out_shape=jax.ShapeDtypeStruct(x.shape, x.dty...]
    all_to_all x2 -> x0, blocking collectives: 73.3 us -> none  [expert_chunk(): lax.all_to_all(send, 'expert', split_axis=0, concat_axis=0, tiled=True)]
    reduce_scatter x2, waiting for transfers between devices: 77.9 us -> 29.9 us  [expert_chunk(): sums = lax.psum_scatter(parts, 'tensor', scatter_dimension=3, tiled=True)]
    all_to_all x2 -> x0, starting transfers between devices: 21.9 us -> none  [expert_chunk(): lax.all_to_all(sums, 'expert', split_axis=0, concat_axis=0, tiled=True)]
    all_to_all x2 -> x0, waiting for transfers between devices: 14.4 us -> none  [expert_chunk(): lax.all_to_all(sums, 'expert', split_axis=0, concat_axis=0, tiled=True)]
    another operation x0 -> x2, local copies, waits for them, and re-layouts: none -> 11.1 us
    unnamed x52 -> x50, local copies, waits for them, and re-layouts: 4.99 us -> 12.4 us
    all_gather x2, waiting for transfers between devices: 52.3 us -> 46.4 us  [expert_chunk(): whole = lax.all_gather(arrived, 'tensor', axis=3, tiled=True)]
  transfers between devices with their start and end apart: 6 -> 4, of which waited for: 5 -> 4; matrix products, arithmetic and copies ran while one was open for 13% -> 19% of each run, Pallas kernels for 0% -> 22%
where the time goes in v3:
time: 313 us; the launch traced here: 308 us
  Pallas kernels  139 us (44%)
  waiting for transfers between devices  76.4 us (24%)
  local copies, waits for them, and re-layouts  32.7 us (10%)
  matrix products  31.9 us (10%)
  between operations  14.5 us (5%)
  other arithmetic  12.7 us (4%)
    pallas_call x4, Pallas kernels, expert_all_to_all(): pl.pallas_call(_a2a_kernel, out_shape=jax.ShapeDtypeStruct(x.shape, x.dty...  139 us
    all_gather x2, waiting for transfers between devices, expert_chunk(): whole = lax.all_gather(arrived, 'tensor', axis=3, tiled=True)  46.4 us
    reduce_scatter x2, waiting for transfers between devices, expert_chunk(): sums = lax.psum_scatter(parts, 'tensor', scatter_dimension=3, tiled=True)  29.9 us
    unnamed x50, local copies, waits for them, and re-layouts  12.4 us
    another operation x2, local copies, waits for them, and re-layouts  11.1 us
    dot_general x2, matrix products, expert_chunk(): jnp.einsum('nesh,nesd->ehd', hidden, expert_scaled, preferred_element_typ...  7.68 us
    dot_general x2, matrix products, expert_chunk(): jnp.einsum('nesd,nesh->edh', expert_rows, grad_preact, preferred_element_...  7.2 us
    concatenate x2, other arithmetic, expert_chunk(): jnp.concatenate([out_part.astype(jnp.bfloat16), grad_part.astype(jnp.bflo...  7.08 us
  transfers between devices with their start and end apart: 4, of which 4 were waited for; matrix products, arithmetic and copies ran while one was open for 19% of the time, Pallas kernels for 22%

profile of v3, /device:TPU:7, one launch (start us, length us, event | category | flops | bytes accessed | tf_op | source)
XLA Modules:
  0.0 308.5 jit_solution(6251797203868392320)
XLA Ops:
  10.0 1.9 gather_fusion
  17.3 36.8 %slot_chunk1.2 = bf16[64,8,1024]{2,1,0:T(8,128)(2,1)} custom-call(bf16[64,8,1024]{2,1,0:T(8,128)(2,1)} %maximum_bitcast_fusion.1.x_ref), custom_call_target="tpu_custom_call" | custom-call | bytes 2097152 | tf_op jit(solution)/shard_map/slot_chunk1/pallas_call | solution.py:63
  54.2 2.7 maximum_bitcast_fusion.x_ref
  56.9 32.6 %slot_chunk0.2 = bf16[64,8,1024]{2,1,0:T(8,128)(2,1)} custom-call(bf16[64,8,1024]{2,1,0:T(8,128)(2,1)} %maximum_bitcast_fusion.x_ref), custom_call_target="tpu_custom_call" | custom-call | bytes 2097152 | tf_op jit(solution)/shard_map/slot_chunk0/pallas_call | solution.py:63
  90.1 13.9 %all-gather.7.cloned.1.call-done = bf16[64,8,4096]{2,1,0:T(8,128)(2,1)} async-done(((bf16[64,8,1024]{2,1,0:T(8,128)(2,1)}), bf16[64,8,4096]{2,1,0:T(8,128)(2,1)}) %all-gather.7.cloned.1.call-update) | async-done | bytes 4194320 | tf_op jit(solution)/shard_map/slot_chunk1/all_gather | solution.py:84
  103.9 5.6 %slice_bitcast_fusion.1 = (bf16[64,4,4096]{2,1,0:T(4,128)(2,1)S(1)}, bf16[64,4,4096]{2,1,0:T(4,128)(2,1)S(1)}) fusion(bf16[64,1,8,4096]{3,2,0,1:T(8,128)(2,1)} %bitcast.196), kind=kLoop, calls=%fused_computation.30 | loop fusion | bytes 8388608 | tf_op jit(solution)/shard_map/reshape.28
  109.6 1.8 fusion.33
  113.1 1.8 fusion.78
  120.7 3.4 %pad_maximum_fusion.1 = bf16[64,1,8,4096]{3,2,0,1:T(8,128)(2,1)} fusion(bf16[64,1,4,4096]{3,2,0,1:T(4,128)(2,1)S(1)} %bitcast.191, bf16[64,1,4,4096]{3,2,0,1:T(4,128)(2,1)S(1)} %bitcast.193), kind=kLoop, calls=%fused_computation.12 | loop fusion | flops 8388608 | bytes 8388608 | tf_op jit(solution)/shard_map/slot_chunk1/concatenate | solution.py:104
  124.4 32.6 %all-gather.5.cloned.1.call-done = bf16[64,8,4096]{2,1,0:T(8,128)(2,1)} async-done(((bf16[64,8,1024]{2,1,0:T(8,128)(2,1)}), bf16[64,8,4096]{2,1,0:T(8,128)(2,1)}) %all-gather.5.cloned.1.call-update) | async-done | bytes 4194320 | tf_op jit(solution)/shard_map/slot_chunk0/all_gather | solution.py:84
  157.0 5.5 %slice_bitcast_fusion.3 = (bf16[64,4,4096]{2,1,0:T(4,128)(2,1)S(1)}, bf16[64,4,4096]{2,1,0:T(4,128)(2,1)S(1)}) fusion(bf16[64,1,8,4096]{3,2,0,1:T(8,128)(2,1)} %bitcast.195), kind=kLoop, calls=%fused_computation.32 | loop fusion | bytes 8388608 | tf_op jit(solution)/shard_map/reshape.4
  162.5 1.8 fusion.28
  166.1 1.8 fusion.83
  173.7 3.6 %pad_maximum_fusion = bf16[64,1,8,4096]{3,2,0,1:T(8,128)(2,1)} fusion(bf16[64,1,4,4096]{3,2,0,1:T(4,128)(2,1)S(1)} %bitcast.192, bf16[64,1,4,4096]{3,2,0,1:T(4,128)(2,1)S(1)} %bitcast.194), kind=kLoop, calls=%fused_computation.11 | loop fusion | flops 8388608 | bytes 8388608 | tf_op jit(solution)/shard_map/slot_chunk0/concatenate | solution.py:104
  178.3 3.5 %fusion.23 = f32[4096,384,1]{1,0,2:T(8,128)S(1)} fusion(bf16[64,4,384]{2,0,1:T(8,128)(2,1)S(1)} %copy-done.12, bf16[64,4,4096]{2,1,0:T(4,128)(2,1)} %copy-done.8), kind=kOutput, calls=%fused_computation.40 | convolution fusion | flops 805306368 | bytes 8585216 | tf_op jit(solution)/shard_map/slot_chunk0/nesd,nesh->edh/dot_general | solution.py:100
  181.8 2.9 fusion.20
  184.8 3.7 %fusion.2 = bf16[1,4096,384]{2,1,0:T(8,128)(2,1)} fusion(bf16[64,4,384]{2,0,1:T(8,128)(2,1)S(1)} %fusion.78, f32[4096,384,1]{1,0,2:T(8,128)S(1)} %fusion.23, bf16[64,4,4096]{2,1,0:T(4,128)(2,1)S(1)} %copy-done.5), kind=kOutput, calls=%fused_computation.9 | convolution fusion | flops 808452096 | bytes 11730944 | tf_op jit(solution)/shard_map/slot_chunk1/nesd,nesh->edh/dot_general | solution.py:100
  188.5 4.8 %fusion.3 = bf16[1,384,4096]{2,1,0:T(8,128)(2,1)} fusion(f32[384,4096,1]{1,0,2:T(8,128)S(1)} %fusion.20, bf16[64,4,4096]{2,1,0:T(4,128)(2,1)S(1)} %copy-done.3, f32[64,1,4,384]{3,0,2,1:T(8,128)S(1)} %copy-done.19), kind=kOutput, calls=%fused_computation.10 | convolution fusion | flops 808943616 | bytes 11927552 | tf_op jit(solution)/shard_map/slot_chunk1/nesh,nesd->ehd/dot_general | solution.py:97
  193.3 16.1 %reduce-scatter.5.cloned.1.call-done = bf16[64,1,8,1024]{3,2,0,1:T(8,128)(2,1)} async-done(((bf16[64,1,8,4096]{3,2,0,1:T(8,128)(2,1)}), bf16[64,1,8,1024]{3,2,0,1:T(8,128)(2,1)}) %reduce-scatter.5.cloned.1.call-update) | async-done | bytes 1048592 | tf_op jit(solution)/shard_map/slot_chunk1/reduce_scatter | solution.py:107
  209.4 34.9 %slot_chunk1.3 = bf16[64,8,1024]{2,1,0:T(8,128)(2,1)} custom-call(bf16[64,8,1024]{2,1,0:T(8,128)(2,1)} %bitcast.199), custom_call_target="tpu_custom_call" | custom-call | bytes 2097152 | tf_op jit(solution)/shard_map/slot_chunk1/pallas_call | solution.py:63
  244.3 3.0 fusion.100
  247.3 13.8 %reduce-scatter.3.cloned.1.call-done = bf16[64,1,8,1024]{3,2,0,1:T(8,128)(2,1)} async-done(((bf16[64,1,8,4096]{3,2,0,1:T(8,128)(2,1)}), bf16[64,1,8,1024]{3,2,0,1:T(8,128)(2,1)}) %reduce-scatter.3.cloned.1.call-update) | async-done | bytes 1048592 | tf_op jit(solution)/shard_map/slot_chunk0/reduce_scatter | solution.py:107
  261.1 35.1 %slot_chunk0.3 = bf16[64,8,1024]{2,1,0:T(8,128)(2,1)} custom-call(bf16[64,8,1024]{2,1,0:T(8,128)(2,1)} %bitcast.200), custom_call_target="tpu_custom_call" | custom-call | bytes 2097152 | tf_op jit(solution)/shard_map/slot_chunk0/pallas_call | solution.py:63
  296.3 2.1 fusion.99
  (79 shorter events, 28.1 us)
Async XLA Ops:
  7.2 102.4 %copy-start = (bf16[1,4096,384]{2,1,0:T(8,128)(2,1)S(1)}, bf16[1,4096,384]{2,1,0:T(8,128)(2,1)}, u32[]{:S(2)}) copy-start(bf16[1,4096,384]{2,1,0:T(8,128)(2,1)} %param.10) | copy-start | bytes 9437188
  7.2 96.7 %all-gather.7.cloned.1.call-start = ((), (), s32[]{:S(2)}) async-start(), calls=%async_computation.5 | async-start | bytes 5242880 | tf_op jit(solution)/shard_map/slot_chunk1/all_gather | solution.py:84
  10.0 2.1 copy-start.15
  10.0 2.6 copy-start.13
  10.0 3.1 copy-start.14
  54.1 102.8 %all-gather.5.cloned.1.call-start = ((), (), s32[]{:S(2)}) async-start(), calls=%async_computation.4 | async-start | bytes 5242880 | tf_op jit(solution)/shard_map/slot_chunk0/all_gather | solution.py:84
  89.5 119.9 %reduce-scatter.5.cloned.1.call-start = ((), (), s32[]{:S(2)}) async-start(), calls=%async_computation.3 | async-start | bytes 5242880 | tf_op jit(solution)/shard_map/slot_chunk1/reduce_scatter | solution.py:107
  109.5 1.9 copy-start.4
  109.5 2.1 copy-start.2
  109.5 3.5 %copy-start.16 = (bf16[1,384,4096]{2,1,0:T(8,128)(2,1)S(1)}, bf16[1,384,4096]{2,1,0:T(8,128)(2,1)}, u32[]{:S(2)}) copy-start(bf16[1,384,4096]{2,1,0:T(8,128)(2,1)} %param.11) | copy-start | bytes 9437188
  111.4 6.4 %copy-start.18 = (f32[64,1,4,384]{3,0,2,1:T(8,128)}, f32[64,1,4,384]{3,0,2,1:T(8,128)S(1)}, u32[]{:S(2)}) copy-start(f32[64,1,4,384]{3,0,2,1:T(8,128)S(1)} %fusion.33) | copy-start | bytes 1179652
  124.2 136.9 %reduce-scatter.3.cloned.1.call-start = ((), (), s32[]{:S(2)}) async-start(), calls=%async_computation.2 | async-start | bytes 5242880 | tf_op jit(solution)/shard_map/slot_chunk0/reduce_scatter | solution.py:107
  162.5 1.9 copy-start.8
  162.5 2.1 copy-start.6
  162.5 3.5 %copy-start.17 = (bf16[1,384,4096]{2,1,0:T(8,128)(2,1)S(1)}, bf16[1,384,4096]{2,1,0:T(8,128)(2,1)}, u32[]{:S(2)}) copy-start(bf16[1,384,4096]{2,1,0:T(8,128)(2,1)} %param.11) | copy-start | bytes 9437188
  164.4 6.4 %copy-start.20 = (f32[64,1,4,384]{3,0,2,1:T(8,128)}, f32[64,1,4,384]{3,0,2,1:T(8,128)S(1)}, u32[]{:S(2)}) copy-start(f32[64,1,4,384]{3,0,2,1:T(8,128)S(1)} %fusion.28) | copy-start | bytes 1179652
  178.3 3.5 %copy-start.7 = (bf16[64,4,4096]{2,1,0:T(4,128)(2,1)S(1)}, bf16[64,4,4096]{2,1,0:T(4,128)(2,1)}, u32[]{:S(2)}) copy-start(bf16[64,4,4096]{2,1,0:T(4,128)(2,1)} %copy-done.6) | copy-start | bytes 6291460
  178.3 3.5 %copy-start.21 = (f32[64,1,4,384]{3,0,2,1:T(8,128)S(1)}, f32[64,1,4,384]{3,0,2,1:T(8,128)}, u32[]{:S(2)}) copy-start(f32[64,1,4,384]{3,0,2,1:T(8,128)} %copy-done.20) | copy-start | bytes 1179652
  181.8 2.9 copy-start.5
  184.8 3.7 %copy-start.3 = (bf16[64,4,4096]{2,1,0:T(4,128)(2,1)S(1)}, bf16[64,4,4096]{2,1,0:T(4,128)(2,1)}, u32[]{:S(2)}) copy-start(bf16[64,4,4096]{2,1,0:T(4,128)(2,1)} %copy-done.2) | copy-start | bytes 6291460
  184.8 3.7 %copy-start.19 = (f32[64,1,4,384]{3,0,2,1:T(8,128)S(1)}, f32[64,1,4,384]{3,0,2,1:T(8,128)}, u32[]{:S(2)}) copy-start(f32[64,1,4,384]{3,0,2,1:T(8,128)} %copy-done.18) | copy-start | bytes 1179652
  296.3 2.2 copy-start.10
  296.3 3.8 %copy-start.9 = (bf16[64,1,4,1024]{3,2,0,1:T(4,128)(2,1)S(1)}, bf16[64,1,4,1024]{3,2,0,1:T(4,128)(2,1)}, u32[]{:S(2)}) copy-start(bf16[64,1,4,1024]{3,2,0,1:T(4,128)(2,1)} %get-tuple-element.12) | copy-start | bytes 1572868
  296.3 5.4 %copy-start.1 = (bf16[1,4096,384]{2,1,0:T(8,128)(2,1)S(1)}, bf16[1,4096,384]{2,1,0:T(8,128)(2,1)}, u32[]{:S(2)}) copy-start(bf16[1,4096,384]{2,1,0:T(8,128)(2,1)} %param.10) | copy-start | bytes 9437188
  (2 other events, 2.2 us)
Sparse Core Ops, SparseCore 0:
  54.2 49.6 all-gather.6
  105.7 51.1 all-gather.4
  159.5 49.8 reduce-scatter.4
  211.9 49.1 reduce-scatter.2

commit v4 on v3

--- a/solution.py
+++ b/solution.py
@@ -77,11 +77,134 @@
     )(x)
 
 
+def _dispatch_kernel(x_ref, o_ref, xz_send, xz_recv, y_send, y_recv, local_sem):
+    n = x_ref.shape[0]
+    groups = o_ref.shape[1]
+    me = lax.axis_index("expert")
+    tau = lax.axis_index("tensor")
+    barrier = pltpu.get_barrier_semaphore()
+
+    def greet(k, carry):
+        pl.semaphore_signal(
+            barrier, inc=1, device_id=(lax.rem(me + k, n), tau), device_id_type=pl.DeviceIdType.MESH
+        )
+        return carry
+
+    lax.fori_loop(1, n, greet, 0)
+    for j in range(1, groups):
+        pl.semaphore_signal(
+            barrier, inc=1, device_id=(me, lax.rem(tau + j, groups)), device_id_type=pl.DeviceIdType.MESH
+        )
+    pl.semaphore_wait(barrier, n - 1 + groups - 1)
+
+    local = pltpu.make_async_copy(x_ref.at[me], o_ref.at[me, tau], local_sem)
+    local.start()
+
+    def xz_copy(k):
+        peer = lax.rem(me + k, n)
+        return pltpu.make_async_remote_copy(
+            src_ref=x_ref.at[peer],
+            dst_ref=o_ref.at[me, tau],
+            send_sem=xz_send.at[k],
+            recv_sem=xz_recv.at[k],
+            device_id=(peer, tau),
+            device_id_type=pl.DeviceIdType.MESH,
+        )
+
+    def xz_arrival(k):
+        peer = lax.rem(me + k, n)
+        source = lax.rem(me + n - k, n)
+        return pltpu.make_async_remote_copy(
+            src_ref=x_ref.at[peer],
+            dst_ref=o_ref.at[source, tau],
+            send_sem=xz_send.at[k],
+            recv_sem=xz_recv.at[k],
+            device_id=(peer, tau),
+            device_id_type=pl.DeviceIdType.MESH,
+        )
+
+    def y_copy(j, k):
+        source = lax.rem(me + n - k, n)
+        return pltpu.make_async_remote_copy(
+            src_ref=o_ref.at[source, tau],
+            dst_ref=o_ref.at[source, tau],
+            send_sem=y_send.at[j - 1, k],
+            recv_sem=y_recv.at[j - 1, k],
+            device_id=(me, lax.rem(tau + j, groups)),
+            device_id_type=pl.DeviceIdType.MESH,
+        )
+
+    def y_arrival(j, k):
+        source = lax.rem(me + n - k, n)
+        return pltpu.make_async_remote_copy(
+            src_ref=o_ref.at[source, tau],
+            dst_ref=o_ref.at[source, lax.rem(tau + groups - j, groups)],
+            send_sem=y_send.at[j - 1, k],
+            recv_sem=y_recv.at[j - 1, k],
+            device_id=(me, lax.rem(tau + j, groups)),
+            device_id_type=pl.DeviceIdType.MESH,
+        )
+
+    def push(k, carry):
+        xz_copy(k).start()
+        return carry
+
+    lax.fori_loop(1, n, push, 0)
+
+    local.wait()
+    for j in range(1, groups):
+        y_copy(j, 0).start()
+
+    def forward(k, carry):
+        xz_arrival(k).wait_recv()
+        for j in range(1, groups):
+            y_copy(j, k).start()
+        return carry
+
+    lax.fori_loop(1, n, forward, 0)
+
+    def settle(k, carry):
+        xz_copy(k).wait_send()
+        return carry
+
+    lax.fori_loop(1, n, settle, 0)
+
+    def settle_y(k, carry):
+        for j in range(1, groups):
+            y_copy(j, k).wait_send()
+            y_arrival(j, k).wait_recv()
+        return carry
+
+    lax.fori_loop(0, n, settle_y, 0)
+
+
+def dispatch(x, groups, collective_id):
+    n, rows, width = x.shape
+    return pl.pallas_call(
+        _dispatch_kernel,
+        out_shape=jax.ShapeDtypeStruct((n, groups, rows, width), x.dtype),
+        in_specs=[pl.BlockSpec(memory_space=pl.ANY)],
+        out_specs=pl.BlockSpec(memory_space=pl.ANY),
+        scratch_shapes=[
+            pltpu.SemaphoreType.DMA((n,)),
+            pltpu.SemaphoreType.DMA((n,)),
+            pltpu.SemaphoreType.DMA((groups - 1, n)),
+            pltpu.SemaphoreType.DMA((groups - 1, n)),
+            pltpu.SemaphoreType.DMA(()),
+        ],
+        compiler_params=pltpu.CompilerParams(collective_id=collective_id, has_side_effects=True),
+        cost_estimate=pl.CostEstimate(
+            flops=0, transcendentals=0, bytes_accessed=(1 + 2 * groups) * x.size * x.dtype.itemsize
+        ),
+    )(x)
+
+
 def expert_chunk(rows, scaled, w_in, w_out, quarter, ids):
     slots = rows.shape[2]
     send = jnp.concatenate([rows, scaled], axis=2)
-    arrived = expert_all_to_all(send.reshape(send.shape[0], -1, quarter), ids[0]).reshape(send.shape)
-    whole = lax.all_gather(arrived, "tensor", axis=3, tiled=True)
+    groups = lax.axis_size("tensor")
+    spread = dispatch(send.reshape(send.shape[0], -1, quarter), groups, ids[0])
+    whole = jnp.swapaxes(spread, 1, 2).reshape(send.shape[:3] + (groups * quarter,))
     expert_rows = whole[:, :, :slots]
     expert_scaled = whole[:, :, slots:]
     preact = jnp.einsum("nesd,edh->nesh", expert_rows, w_in, preferred_element_type=jnp.float32)

time: 313 us -> 323 us (1.032)
  Pallas kernels: 139 us -> 229 us
  waiting for transfers between devices: 76.4 us -> 0.04 us
    pallas_call x0 -> x2, Pallas kernels: none -> 161 us  [dispatch(): pl.pallas_call(_dispatch_kernel, out_shape=jax.ShapeDtypeStruct((n, group...]
    pallas_call x4 -> x2, Pallas kernels: 139 us -> 67.8 us  [expert_all_to_all(): pl.pallas_call(_a2a_kernel, out_shape=jax.ShapeDtypeStruct(x.shape, x.dty...]
    all_gather x2 -> x0, waiting for transfers between devices: 46.4 us -> none  [expert_chunk(): whole = lax.all_gather(arrived, 'tensor', axis=3, tiled=True)]
    reduce_scatter x2, waiting for transfers between devices: 29.9 us -> 0.01 us  [expert_chunk(): sums = lax.psum_scatter(parts, 'tensor', scatter_dimension=3, tiled=True)]
    slice x0 -> x3, local copies, waits for them, and re-layouts: none -> 12 us  [the longest x2 11.6 us: expert_chunk(): expert_rows = whole[:, :, :slots]]
    another operation x2 -> x0, local copies, waits for them, and re-layouts: 11.1 us -> none
    unnamed x50 -> x52, local copies, waits for them, and re-layouts: 12.4 us -> 11.6 us
  transfers between devices with their start and end apart: 4 -> 2, of which waited for: 4 -> 0; matrix products, arithmetic and copies ran while one was open for 19% -> 11% of each run, Pallas kernels for 22% -> 41%
where the time goes in v4:
time: 323 us; the launch traced here: 318 us
  Pallas kernels  229 us (71%)
  matrix products  32 us (10%)
  local copies, waits for them, and re-layouts  31.5 us (10%)
  between operations  14.8 us (5%)
  other arithmetic  10.7 us (3%)
    pallas_call x2, Pallas kernels, dispatch(): pl.pallas_call(_dispatch_kernel, out_shape=jax.ShapeDtypeStruct((n, group...  161 us
    pallas_call x2, Pallas kernels, expert_all_to_all(): pl.pallas_call(_a2a_kernel, out_shape=jax.ShapeDtypeStruct(x.shape, x.dty...  67.8 us
    slice x2, local copies, waits for them, and re-layouts, expert_chunk(): expert_rows = whole[:, :, :slots]  11.6 us
    unnamed x52, local copies, waits for them, and re-layouts  11.6 us
    dot_general x2, matrix products, expert_chunk(): jnp.einsum('nesh,nesd->ehd', hidden, expert_scaled, preferred_element_typ...  7.68 us
    dot_general x2, matrix products, expert_chunk(): jnp.einsum('nesd,nesh->edh', expert_rows, grad_preact, preferred_element_...  7.2 us
    concatenate x2, other arithmetic, expert_chunk(): jnp.concatenate([out_part.astype(jnp.bfloat16), grad_part.astype(jnp.bflo...  7.09 us
  transfers between devices with their start and end apart: 2, of which 0 were waited for; matrix products, arithmetic and copies ran while one was open for 11% of the time, Pallas kernels for 41%

profile of v4, /device:TPU:7, one launch (start us, length us, event | category | flops | bytes accessed | tf_op | source)
XLA Modules:
  0.0 317.7 jit_solution(15277549002876796757)
XLA Ops:
  9.2 1.9 gather_fusion
  14.1 2.4 maximum_bitcast_fusion
  16.5 64.2 %slot_chunk1.2 = bf16[64,4,8,1024]{3,2,1,0:T(8,128)(2,1)} custom-call(bf16[64,8,1024]{2,1,0:T(8,128)(2,1)} %get-tuple-element.19.x_ref), custom_call_target="tpu_custom_call" | custom-call | bytes 9437184 | tf_op jit(solution)/shard_map/slot_chunk1/pallas_call | solution.py:183
  80.7 6.1 %fusion.68 = (bf16[64,1,4,4096]{3,2,0,1:T(4,128)(2,1)S(1)}, bf16[64,1,4,4096]{3,2,0,1:T(4,128)(2,1)S(1)}) fusion(bf16[64,1,8,4096]{3,2,0,1:T(8,128)(2,1)} %bitcast.227), kind=kLoop, calls=%fused_computation.81 | loop fusion | bytes 8388608 | tf_op jit(solution)/shard_map/slot_chunk1/slice | solution.py:208
  86.9 1.9 fusion.23
  91.6 1.8 fusion.50
  94.7 1.6 copy.106
  96.3 1.6 copy.107
  97.9 3.4 %pad_maximum_fusion.1 = bf16[64,1,8,4096]{3,2,0,1:T(8,128)(2,1)} fusion(bf16[64,1,4,4096]{3,2,0,1:T(4,128)(2,1)S(1)} %bitcast.230, bf16[64,1,4,4096]{3,2,0,1:T(4,128)(2,1)S(1)} %bitcast.231), kind=kLoop, calls=%fused_computation.12 | loop fusion | flops 8388608 | bytes 8388608 | tf_op jit(solution)/shard_map/slot_chunk1/concatenate | solution.py:227
  101.4 96.6 %slot_chunk0.2 = bf16[64,4,8,1024]{3,2,1,0:T(8,128)(2,1)} custom-call(bf16[64,8,1024]{2,1,0:T(8,128)(2,1)} %get-tuple-element.18.x_ref), custom_call_target="tpu_custom_call" | custom-call | bytes 9437184 | tf_op jit(solution)/shard_map/slot_chunk0/pallas_call | solution.py:183
  198.0 5.5 %fusion.67 = (bf16[64,1,4,4096]{3,2,0,1:T(4,128)(2,1)S(1)}, bf16[64,1,4,4096]{3,2,0,1:T(4,128)(2,1)S(1)}) fusion(bf16[64,1,8,4096]{3,2,0,1:T(8,128)(2,1)} %bitcast.228), kind=kLoop, calls=%fused_computation.80 | loop fusion | bytes 8388608 | tf_op jit(solution)/shard_map/slot_chunk0/slice | solution.py:208
  203.6 1.8 fusion.20
  207.1 1.8 fusion.53
  210.2 1.6 copy.108
  213.2 1.6 copy.109
  214.8 3.6 %pad_maximum_fusion = bf16[64,1,8,4096]{3,2,0,1:T(8,128)(2,1)} fusion(bf16[64,1,4,4096]{3,2,0,1:T(4,128)(2,1)S(1)} %bitcast.229, bf16[64,1,4,4096]{3,2,0,1:T(4,128)(2,1)S(1)} %bitcast.232), kind=kLoop, calls=%fused_computation.11 | loop fusion | flops 8388608 | bytes 8388608 | tf_op jit(solution)/shard_map/slot_chunk0/concatenate | solution.py:227
  219.4 3.5 %fusion.16 = f32[4096,384,1]{1,0,2:T(8,128)S(1)} fusion(bf16[64,4,384]{2,0,1:T(8,128)(2,1)S(1)} %copy-done.12, bf16[64,1,4,4096]{3,2,0,1:T(4,128)(2,1)} %copy-done.8), kind=kOutput, calls=%fused_computation.33 | convolution fusion | flops 805306368 | bytes 8585216 | tf_op jit(solution)/shard_map/slot_chunk0/nesd,nesh->edh/dot_general | solution.py:223
  222.9 2.9 fusion.17
  225.8 3.7 %fusion.2 = bf16[1,4096,384]{2,1,0:T(8,128)(2,1)} fusion(bf16[64,4,384]{2,0,1:T(8,128)(2,1)S(1)} %fusion.50, f32[4096,384,1]{1,0,2:T(8,128)S(1)} %fusion.16, bf16[64,1,4,4096]{3,2,0,1:T(4,128)(2,1)S(1)} %copy-done.5), kind=kOutput, calls=%fused_computation.9 | convolution fusion | flops 808452096 | bytes 11730944 | tf_op jit(solution)/shard_map/slot_chunk1/nesd,nesh->edh/dot_general | solution.py:223
  229.5 4.8 %fusion.3 = bf16[1,384,4096]{2,1,0:T(8,128)(2,1)} fusion(f32[384,4096,1]{1,0,2:T(8,128)S(1)} %fusion.17, bf16[64,1,4,4096]{3,2,0,1:T(4,128)(2,1)S(1)} %copy-done.3, f32[64,1,4,384]{3,0,2,1:T(8,128)S(1)} %copy-done.20), kind=kOutput, calls=%fused_computation.10 | convolution fusion | flops 808943616 | bytes 11927552 | tf_op jit(solution)/shard_map/slot_chunk1/nesh,nesd->ehd/dot_general | solution.py:220
  234.3 33.4 %slot_chunk1.3 = bf16[64,8,1024]{2,1,0:T(8,128)(2,1)} custom-call(bf16[64,8,1024]{2,1,0:T(8,128)(2,1)} %bitcast.235), custom_call_target="tpu_custom_call" | custom-call | bytes 2097152 | tf_op jit(solution)/shard_map/slot_chunk1/pallas_call | solution.py:63
  267.7 3.0 fusion.70
  270.8 34.5 %slot_chunk0.3 = bf16[64,8,1024]{2,1,0:T(8,128)(2,1)} custom-call(bf16[64,8,1024]{2,1,0:T(8,128)(2,1)} %bitcast.236), custom_call_target="tpu_custom_call" | custom-call | bytes 2097152 | tf_op jit(solution)/shard_map/slot_chunk0/pallas_call | solution.py:63
  305.3 2.1 fusion.69
  (75 shorter events, 17.4 us)
Async XLA Ops:
  7.2 79.7 %copy-start = (bf16[1,4096,384]{2,1,0:T(8,128)(2,1)S(1)}, bf16[1,4096,384]{2,1,0:T(8,128)(2,1)}, u32[]{:S(2)}) copy-start(bf16[1,4096,384]{2,1,0:T(8,128)(2,1)} %param.10) | copy-start | bytes 9437188
  7.2 227.1 %reduce-scatter.5.cloned.1.call-start = ((), (), s32[]{:S(2)}) async-start(), calls=%async_computation.3 | async-start | bytes 5242880 | tf_op jit(solution)/shard_map/slot_chunk1/reduce_scatter | solution.py:230
  9.2 2.2 copy-start.15
  9.2 2.2 copy-start.16
  9.2 2.7 copy-start.13
  11.2 2.1 copy-start.14
  86.8 2.0 copy-start.4
  86.8 4.7 %copy-start.2 = (bf16[64,1,4,4096]{3,2,0,1:T(4,128)(2,1)}, bf16[64,1,4,4096]{3,2,0,1:T(4,128)(2,1)S(1)}, u32[]{:S(2)}) copy-start(bf16[64,1,4,4096]{3,2,0,1:T(4,128)(2,1)S(1)} %get-tuple-element.9) | copy-start | bytes 6291460
  86.9 3.4 %copy-start.17 = (bf16[1,384,4096]{2,1,0:T(8,128)(2,1)S(1)}, bf16[1,384,4096]{2,1,0:T(8,128)(2,1)}, u32[]{:S(2)}) copy-start(bf16[1,384,4096]{2,1,0:T(8,128)(2,1)} %param.11) | copy-start | bytes 9437188
  90.3 1.3 copy-start.19
  101.4 169.4 %reduce-scatter.3.cloned.1.call-start = ((), (), s32[]{:S(2)}) async-start(), calls=%async_computation.2 | async-start | bytes 5242880 | tf_op jit(solution)/shard_map/slot_chunk0/reduce_scatter | solution.py:230
  203.6 1.9 copy-start.8
  203.6 2.1 copy-start.6
  203.6 3.5 %copy-start.18 = (bf16[1,384,4096]{2,1,0:T(8,128)(2,1)S(1)}, bf16[1,384,4096]{2,1,0:T(8,128)(2,1)}, u32[]{:S(2)}) copy-start(bf16[1,384,4096]{2,1,0:T(8,128)(2,1)} %param.11) | copy-start | bytes 9437188
  205.4 6.4 %copy-start.21 = (f32[64,1,4,384]{3,0,2,1:T(8,128)}, f32[64,1,4,384]{3,0,2,1:T(8,128)S(1)}, u32[]{:S(2)}) copy-start(f32[64,1,4,384]{3,0,2,1:T(8,128)S(1)} %fusion.20) | copy-start | bytes 1179652
  208.9 1.3 copy-start.11
  219.4 3.5 %copy-start.7 = (bf16[64,1,4,4096]{3,2,0,1:T(4,128)(2,1)S(1)}, bf16[64,1,4,4096]{3,2,0,1:T(4,128)(2,1)}, u32[]{:S(2)}) copy-start(bf16[64,1,4,4096]{3,2,0,1:T(4,128)(2,1)} %copy-done.6) | copy-start | bytes 6291460
  219.4 3.5 %copy-start.22 = (f32[64,1,4,384]{3,0,2,1:T(8,128)S(1)}, f32[64,1,4,384]{3,0,2,1:T(8,128)}, u32[]{:S(2)}) copy-start(f32[64,1,4,384]{3,0,2,1:T(8,128)} %copy-done.21) | copy-start | bytes 1179652
  222.9 2.9 copy-start.5
  225.8 3.7 %copy-start.3 = (bf16[64,1,4,4096]{3,2,0,1:T(4,128)(2,1)S(1)}, bf16[64,1,4,4096]{3,2,0,1:T(4,128)(2,1)}, u32[]{:S(2)}) copy-start(bf16[64,1,4,4096]{3,2,0,1:T(4,128)(2,1)} %copy-done.2) | copy-start | bytes 6291460
  225.8 3.7 %copy-start.20 = (f32[64,1,4,384]{3,0,2,1:T(8,128)S(1)}, f32[64,1,4,384]{3,0,2,1:T(8,128)}, u32[]{:S(2)}) copy-start(f32[64,1,4,384]{3,0,2,1:T(8,128)} %copy-done.19) | copy-start | bytes 1179652
  305.2 2.2 copy-start.10
  305.2 3.8 %copy-start.9 = (bf16[64,1,4,1024]{3,2,0,1:T(4,128)(2,1)S(1)}, bf16[64,1,4,1024]{3,2,0,1:T(4,128)(2,1)}, u32[]{:S(2)}) copy-start(bf16[64,1,4,1024]{3,2,0,1:T(4,128)(2,1)} %get-tuple-element.12) | copy-start | bytes 1572868
  305.2 5.4 %copy-start.1 = (bf16[1,4096,384]{2,1,0:T(8,128)(2,1)S(1)}, bf16[1,4096,384]{2,1,0:T(8,128)(2,1)}, u32[]{:S(2)}) copy-start(bf16[1,4096,384]{2,1,0:T(8,128)(2,1)} %param.10) | copy-start | bytes 9437188
  (1 other events, 0.9 us)
Sparse Core Ops, SparseCore 0:
  101.5 92.4 reduce-scatter.4
  218.6 46.9 reduce-scatter.2

commit v5 on v4

--- a/solution.py
+++ b/solution.py
@@ -199,14 +199,8 @@
     )(x)
 
 
-def expert_chunk(rows, scaled, w_in, w_out, quarter, ids):
-    slots = rows.shape[2]
-    send = jnp.concatenate([rows, scaled], axis=2)
-    groups = lax.axis_size("tensor")
-    spread = dispatch(send.reshape(send.shape[0], -1, quarter), groups, ids[0])
-    whole = jnp.swapaxes(spread, 1, 2).reshape(send.shape[:3] + (groups * quarter,))
-    expert_rows = whole[:, :, :slots]
-    expert_scaled = whole[:, :, slots:]
+def expert_chunk(expert_rows, expert_scaled, w_in, w_out, quarter, collective_id):
+    slots = expert_rows.shape[2]
     preact = jnp.einsum("nesd,edh->nesh", expert_rows, w_in, preferred_element_type=jnp.float32)
     sigmoid_val = jax.nn.sigmoid(preact)
     hidden = (preact * sigmoid_val).astype(jnp.bfloat16)
@@ -228,12 +222,13 @@
         [out_part.astype(jnp.bfloat16), grad_part.astype(jnp.bfloat16)], axis=2
     )
     sums = lax.psum_scatter(parts, "tensor", scatter_dimension=3, tiled=True)
-    back = expert_all_to_all(sums.reshape(sums.shape[0], -1, quarter), ids[1]).reshape(sums.shape)
+    back = expert_all_to_all(sums.reshape(sums.shape[0], -1, quarter), collective_id).reshape(sums.shape)
     return back[:, :, :slots], back[:, :, slots:], d_w_in, d_w_out
 
 
 def shards(tokens, cotangent, routing, gates, w_in, w_out):
     devices = lax.axis_size("expert")
+    groups = lax.axis_size("tensor")
     local_experts = w_in.shape[0]
     experts = devices * local_experts
     tok_rows = routing.shape[0]
@@ -261,15 +256,22 @@
     scaled = jnp.einsum(
         "tr,td->rd", weighting, cotangent.astype(jnp.float32), precision=highest
     ).astype(jnp.bfloat16)
-    rows = rows.reshape(devices, local_experts, capacity, quarter)
-    scaled = scaled.reshape(devices, local_experts, capacity, quarter)
+    send = jnp.concatenate(
+        [
+            rows.reshape(devices, local_experts * capacity, quarter),
+            scaled.reshape(devices, local_experts * capacity, quarter),
+        ],
+        axis=1,
+    )
+    spread = dispatch(send, groups, 0)
+    whole = jnp.swapaxes(spread, 1, 2).reshape(devices, 2, local_experts, capacity, groups * quarter)
     step = capacity // CHUNKS
     back_out, back_grad, d_w_in, d_w_out = [], [], None, None
     for c in range(CHUNKS):
         window = slice(c * step, (c + 1) * step)
         with jax.named_scope(f"slot_chunk{c}"):
             b_out, b_grad, g_in, g_out = expert_chunk(
-                rows[:, :, window], scaled[:, :, window], w_in, w_out, quarter, (2 * c, 2 * c + 1)
+                whole[:, 0, :, window], whole[:, 1, :, window], w_in, w_out, quarter, 1 + c
             )
         back_out.append(b_out)
         back_grad.append(b_grad)

time: 323 us -> 327 us (1.012); the launches traced: 318 us -> 326 us
  Pallas kernels: 229 us -> 183 us
  waiting for transfers between devices: 0.04 us -> 27.7 us
  local copies, waits for them, and re-layouts: 31.5 us -> 54.4 us
  matrix products: 32 us -> 37.5 us
    pallas_call x2 -> x1, Pallas kernels: 161 us -> 113 us  [dispatch(): pl.pallas_call(_dispatch_kernel, out_shape=jax.ShapeDtypeStruct((n, group...]
    reduce_scatter x2, waiting for transfers between devices: 0.01 us -> 27.6 us  [expert_chunk(): sums = lax.psum_scatter(parts, 'tensor', scatter_dimension=3, tiled=True)]
    reshape x0 -> x2, local copies, waits for them, and re-layouts: none -> 26.5 us  [shards(): jnp.swapaxes(spread, 1, 2)]
    convert_element_type x0 -> x2, local copies, waits for them, and re-layouts: none -> 18 us  [expert_chunk(): grad_part.astype(jnp.bfloat16)]
    slice x4 -> x0, local copies, waits for them, and re-layouts: 12.3 us -> none  [the longest x2 11.6 us: expert_chunk(): expert_rows = whole[:, :, :slots]]
    unnamed x52 -> x34, local copies, waits for them, and re-layouts: 11.6 us -> 2.5 us
  transfers between devices with their start and end apart: 2 -> 2, of which waited for: 0 -> 2; matrix products, arithmetic and copies ran while one was open for 11% -> 12% of each run, Pallas kernels for 41% -> 11%
where the time goes in v5:
time: 327 us; the launch traced here: 326 us
  Pallas kernels  183 us (56%)
  local copies, waits for them, and re-layouts  54.4 us (17%)
  matrix products  37.5 us (11%)
  waiting for transfers between devices  27.7 us (8%)
  between operations  14.4 us (4%)
  other arithmetic  9.81 us (3%)
    pallas_call x1, Pallas kernels, dispatch(): pl.pallas_call(_dispatch_kernel, out_shape=jax.ShapeDtypeStruct((n, group...  113 us
    pallas_call x2, Pallas kernels, expert_all_to_all(): pl.pallas_call(_a2a_kernel, out_shape=jax.ShapeDtypeStruct(x.shape, x.dty...  69.8 us
    reduce_scatter x2, waiting for transfers between devices, expert_chunk(): sums = lax.psum_scatter(parts, 'tensor', scatter_dimension=3, tiled=True)  27.6 us
    reshape x2, local copies, waits for them, and re-layouts, shards(): jnp.swapaxes(spread, 1, 2)  26.5 us
    convert_element_type x2, local copies, waits for them, and re-layouts, expert_chunk(): grad_part.astype(jnp.bfloat16)  18 us
    dot_general x2, matrix products, expert_chunk(): jnp.einsum('nesd,nesh->edh', expert_rows, grad_preact, preferred_element_...  7.65 us
    dot_general x2, matrix products, expert_chunk(): jnp.einsum('nesh,nesd->ehd', hidden, expert_scaled, preferred_element_typ...  7.13 us
    concatenate x2, other arithmetic, expert_chunk(): jnp.concatenate([out_part.astype(jnp.bfloat16), grad_part.astype(jnp.bflo...  6.9 us
  transfers between devices with their start and end apart: 2, of which 2 were waited for; matrix products, arithmetic and copies ran while one was open for 12% of the time, Pallas kernels for 11%

profile of v5, /device:TPU:7, one launch (start us, length us, event | category | flops | bytes accessed | tf_op | source)
XLA Modules:
  0.0 326.3 jit_solution(12020977711444691166)
XLA Ops:
  10.0 1.9 gather_fusion
  15.8 112.7 %shard_map.93 = bf16[64,4,16,1024]{3,2,1,0:T(8,128)(2,1)} custom-call(bf16[64,16,1024]{2,1,0:T(8,128)(2,1)} %pad_maximum_fusion.2.x_ref), custom_call_target="tpu_custom_call" | custom-call | bytes 18874368 | tf_op jit(solution)/shard_map/pallas_call | solution.py:183
  128.6 12.1 %copy.61 = bf16[64,16,4,1024]{3,2,0,1:T(4,128)(2,1)} copy(bf16[64,16,4,1024]{3,1,2,0:T(8,128)(2,1)} %bitcast.216) | data formatting | bytes 16777216 | tf_op jit(solution)/shard_map/reshape | solution.py:267
  140.7 14.4 %reshape.156 = bf16[64,2,1,8,4096]{4,0,3,2,1:T(8,128)(2,1)} reshape(bf16[64,16,4,1024]{3,2,0,1:T(4,128)(2,1)} %copy.61) | data formatting | bytes 16777216 | tf_op jit(solution)/shard_map/reshape | solution.py:267
  155.1 3.0 fusion.20
  158.1 2.9 fusion.53
  163.6 9.0 %copy_bitcast_fusion.2 = (bf16[64,1,4,4096]{3,2,0,1:T(4,128)(2,1)S(1)}, bf16[64,1,4,4096]{3,2,0,1:T(4,128)(2,1)S(1)}) fusion(bf16[64,4,4096]{2,0,1:T(8,128)(2,1)S(1)} %convolution_convert_fusion.2, bf16[64,4,4096]{2,0,1:T(8,128)(2,1)S(1)} %convolution_convert_fusion.3), kind=kLoop, calls=%fused_computation.27 | loop fusion | bytes 8388608 | tf_op jit(solution)/shard_map/slot_chunk0/convert_element_type | solution.py:222
  172.5 3.4 %pad_maximum_fusion = bf16[64,1,8,4096]{3,2,0,1:T(8,128)(2,1)} fusion(bf16[64,1,4,4096]{3,2,0,1:T(4,128)(2,1)S(1)} %get-tuple-element.12, bf16[64,1,4,4096]{3,2,0,1:T(4,128)(2,1)S(1)} %get-tuple-element.13), kind=kLoop, calls=%fused_computation.11 | loop fusion | flops 8388608 | bytes 8388608 | tf_op jit(solution)/shard_map/slot_chunk0/concatenate | solution.py:221
  176.1 3.0 fusion.23
  179.1 3.0 fusion.50
  185.3 9.0 %copy_bitcast_fusion = (bf16[64,1,4,4096]{3,2,0,1:T(4,128)(2,1)S(1)}, bf16[64,1,4,4096]{3,2,0,1:T(4,128)(2,1)S(1)}) fusion(bf16[64,4,4096]{2,0,1:T(8,128)(2,1)S(1)} %convolution_convert_fusion, bf16[64,4,4096]{2,0,1:T(8,128)(2,1)S(1)} %convolution_convert_fusion.1), kind=kLoop, calls=%fused_computation.25 | loop fusion | bytes 8388608 | tf_op jit(solution)/shard_map/slot_chunk1/convert_element_type | solution.py:222
  194.3 3.5 %pad_maximum_fusion.1 = bf16[64,1,8,4096]{3,2,0,1:T(8,128)(2,1)} fusion(bf16[64,1,4,4096]{3,2,0,1:T(4,128)(2,1)S(1)} %get-tuple-element.10, bf16[64,1,4,4096]{3,2,0,1:T(4,128)(2,1)S(1)} %get-tuple-element.11), kind=kLoop, calls=%fused_computation.12 | loop fusion | flops 8388608 | bytes 8388608 | tf_op jit(solution)/shard_map/slot_chunk1/concatenate | solution.py:221
  197.8 2.9 fusion.16
  200.8 2.7 fusion.17
  203.5 4.7 %fusion.2 = bf16[1,4096,384]{2,1,0:T(8,128)(2,1)} fusion(bf16[64,4,384]{2,0,1:T(8,128)(2,1)S(1)} %copy-done.8, f32[4096,384,1]{1,0,2:T(8,128)S(1)} %fusion.16, bf16[64,2,1,8,4096]{4,0,3,2,1:T(8,128)(2,1)} %reshape.156), kind=kOutput, calls=%fused_computation.9 | convolution fusion | flops 808452096 | bytes 11730944 | tf_op jit(solution)/shard_map/slot_chunk1/nesd,nesh->edh/dot_general | solution.py:217
  208.2 4.4 %fusion.3 = bf16[1,384,4096]{2,1,0:T(8,128)(2,1)} fusion(f32[384,4096,1]{1,0,2:T(8,128)S(1)} %fusion.17, bf16[64,2,1,8,4096]{4,0,3,2,1:T(8,128)(2,1)} %reshape.156, f32[64,1,4,384]{3,0,2,1:T(8,128)S(1)} %copy-done.15), kind=kOutput, calls=%fused_computation.10 | convolution fusion | flops 808943616 | bytes 11927552 | tf_op jit(solution)/shard_map/slot_chunk1/nesh,nesd->ehd/dot_general | solution.py:214
  212.7 13.7 %reduce-scatter.3.cloned.1.call-done = bf16[64,1,8,1024]{3,2,0,1:T(8,128)(2,1)} async-done(((bf16[64,1,8,4096]{3,2,0,1:T(8,128)(2,1)}), bf16[64,1,8,1024]{3,2,0,1:T(8,128)(2,1)}) %reduce-scatter.3.cloned.1.call-update) | async-done | bytes 1048592 | tf_op jit(solution)/shard_map/slot_chunk0/reduce_scatter | solution.py:224
  226.4 34.9 %slot_chunk0.1 = bf16[64,8,1024]{2,1,0:T(8,128)(2,1)} custom-call(bf16[64,8,1024]{2,1,0:T(8,128)(2,1)} %bitcast.219), custom_call_target="tpu_custom_call" | custom-call | bytes 2097152 | tf_op jit(solution)/shard_map/slot_chunk0/pallas_call | solution.py:63
  261.3 3.0 fusion.67
  264.3 13.9 %reduce-scatter.5.cloned.1.call-done = bf16[64,1,8,1024]{3,2,0,1:T(8,128)(2,1)} async-done(((bf16[64,1,8,4096]{3,2,0,1:T(8,128)(2,1)}), bf16[64,1,8,1024]{3,2,0,1:T(8,128)(2,1)}) %reduce-scatter.5.cloned.1.call-update) | async-done | bytes 1048592 | tf_op jit(solution)/shard_map/slot_chunk1/reduce_scatter | solution.py:224
  278.2 34.9 %slot_chunk1.1 = bf16[64,8,1024]{2,1,0:T(8,128)(2,1)} custom-call(bf16[64,8,1024]{2,1,0:T(8,128)(2,1)} %bitcast.220), custom_call_target="tpu_custom_call" | custom-call | bytes 2097152 | tf_op jit(solution)/shard_map/slot_chunk1/pallas_call | solution.py:63
  313.2 2.0 fusion.68
  315.2 2.7 convolution_convert_fusion.7
  317.9 1.6 convolution_convert_fusion.6
  (56 shorter events, 12.5 us)
Async XLA Ops:
  7.2 147.9 %copy-start = (bf16[1,4096,384]{2,1,0:T(8,128)(2,1)S(1)}, bf16[1,4096,384]{2,1,0:T(8,128)(2,1)}, u32[]{:S(2)}) copy-start(bf16[1,4096,384]{2,1,0:T(8,128)(2,1)} %param.10) | copy-start | bytes 9437188
  7.2 219.2 %reduce-scatter.3.cloned.1.call-start = ((), (), s32[]{:S(2)}) async-start(), calls=%async_computation.2 | async-start | bytes 5242880 | tf_op jit(solution)/shard_map/slot_chunk0/reduce_scatter | solution.py:224
  10.0 2.1 copy-start.11
  10.0 2.6 copy-start.9
  10.0 3.3 copy-start.10
  12.6 0.6 copy-start.2
  12.6 0.6 copy-start.4
  155.1 3.0 copy-start.12
  161.0 2.6 copy-start.6
  176.0 102.2 %reduce-scatter.5.cloned.1.call-start = ((), (), s32[]{:S(2)}) async-start(), calls=%async_computation.3 | async-start | bytes 5242880 | tf_op jit(solution)/shard_map/slot_chunk1/reduce_scatter | solution.py:224
  176.0 3.0 copy-start.13
  179.1 5.0 %copy-start.14 = (f32[64,1,4,384]{3,0,2,1:T(8,128)}, f32[64,1,4,384]{3,0,2,1:T(8,128)S(1)}, u32[]{:S(2)}) copy-start(f32[64,1,4,384]{3,0,2,1:T(8,128)S(1)} %fusion.23) | copy-start | bytes 1179652
  182.1 0.7 copy-start.7
  200.8 2.7 copy-start.8
  203.5 4.7 %copy-start.15 = (f32[64,1,4,384]{3,0,2,1:T(8,128)S(1)}, f32[64,1,4,384]{3,0,2,1:T(8,128)}, u32[]{:S(2)}) copy-start(f32[64,1,4,384]{3,0,2,1:T(8,128)} %copy-done.14) | copy-start | bytes 1179652
  261.3 53.9 %copy-start.5 = (f32[32,512]{1,0:T(8,128)S(1)}, f32[32,512]{1,0:T(8,128)}, u32[]{:S(2)}) copy-start(f32[32,512]{1,0:T(8,128)} %copy-done.4) | copy-start | bytes 196612
  264.3 53.6 %copy-start.3 = (f32[32,512]{1,0:T(8,128)S(1)}, f32[32,512]{1,0:T(8,128)}, u32[]{:S(2)}) copy-start(f32[32,512]{1,0:T(8,128)} %copy-done.2) | copy-start | bytes 196612
  313.2 4.7 %copy-start.1 = (bf16[64,1,4,1024]{3,2,0,1:T(4,128)(2,1)S(1)}, bf16[64,1,4,1024]{3,2,0,1:T(4,128)(2,1)}, u32[]{:S(2)}) copy-start(bf16[64,1,4,1024]{3,2,0,1:T(4,128)(2,1)} %get-tuple-element.6) | copy-start | bytes 1572868
Sparse Core Ops, SparseCore 0:
  176.1 50.2 reduce-scatter.2
  229.1 49.1 reduce-scatter.4

commit v6 on v5

--- a/solution.py
+++ b/solution.py
@@ -78,11 +78,14 @@
 
 
 def _dispatch_kernel(x_ref, o_ref, xz_send, xz_recv, y_send, y_recv, local_sem):
-    n = x_ref.shape[0]
-    groups = o_ref.shape[1]
+    n, rows, width = x_ref.shape
+    groups = o_ref.shape[2] // width
     me = lax.axis_index("expert")
     tau = lax.axis_index("tensor")
     barrier = pltpu.get_barrier_semaphore()
+
+    def cols(g):
+        return pl.ds(pl.multiple_of(g * width, 128), width)
 
     def greet(k, carry):
         pl.semaphore_signal(
@@ -97,14 +100,14 @@
         )
     pl.semaphore_wait(barrier, n - 1 + groups - 1)
 
-    local = pltpu.make_async_copy(x_ref.at[me], o_ref.at[me, tau], local_sem)
+    local = pltpu.make_async_copy(x_ref.at[me], o_ref.at[me, :, cols(tau)], local_sem)
     local.start()
 
     def xz_copy(k):
         peer = lax.rem(me + k, n)
         return pltpu.make_async_remote_copy(
             src_ref=x_ref.at[peer],
-            dst_ref=o_ref.at[me, tau],
+            dst_ref=o_ref.at[me, :, cols(tau)],
             send_sem=xz_send.at[k],
             recv_sem=xz_recv.at[k],
             device_id=(peer, tau),
@@ -116,7 +119,7 @@
         source = lax.rem(me + n - k, n)
         return pltpu.make_async_remote_copy(
             src_ref=x_ref.at[peer],
-            dst_ref=o_ref.at[source, tau],
+            dst_ref=o_ref.at[source, :, cols(tau)],
             send_sem=xz_send.at[k],
             recv_sem=xz_recv.at[k],
             device_id=(peer, tau),
@@ -126,8 +129,8 @@
     def y_copy(j, k):
         source = lax.rem(me + n - k, n)
         return pltpu.make_async_remote_copy(
-            src_ref=o_ref.at[source, tau],
-            dst_ref=o_ref.at[source, tau],
+            src_ref=o_ref.at[source, :, cols(tau)],
+            dst_ref=o_ref.at[source, :, cols(tau)],
             send_sem=y_send.at[j - 1, k],
             recv_sem=y_recv.at[j - 1, k],
             device_id=(me, lax.rem(tau + j, groups)),
@@ -137,8 +140,8 @@
     def y_arrival(j, k):
         source = lax.rem(me + n - k, n)
         return pltpu.make_async_remote_copy(
-            src_ref=o_ref.at[source, tau],
-            dst_ref=o_ref.at[source, lax.rem(tau + groups - j, groups)],
+            src_ref=o_ref.at[source, :, cols(tau)],
+            dst_ref=o_ref.at[source, :, cols(lax.rem(tau + groups - j, groups))],
             send_sem=y_send.at[j - 1, k],
             recv_sem=y_recv.at[j - 1, k],
             device_id=(me, lax.rem(tau + j, groups)),
@@ -182,7 +185,7 @@
     n, rows, width = x.shape
     return pl.pallas_call(
         _dispatch_kernel,
-        out_shape=jax.ShapeDtypeStruct((n, groups, rows, width), x.dtype),
+        out_shape=jax.ShapeDtypeStruct((n, rows, groups * width), x.dtype),
         in_specs=[pl.BlockSpec(memory_space=pl.ANY)],
         out_specs=pl.BlockSpec(memory_space=pl.ANY),
         scratch_shapes=[
@@ -256,22 +259,21 @@
     scaled = jnp.einsum(
         "tr,td->rd", weighting, cotangent.astype(jnp.float32), precision=highest
     ).astype(jnp.bfloat16)
+    step = capacity // CHUNKS
     send = jnp.concatenate(
         [
-            rows.reshape(devices, local_experts * capacity, quarter),
-            scaled.reshape(devices, local_experts * capacity, quarter),
+            rows.reshape(devices, local_experts, CHUNKS, step, quarter),
+            scaled.reshape(devices, local_experts, CHUNKS, step, quarter),
         ],
-        axis=1,
-    )
-    spread = dispatch(send, groups, 0)
-    whole = jnp.swapaxes(spread, 1, 2).reshape(devices, 2, local_experts, capacity, groups * quarter)
-    step = capacity // CHUNKS
+        axis=3,
+    )
+    spread = dispatch(send.reshape(devices, -1, quarter), groups, 0)
+    whole = spread.reshape(devices, local_experts, CHUNKS, 2 * step, groups * quarter)
     back_out, back_grad, d_w_in, d_w_out = [], [], None, None
     for c in range(CHUNKS):
-        window = slice(c * step, (c + 1) * step)
         with jax.named_scope(f"slot_chunk{c}"):
             b_out, b_grad, g_in, g_out = expert_chunk(
-                whole[:, 0, :, window], whole[:, 1, :, window], w_in, w_out, quarter, 1 + c
+                whole[:, :, c, :step], whole[:, :, c, step:], w_in, w_out, quarter, 1 + c
             )
         back_out.append(b_out)
         back_grad.append(b_grad)

time: 327 us -> 322 us (0.985); the launches traced: 326 us -> 317 us
  local copies, waits for them, and re-layouts: 54.4 us -> 42.1 us
    reshape x2, local copies, waits for them, and re-layouts: 26.5 us -> 4.48 us  [the longest x1 2.25 us: shards(): rows.reshape(devices, local_experts, CHUNKS, step, quarter)]
    slice x0 -> x1, local copies, waits for them, and re-layouts: none -> 10 us  [shards(): whole[:, :, c, :step]]
    reshape x0 -> x1, other arithmetic: none -> 3.94 us  [shards(): spread = dispatch(send.reshape(devices, -1, quarter), groups, 0)]
where the time goes in v6:
time: 322 us; the launch traced here: 317 us
  Pallas kernels  183 us (57%)
  local copies, waits for them, and re-layouts  42.1 us (13%)
  matrix products  35.8 us (11%)
  waiting for transfers between devices  28.6 us (9%)
  between operations  14.7 us (5%)
  other arithmetic  12.3 us (4%)
    pallas_call x1, Pallas kernels, dispatch(): pl.pallas_call(_dispatch_kernel, out_shape=jax.ShapeDtypeStruct((n, rows,...  113 us
    pallas_call x2, Pallas kernels, expert_all_to_all(): pl.pallas_call(_a2a_kernel, out_shape=jax.ShapeDtypeStruct(x.shape, x.dty...  70 us
    reduce_scatter x2, waiting for transfers between devices, expert_chunk(): sums = lax.psum_scatter(parts, 'tensor', scatter_dimension=3, tiled=True)  28.6 us
    convert_element_type x2, local copies, waits for them, and re-layouts, expert_chunk(): grad_part.astype(jnp.bfloat16)  17.6 us
    slice x1, local copies, waits for them, and re-layouts, shards(): whole[:, :, c, :step]  10 us
    dot_general x2, matrix products, expert_chunk(): jnp.einsum('nesh,nesd->ehd', hidden, expert_scaled, preferred_element_typ...  7.67 us
    dot_general x2, matrix products, expert_chunk(): jnp.einsum('nesd,nesh->edh', expert_rows, grad_preact, preferred_element_...  7.23 us
    concatenate x2, other arithmetic, expert_chunk(): jnp.concatenate([out_part.astype(jnp.bfloat16), grad_part.astype(jnp.bflo...  7.1 us
  transfers between devices with their start and end apart: 2, of which 2 were waited for; matrix products, arithmetic and copies ran while one was open for 12% of the time, Pallas kernels for 11%

profile of v6, /device:TPU:7, one launch (start us, length us, event | category | flops | bytes accessed | tf_op | source)
XLA Modules:
  0.0 316.6 jit_solution(13125865204884227037)
XLA Ops:
  9.2 1.9 gather_fusion
  13.4 2.2 reshape.123
  15.6 2.0 convolution_convert_fusion.4
  17.6 2.2 reshape.124
  19.8 3.9 %maximum_bitcast_fusion.x_ref = bf16[64,16,1024]{2,1,0:T(8,128)(2,1)} fusion(bf16[64,1,2,4,1024]{4,3,2,0,1:T(4,128)(2,1)} %reshape.124, bf16[64,1,2,4,1024]{4,3,2,0,1:T(4,128)(2,1)} %reshape.123), kind=kLoop, calls=%fused_computation.29 | loop fusion | flops 4194304 | bytes 4194304 | tf_op jit(solution)/shard_map/reshape | solution.py:270
  23.8 112.7 %shard_map.93 = bf16[64,16,4096]{2,1,0:T(8,128)(2,1)} custom-call(bf16[64,16,1024]{2,1,0:T(8,128)(2,1)} %maximum_bitcast_fusion.x_ref), custom_call_target="tpu_custom_call" | custom-call | bytes 18874368 | tf_op jit(solution)/shard_map/pallas_call | solution.py:186
  136.5 10.0 %fusion.65 = (bf16[64,1,1,4,4096]{4,3,2,0,1:T(4,128)(2,1)S(1)}, bf16[64,1,1,4,4096]{4,3,2,0,1:T(4,128)(2,1)}, bf16[64,1,1,4,4096]{4,3,2,0,1:T(4,128)(2,1)S(1)}, bf16[64,1,1,4,4096]{4,3,2,0,1:T(4,128)(2,1)}) fusion(bf16[64,1,2,8,4096]{4,3,2,0,1:T(8,128)(2,1)} %bitcast.212), kind=kLoop, calls=%fused_computation.77 | loop fusion | bytes 16777216 | tf_op jit(solution)/shard_map/slot_chunk0/slice | solution.py:276
  146.6 1.9 fusion.18
  151.3 1.9 fusion.51
  154.4 8.8 %copy_bitcast_fusion.2 = (bf16[64,1,4,4096]{3,2,0,1:T(4,128)(2,1)S(1)}, bf16[64,1,4,4096]{3,2,0,1:T(4,128)(2,1)S(1)}) fusion(bf16[64,4,4096]{2,0,1:T(8,128)(2,1)S(1)} %convolution_convert_fusion.2, bf16[64,4,4096]{2,0,1:T(8,128)(2,1)S(1)} %convolution_convert_fusion.3), kind=kLoop, calls=%fused_computation.27 | loop fusion | bytes 8388608 | tf_op jit(solution)/shard_map/slot_chunk0/convert_element_type | solution.py:225
  163.2 3.5 %pad_maximum_fusion = bf16[64,1,8,4096]{3,2,0,1:T(8,128)(2,1)} fusion(bf16[64,1,4,4096]{3,2,0,1:T(4,128)(2,1)S(1)} %get-tuple-element.16, bf16[64,1,4,4096]{3,2,0,1:T(4,128)(2,1)S(1)} %get-tuple-element.17), kind=kLoop, calls=%fused_computation.11 | loop fusion | flops 8388608 | bytes 8388608 | tf_op jit(solution)/shard_map/slot_chunk0/concatenate | solution.py:224
  167.0 3.6 %fusion.21 = f32[64,1,4,384]{3,0,2,1:T(8,128)S(1)} fusion(bf16[1,4096,384]{2,1,0:T(8,128)(2,1)S(1)} %copy-done, bf16[64,1,1,4,4096]{4,3,2,0,1:T(4,128)(2,1)} %get-tuple-element.7), kind=kOutput, calls=%fused_computation.39 | convolution fusion | flops 805306368 | bytes 5636096 | tf_op jit(solution)/shard_map/slot_chunk1/nesd,edh->nesh/dot_general | solution.py:207
  175.0 8.8 %copy_bitcast_fusion = (bf16[64,1,4,4096]{3,2,0,1:T(4,128)(2,1)S(1)}, bf16[64,1,4,4096]{3,2,0,1:T(4,128)(2,1)S(1)}) fusion(bf16[64,4,4096]{2,0,1:T(8,128)(2,1)S(1)} %convolution_convert_fusion, bf16[64,4,4096]{2,0,1:T(8,128)(2,1)S(1)} %convolution_convert_fusion.1), kind=kLoop, calls=%fused_computation.25 | loop fusion | bytes 8388608 | tf_op jit(solution)/shard_map/slot_chunk1/convert_element_type | solution.py:225
  183.8 3.6 %pad_maximum_fusion.1 = bf16[64,1,8,4096]{3,2,0,1:T(8,128)(2,1)} fusion(bf16[64,1,4,4096]{3,2,0,1:T(4,128)(2,1)S(1)} %get-tuple-element.14, bf16[64,1,4,4096]{3,2,0,1:T(4,128)(2,1)S(1)} %get-tuple-element.15), kind=kLoop, calls=%fused_computation.12 | loop fusion | flops 8388608 | bytes 8388608 | tf_op jit(solution)/shard_map/slot_chunk1/concatenate | solution.py:224
  187.5 3.5 %fusion.16 = f32[4096,384,1]{1,0,2:T(8,128)S(1)} fusion(bf16[64,4,384]{2,0,1:T(8,128)(2,1)S(1)} %fusion.51, bf16[64,1,1,4,4096]{4,3,2,0,1:T(4,128)(2,1)} %copy-done.7), kind=kOutput, calls=%fused_computation.34 | convolution fusion | flops 805306368 | bytes 8585216 | tf_op jit(solution)/shard_map/slot_chunk0/nesd,nesh->edh/dot_general | solution.py:220
  191.0 2.9 fusion.17
  194.0 3.7 %fusion.2 = bf16[1,4096,384]{2,1,0:T(8,128)(2,1)} fusion(bf16[64,4,384]{2,0,1:T(8,128)(2,1)S(1)} %copy-done.11, f32[4096,384,1]{1,0,2:T(8,128)S(1)} %fusion.16, bf16[64,1,1,4,4096]{4,3,2,0,1:T(4,128)(2,1)S(1)} %copy-done.4), kind=kOutput, calls=%fused_computation.9 | convolution fusion | flops 808452096 | bytes 11730944 | tf_op jit(solution)/shard_map/slot_chunk1/nesd,nesh->edh/dot_general | solution.py:220
  197.7 4.8 %fusion.3 = bf16[1,384,4096]{2,1,0:T(8,128)(2,1)} fusion(f32[384,4096,1]{1,0,2:T(8,128)S(1)} %fusion.17, bf16[64,1,1,4,4096]{4,3,2,0,1:T(4,128)(2,1)S(1)} %copy-done.3, f32[64,1,4,384]{3,0,2,1:T(8,128)S(1)} %copy-done.21), kind=kOutput, calls=%fused_computation.10 | convolution fusion | flops 808943616 | bytes 11927552 | tf_op jit(solution)/shard_map/slot_chunk1/nesh,nesd->ehd/dot_general | solution.py:217
  202.5 14.6 %reduce-scatter.3.cloned.1.call-done = bf16[64,1,8,1024]{3,2,0,1:T(8,128)(2,1)} async-done(((bf16[64,1,8,4096]{3,2,0,1:T(8,128)(2,1)}), bf16[64,1,8,1024]{3,2,0,1:T(8,128)(2,1)}) %reduce-scatter.3.cloned.1.call-update) | async-done | bytes 1048592 | tf_op jit(solution)/shard_map/slot_chunk0/reduce_scatter | solution.py:227
  217.1 34.9 %slot_chunk0.1 = bf16[64,8,1024]{2,1,0:T(8,128)(2,1)} custom-call(bf16[64,8,1024]{2,1,0:T(8,128)(2,1)} %bitcast.215), custom_call_target="tpu_custom_call" | custom-call | bytes 2097152 | tf_op jit(solution)/shard_map/slot_chunk0/pallas_call | solution.py:63
  252.0 3.0 fusion.66
  255.1 13.9 %reduce-scatter.5.cloned.1.call-done = bf16[64,1,8,1024]{3,2,0,1:T(8,128)(2,1)} async-done(((bf16[64,1,8,4096]{3,2,0,1:T(8,128)(2,1)}), bf16[64,1,8,1024]{3,2,0,1:T(8,128)(2,1)}) %reduce-scatter.5.cloned.1.call-update) | async-done | bytes 1048592 | tf_op jit(solution)/shard_map/slot_chunk1/reduce_scatter | solution.py:227
  269.0 35.1 %slot_chunk1.1 = bf16[64,8,1024]{2,1,0:T(8,128)(2,1)} custom-call(bf16[64,8,1024]{2,1,0:T(8,128)(2,1)} %bitcast.216), custom_call_target="tpu_custom_call" | custom-call | bytes 2097152 | tf_op jit(solution)/shard_map/slot_chunk1/pallas_call | solution.py:63
  304.2 2.1 fusion.67
  (69 shorter events, 16.1 us)
Async XLA Ops:
  7.2 139.4 %copy-start = (bf16[1,4096,384]{2,1,0:T(8,128)(2,1)S(1)}, bf16[1,4096,384]{2,1,0:T(8,128)(2,1)}, u32[]{:S(2)}) copy-start(bf16[1,4096,384]{2,1,0:T(8,128)(2,1)} %param.10) | copy-start | bytes 9437188
  7.2 209.9 %reduce-scatter.3.cloned.1.call-start = ((), (), s32[]{:S(2)}) async-start(), calls=%async_computation.2 | async-start | bytes 5242880 | tf_op jit(solution)/shard_map/slot_chunk0/reduce_scatter | solution.py:227
  9.2 2.2 copy-start.14
  9.2 2.2 copy-start.15
  9.2 2.7 copy-start.12
  11.2 4.4 %copy-start.13 = (bf16[32,1024]{1,0:T(8,128)(2,1)S(1)}, bf16[32,1024]{1,0:T(8,128)(2,1)}, u32[]{:S(2)}) copy-start(bf16[32,1024]{1,0:T(8,128)(2,1)} %param.7) | copy-start | bytes 196612
  146.6 2.0 copy-start.7
  146.6 4.7 %copy-start.5 = (bf16[64,1,1,4,4096]{4,3,2,0,1:T(4,128)(2,1)}, bf16[64,1,1,4,4096]{4,3,2,0,1:T(4,128)(2,1)S(1)}, u32[]{:S(2)}) copy-start(bf16[64,1,1,4,4096]{4,3,2,0,1:T(4,128)(2,1)S(1)} %get-tuple-element.8) | copy-start | bytes 6291460
  146.6 3.4 %copy-start.16 = (bf16[1,384,4096]{2,1,0:T(8,128)(2,1)S(1)}, bf16[1,384,4096]{2,1,0:T(8,128)(2,1)}, u32[]{:S(2)}) copy-start(bf16[1,384,4096]{2,1,0:T(8,128)(2,1)} %param.11) | copy-start | bytes 9437188
  150.0 1.3 copy-start.18
  166.7 102.2 %reduce-scatter.5.cloned.1.call-start = ((), (), s32[]{:S(2)}) async-start(), calls=%async_computation.3 | async-start | bytes 5242880 | tf_op jit(solution)/shard_map/slot_chunk1/reduce_scatter | solution.py:227
  167.0 3.6 %copy-start.2 = (bf16[64,1,1,4,4096]{4,3,2,0,1:T(4,128)(2,1)S(1)}, bf16[64,1,1,4,4096]{4,3,2,0,1:T(4,128)(2,1)}, u32[]{:S(2)}) copy-start(bf16[64,1,1,4,4096]{4,3,2,0,1:T(4,128)(2,1)} %get-tuple-element.9) | copy-start | bytes 6291460
  167.0 3.6 %copy-start.17 = (bf16[1,384,4096]{2,1,0:T(8,128)(2,1)S(1)}, bf16[1,384,4096]{2,1,0:T(8,128)(2,1)}, u32[]{:S(2)}) copy-start(bf16[1,384,4096]{2,1,0:T(8,128)(2,1)} %param.11) | copy-start | bytes 9437188
  170.6 3.2 %copy-start.20 = (f32[64,1,4,384]{3,0,2,1:T(8,128)}, f32[64,1,4,384]{3,0,2,1:T(8,128)S(1)}, u32[]{:S(2)}) copy-start(f32[64,1,4,384]{3,0,2,1:T(8,128)S(1)} %fusion.21) | copy-start | bytes 1179652
  172.4 1.3 copy-start.10
  187.5 3.5 %copy-start.6 = (bf16[64,1,1,4,4096]{4,3,2,0,1:T(4,128)(2,1)S(1)}, bf16[64,1,1,4,4096]{4,3,2,0,1:T(4,128)(2,1)}, u32[]{:S(2)}) copy-start(bf16[64,1,1,4,4096]{4,3,2,0,1:T(4,128)(2,1)} %copy-done.5) | copy-start | bytes 6291460
  187.5 3.5 %copy-start.19 = (f32[64,1,4,384]{3,0,2,1:T(8,128)S(1)}, f32[64,1,4,384]{3,0,2,1:T(8,128)}, u32[]{:S(2)}) copy-start(f32[64,1,4,384]{3,0,2,1:T(8,128)} %copy-done.18) | copy-start | bytes 1179652
  191.0 2.9 copy-start.4
  191.0 2.9 copy-start.11
  194.0 3.7 %copy-start.3 = (bf16[64,1,1,4,4096]{4,3,2,0,1:T(4,128)(2,1)S(1)}, bf16[64,1,1,4,4096]{4,3,2,0,1:T(4,128)(2,1)}, u32[]{:S(2)}) copy-start(bf16[64,1,1,4,4096]{4,3,2,0,1:T(4,128)(2,1)} %get-tuple-element.9) | copy-start | bytes 6291460
  194.0 3.7 %copy-start.21 = (f32[64,1,4,384]{3,0,2,1:T(8,128)S(1)}, f32[64,1,4,384]{3,0,2,1:T(8,128)}, u32[]{:S(2)}) copy-start(f32[64,1,4,384]{3,0,2,1:T(8,128)} %copy-done.20) | copy-start | bytes 1179652
  304.1 2.2 copy-start.9
  304.1 3.8 %copy-start.8 = (bf16[64,1,4,1024]{3,2,0,1:T(4,128)(2,1)S(1)}, bf16[64,1,4,1024]{3,2,0,1:T(4,128)(2,1)}, u32[]{:S(2)}) copy-start(bf16[64,1,4,1024]{3,2,0,1:T(4,128)(2,1)} %get-tuple-element.11) | copy-start | bytes 1572868
  304.1 5.4 %copy-start.1 = (bf16[1,4096,384]{2,1,0:T(8,128)(2,1)S(1)}, bf16[1,4096,384]{2,1,0:T(8,128)(2,1)}, u32[]{:S(2)}) copy-start(bf16[1,4096,384]{2,1,0:T(8,128)(2,1)} %param.10) | copy-start | bytes 9437188
Sparse Core Ops, SparseCore 0:
  166.9 50.2 reduce-scatter.2
  219.8 49.1 reduce-scatter.4

commit v7 on v6

--- a/solution.py
+++ b/solution.py
@@ -78,8 +78,8 @@
 
 
 def _dispatch_kernel(x_ref, o_ref, xz_send, xz_recv, y_send, y_recv, local_sem):
-    n, rows, width = x_ref.shape
-    groups = o_ref.shape[2] // width
+    n, width = x_ref.shape[0], x_ref.shape[-1]
+    groups = o_ref.shape[-1] // width
     me = lax.axis_index("expert")
     tau = lax.axis_index("tensor")
     barrier = pltpu.get_barrier_semaphore()
@@ -100,14 +100,14 @@
         )
     pl.semaphore_wait(barrier, n - 1 + groups - 1)
 
-    local = pltpu.make_async_copy(x_ref.at[me], o_ref.at[me, :, cols(tau)], local_sem)
+    local = pltpu.make_async_copy(x_ref.at[me], o_ref.at[:, :, me, :, cols(tau)], local_sem)
     local.start()
 
     def xz_copy(k):
         peer = lax.rem(me + k, n)
         return pltpu.make_async_remote_copy(
             src_ref=x_ref.at[peer],
-            dst_ref=o_ref.at[me, :, cols(tau)],
+            dst_ref=o_ref.at[:, :, me, :, cols(tau)],
             send_sem=xz_send.at[k],
             recv_sem=xz_recv.at[k],
             device_id=(peer, tau),
@@ -119,7 +119,7 @@
         source = lax.rem(me + n - k, n)
         return pltpu.make_async_remote_copy(
             src_ref=x_ref.at[peer],
-            dst_ref=o_ref.at[source, :, cols(tau)],
+            dst_ref=o_ref.at[:, :, source, :, cols(tau)],
             send_sem=xz_send.at[k],
             recv_sem=xz_recv.at[k],
             device_id=(peer, tau),
@@ -129,8 +129,8 @@
     def y_copy(j, k):
         source = lax.rem(me + n - k, n)
         return pltpu.make_async_remote_copy(
-            src_ref=o_ref.at[source, :, cols(tau)],
-            dst_ref=o_ref.at[source, :, cols(tau)],
+            src_ref=o_ref.at[:, :, source, :, cols(tau)],
+            dst_ref=o_ref.at[:, :, source, :, cols(tau)],
             send_sem=y_send.at[j - 1, k],
             recv_sem=y_recv.at[j - 1, k],
             device_id=(me, lax.rem(tau + j, groups)),
@@ -140,8 +140,8 @@
     def y_arrival(j, k):
         source = lax.rem(me + n - k, n)
         return pltpu.make_async_remote_copy(
-            src_ref=o_ref.at[source, :, cols(tau)],
-            dst_ref=o_ref.at[source, :, cols(lax.rem(tau + groups - j, groups))],
+            src_ref=o_ref.at[:, :, source, :, cols(tau)],
+            dst_ref=o_ref.at[:, :, source, :, cols(lax.rem(tau + groups - j, groups))],
             send_sem=y_send.at[j - 1, k],
             recv_sem=y_recv.at[j - 1, k],
             device_id=(me, lax.rem(tau + j, groups)),
@@ -182,10 +182,10 @@
 
 
 def dispatch(x, groups, collective_id):
-    n, rows, width = x.shape
+    n, chunks, kinds, slots, width = x.shape
     return pl.pallas_call(
         _dispatch_kernel,
-        out_shape=jax.ShapeDtypeStruct((n, rows, groups * width), x.dtype),
+        out_shape=jax.ShapeDtypeStruct((chunks, kinds, n, slots, groups * width), x.dtype),
         in_specs=[pl.BlockSpec(memory_space=pl.ANY)],
         out_specs=pl.BlockSpec(memory_space=pl.ANY),
         scratch_shapes=[
@@ -260,20 +260,19 @@
         "tr,td->rd", weighting, cotangent.astype(jnp.float32), precision=highest
     ).astype(jnp.bfloat16)
     step = capacity // CHUNKS
-    send = jnp.concatenate(
+    send = jnp.stack(
         [
-            rows.reshape(devices, local_experts, CHUNKS, step, quarter),
-            scaled.reshape(devices, local_experts, CHUNKS, step, quarter),
+            rows.reshape(devices, local_experts * CHUNKS, step, quarter),
+            scaled.reshape(devices, local_experts * CHUNKS, step, quarter),
         ],
-        axis=3,
-    )
-    spread = dispatch(send.reshape(devices, -1, quarter), groups, 0)
-    whole = spread.reshape(devices, local_experts, CHUNKS, 2 * step, groups * quarter)
+        axis=2,
+    )
+    whole = dispatch(send, groups, 0)
     back_out, back_grad, d_w_in, d_w_out = [], [], None, None
     for c in range(CHUNKS):
         with jax.named_scope(f"slot_chunk{c}"):
             b_out, b_grad, g_in, g_out = expert_chunk(
-                whole[:, :, c, :step], whole[:, :, c, step:], w_in, w_out, quarter, 1 + c
+                whole[c, 0][:, None], whole[c, 1][:, None], w_in, w_out, quarter, 1 + c
             )
         back_out.append(b_out)
         back_grad.append(b_grad)

time: 322 us -> 322 us (level)
    another operation x0 -> x3, local copies, waits for them, and re-layouts: none -> 14 us
    slice x1 -> x0, local copies, waits for them, and re-layouts: 10 us -> none  [shards(): whole[:, :, c, :step]]
    reshape x2 -> x0, local copies, waits for them, and re-layouts: 4.48 us -> none  [the longest x1 2.25 us: shards(): rows.reshape(devices, local_experts, CHUNKS, step, quarter)]
    another operation x0 -> x1, other arithmetic: none -> 4.21 us  [shards(): jnp.stack([rows.reshape(devices, local_experts * CHUNKS, step, quarter),...]
    reshape x1 -> x0, other arithmetic: 3.94 us -> none  [shards(): spread = dispatch(send.reshape(devices, -1, quarter), groups, 0)]
where the time goes in v7:
time: 322 us; the launch traced here: 316 us
  Pallas kernels  183 us (57%)
  local copies, waits for them, and re-layouts  41.6 us (13%)
  matrix products  35.9 us (11%)
  waiting for transfers between devices  28.6 us (9%)
  between operations  14.7 us (5%)
  other arithmetic  12.6 us (4%)
    pallas_call x1, Pallas kernels, dispatch(): pl.pallas_call(_dispatch_kernel, out_shape=jax.ShapeDtypeStruct((chunks,...  113 us
    pallas_call x2, Pallas kernels, expert_all_to_all(): pl.pallas_call(_a2a_kernel, out_shape=jax.ShapeDtypeStruct(x.shape, x.dty...  70.1 us
    reduce_scatter x2, waiting for transfers between devices, expert_chunk(): sums = lax.psum_scatter(parts, 'tensor', scatter_dimension=3, tiled=True)  28.5 us
    convert_element_type x2, local copies, waits for them, and re-layouts, expert_chunk(): grad_part.astype(jnp.bfloat16)  17.6 us
    another operation x1, local copies, waits for them, and re-layouts  9.5 us
    dot_general x2, matrix products, expert_chunk(): jnp.einsum('nesh,nesd->ehd', hidden, expert_scaled, preferred_element_typ...  7.68 us
    dot_general x2, matrix products, expert_chunk(): jnp.einsum('nesd,nesh->edh', expert_rows, grad_preact, preferred_element_...  7.22 us
    concatenate x2, other arithmetic, expert_chunk(): jnp.concatenate([out_part.astype(jnp.bfloat16), grad_part.astype(jnp.bflo...  7.1 us
  transfers between devices with their start and end apart: 2, of which 2 were waited for; matrix products, arithmetic and copies ran while one was open for 12% of the time, Pallas kernels for 11%

profile of v7, /device:TPU:7, one launch (start us, length us, event | category | flops | bytes accessed | tf_op | source)
XLA Modules:
  0.0 316.4 jit_solution(16918539963143690363)
XLA Ops:
  9.2 1.9 gather_fusion
  13.4 2.2 stack_reshape.6
  15.6 2.0 convolution_convert_fusion.4
  17.6 2.2 stack_reshape.7
  19.8 4.2 %pad_maximum_fusion.2.x_ref = bf16[64,2,2,4,1024]{4,3,2,1,0:T(4,128)(2,1)} fusion(bf16[64,2,1,4,1024]{4,3,2,1,0:T(4,128)(2,1)} %stack_reshape.7, bf16[64,2,1,4,1024]{4,3,2,1,0:T(4,128)(2,1)} %stack_reshape.6), kind=kLoop, calls=%fused_computation.29 | loop fusion | flops 1048576 | bytes 4194304 | tf_op jit(solution)/shard_map/stack | solution.py:263
  24.1 112.7 %shard_map.93 = bf16[2,2,64,4,4096]{4,3,2,1,0:T(4,128)(2,1)} custom-call(bf16[64,2,2,4,1024]{4,3,2,1,0:T(4,128)(2,1)} %pad_maximum_fusion.2.x_ref), custom_call_target="tpu_custom_call" | custom-call | bytes 18874368 | tf_op jit(solution)/shard_map/pallas_call | solution.py:186
  136.8 9.5 %slice_bitcast_fusion.3 = (bf16[64,4,4096]{2,1,0:T(4,128)(2,1)S(1)}, bf16[64,4,4096]{2,1,0:T(4,128)(2,1)}, bf16[64,4,4096]{2,1,0:T(4,128)(2,1)}, bf16[64,4,4096]{2,1,0:T(4,128)(2,1)S(1)}) fusion(bf16[2,2,64,4,4096]{4,3,2,1,0:T(4,128)(2,1)} %shard_map.93), kind=kLoop, calls=%fused_computation.33 | loop fusion | bytes 16777216 | tf_op jit(solution)/shard_map/reshape.4
  146.4 2.0 fusion.26
  151.0 1.9 fusion.81
  154.2 8.8 %copy_bitcast_fusion.2 = (bf16[64,1,4,4096]{3,2,0,1:T(4,128)(2,1)S(1)}, bf16[64,1,4,4096]{3,2,0,1:T(4,128)(2,1)S(1)}) fusion(bf16[64,4,4096]{2,0,1:T(8,128)(2,1)S(1)} %convolution_convert_fusion.2, bf16[64,4,4096]{2,0,1:T(8,128)(2,1)S(1)} %convolution_convert_fusion.3), kind=kLoop, calls=%fused_computation.27 | loop fusion | bytes 8388608 | tf_op jit(solution)/shard_map/slot_chunk0/convert_element_type | solution.py:225
  163.0 3.5 %pad_maximum_fusion = bf16[64,1,8,4096]{3,2,0,1:T(8,128)(2,1)} fusion(bf16[64,1,4,4096]{3,2,0,1:T(4,128)(2,1)S(1)} %get-tuple-element.16, bf16[64,1,4,4096]{3,2,0,1:T(4,128)(2,1)S(1)} %get-tuple-element.17), kind=kLoop, calls=%fused_computation.11 | loop fusion | flops 8388608 | bytes 8388608 | tf_op jit(solution)/shard_map/slot_chunk0/concatenate | solution.py:224
  166.7 3.6 %fusion.31 = f32[64,1,4,384]{3,0,2,1:T(8,128)S(1)} fusion(bf16[1,4096,384]{2,1,0:T(8,128)(2,1)S(1)} %copy-done, bf16[64,4,4096]{2,1,0:T(4,128)(2,1)} %get-tuple-element.8), kind=kOutput, calls=%fused_computation.47 | convolution fusion | flops 805306368 | bytes 5636096 | tf_op jit(solution)/shard_map/slot_chunk1/nesd,edh->nesh/dot_general | solution.py:207
  174.8 8.8 %copy_bitcast_fusion = (bf16[64,1,4,4096]{3,2,0,1:T(4,128)(2,1)S(1)}, bf16[64,1,4,4096]{3,2,0,1:T(4,128)(2,1)S(1)}) fusion(bf16[64,4,4096]{2,0,1:T(8,128)(2,1)S(1)} %convolution_convert_fusion, bf16[64,4,4096]{2,0,1:T(8,128)(2,1)S(1)} %convolution_convert_fusion.1), kind=kLoop, calls=%fused_computation.25 | loop fusion | bytes 8388608 | tf_op jit(solution)/shard_map/slot_chunk1/convert_element_type | solution.py:225
  183.6 3.6 %pad_maximum_fusion.1 = bf16[64,1,8,4096]{3,2,0,1:T(8,128)(2,1)} fusion(bf16[64,1,4,4096]{3,2,0,1:T(4,128)(2,1)S(1)} %get-tuple-element.14, bf16[64,1,4,4096]{3,2,0,1:T(4,128)(2,1)S(1)} %get-tuple-element.15), kind=kLoop, calls=%fused_computation.12 | loop fusion | flops 8388608 | bytes 8388608 | tf_op jit(solution)/shard_map/slot_chunk1/concatenate | solution.py:224
  187.2 3.5 %fusion.23 = f32[4096,384,1]{1,0,2:T(8,128)S(1)} fusion(bf16[64,4,384]{2,0,1:T(8,128)(2,1)S(1)} %fusion.81, bf16[64,4,4096]{2,1,0:T(4,128)(2,1)} %copy-done.7), kind=kOutput, calls=%fused_computation.41 | convolution fusion | flops 805306368 | bytes 8585216 | tf_op jit(solution)/shard_map/slot_chunk0/nesd,nesh->edh/dot_general | solution.py:220
  190.8 2.9 fusion.20
  193.7 3.7 %fusion.2 = bf16[1,4096,384]{2,1,0:T(8,128)(2,1)} fusion(bf16[64,4,384]{2,0,1:T(8,128)(2,1)S(1)} %copy-done.11, f32[4096,384,1]{1,0,2:T(8,128)S(1)} %fusion.23, bf16[64,4,4096]{2,1,0:T(4,128)(2,1)S(1)} %copy-done.4), kind=kOutput, calls=%fused_computation.9 | convolution fusion | flops 808452096 | bytes 11730944 | tf_op jit(solution)/shard_map/slot_chunk1/nesd,nesh->edh/dot_general | solution.py:220
  197.4 4.8 %fusion.3 = bf16[1,384,4096]{2,1,0:T(8,128)(2,1)} fusion(f32[384,4096,1]{1,0,2:T(8,128)S(1)} %fusion.20, bf16[64,4,4096]{2,1,0:T(4,128)(2,1)S(1)} %copy-done.3, f32[64,1,4,384]{3,0,2,1:T(8,128)S(1)} %copy-done.21), kind=kOutput, calls=%fused_computation.10 | convolution fusion | flops 808943616 | bytes 11927552 | tf_op jit(solution)/shard_map/slot_chunk1/nesh,nesd->ehd/dot_general | solution.py:217
  202.2 14.6 %reduce-scatter.3.cloned.1.call-done = bf16[64,1,8,1024]{3,2,0,1:T(8,128)(2,1)} async-done(((bf16[64,1,8,4096]{3,2,0,1:T(8,128)(2,1)}), bf16[64,1,8,1024]{3,2,0,1:T(8,128)(2,1)}) %reduce-scatter.3.cloned.1.call-update) | async-done | bytes 1048592 | tf_op jit(solution)/shard_map/slot_chunk0/reduce_scatter | solution.py:227
  216.9 34.9 %slot_chunk0.1 = bf16[64,8,1024]{2,1,0:T(8,128)(2,1)} custom-call(bf16[64,8,1024]{2,1,0:T(8,128)(2,1)} %bitcast.179), custom_call_target="tpu_custom_call" | custom-call | bytes 2097152 | tf_op jit(solution)/shard_map/slot_chunk0/pallas_call | solution.py:63
  251.8 3.0 fusion.97
  254.8 13.9 %reduce-scatter.5.cloned.1.call-done = bf16[64,1,8,1024]{3,2,0,1:T(8,128)(2,1)} async-done(((bf16[64,1,8,4096]{3,2,0,1:T(8,128)(2,1)}), bf16[64,1,8,1024]{3,2,0,1:T(8,128)(2,1)}) %reduce-scatter.5.cloned.1.call-update) | async-done | bytes 1048592 | tf_op jit(solution)/shard_map/slot_chunk1/reduce_scatter | solution.py:227
  268.7 35.1 %slot_chunk1.1 = bf16[64,8,1024]{2,1,0:T(8,128)(2,1)} custom-call(bf16[64,8,1024]{2,1,0:T(8,128)(2,1)} %bitcast.180), custom_call_target="tpu_custom_call" | custom-call | bytes 2097152 | tf_op jit(solution)/shard_map/slot_chunk1/pallas_call | solution.py:63
  303.9 2.1 fusion.98
  (69 shorter events, 16.1 us)
Async XLA Ops:
  7.2 139.2 %copy-start = (bf16[1,4096,384]{2,1,0:T(8,128)(2,1)S(1)}, bf16[1,4096,384]{2,1,0:T(8,128)(2,1)}, u32[]{:S(2)}) copy-start(bf16[1,4096,384]{2,1,0:T(8,128)(2,1)} %param.10) | copy-start | bytes 9437188
  7.2 209.7 %reduce-scatter.3.cloned.1.call-start = ((), (), s32[]{:S(2)}) async-start(), calls=%async_computation.2 | async-start | bytes 5242880 | tf_op jit(solution)/shard_map/slot_chunk0/reduce_scatter | solution.py:227
  9.2 2.2 copy-start.14
  9.2 2.2 copy-start.15
  9.2 2.7 copy-start.12
  11.2 4.4 %copy-start.13 = (bf16[32,1024]{1,0:T(8,128)(2,1)S(1)}, bf16[32,1024]{1,0:T(8,128)(2,1)}, u32[]{:S(2)}) copy-start(bf16[32,1024]{1,0:T(8,128)(2,1)} %param.7) | copy-start | bytes 196612
  146.3 2.0 copy-start.7
  146.3 4.7 %copy-start.5 = (bf16[64,4,4096]{2,1,0:T(4,128)(2,1)}, bf16[64,4,4096]{2,1,0:T(4,128)(2,1)S(1)}, u32[]{:S(2)}) copy-start(bf16[64,4,4096]{2,1,0:T(4,128)(2,1)S(1)} %get-tuple-element.9) | copy-start | bytes 6291460
  146.3 3.4 %copy-start.16 = (bf16[1,384,4096]{2,1,0:T(8,128)(2,1)S(1)}, bf16[1,384,4096]{2,1,0:T(8,128)(2,1)}, u32[]{:S(2)}) copy-start(bf16[1,384,4096]{2,1,0:T(8,128)(2,1)} %param.11) | copy-start | bytes 9437188
  149.7 1.3 copy-start.18
  166.5 102.2 %reduce-scatter.5.cloned.1.call-start = ((), (), s32[]{:S(2)}) async-start(), calls=%async_computation.3 | async-start | bytes 5242880 | tf_op jit(solution)/shard_map/slot_chunk1/reduce_scatter | solution.py:227
  166.7 3.6 %copy-start.2 = (bf16[64,4,4096]{2,1,0:T(4,128)(2,1)S(1)}, bf16[64,4,4096]{2,1,0:T(4,128)(2,1)}, u32[]{:S(2)}) copy-start(bf16[64,4,4096]{2,1,0:T(4,128)(2,1)} %get-tuple-element.7) | copy-start | bytes 6291460
  166.7 3.6 %copy-start.17 = (bf16[1,384,4096]{2,1,0:T(8,128)(2,1)S(1)}, bf16[1,384,4096]{2,1,0:T(8,128)(2,1)}, u32[]{:S(2)}) copy-start(bf16[1,384,4096]{2,1,0:T(8,128)(2,1)} %param.11) | copy-start | bytes 9437188
  170.3 3.2 %copy-start.20 = (f32[64,1,4,384]{3,0,2,1:T(8,128)}, f32[64,1,4,384]{3,0,2,1:T(8,128)S(1)}, u32[]{:S(2)}) copy-start(f32[64,1,4,384]{3,0,2,1:T(8,128)S(1)} %fusion.31) | copy-start | bytes 1179652
  172.2 1.3 copy-start.10
  187.2 3.5 %copy-start.6 = (bf16[64,4,4096]{2,1,0:T(4,128)(2,1)S(1)}, bf16[64,4,4096]{2,1,0:T(4,128)(2,1)}, u32[]{:S(2)}) copy-start(bf16[64,4,4096]{2,1,0:T(4,128)(2,1)} %copy-done.5) | copy-start | bytes 6291460
  187.2 3.5 %copy-start.19 = (f32[64,1,4,384]{3,0,2,1:T(8,128)S(1)}, f32[64,1,4,384]{3,0,2,1:T(8,128)}, u32[]{:S(2)}) copy-start(f32[64,1,4,384]{3,0,2,1:T(8,128)} %copy-done.18) | copy-start | bytes 1179652
  190.8 2.9 copy-start.4
  190.8 2.9 copy-start.11
  193.7 3.7 %copy-start.3 = (bf16[64,4,4096]{2,1,0:T(4,128)(2,1)S(1)}, bf16[64,4,4096]{2,1,0:T(4,128)(2,1)}, u32[]{:S(2)}) copy-start(bf16[64,4,4096]{2,1,0:T(4,128)(2,1)} %get-tuple-element.7) | copy-start | bytes 6291460
  193.7 3.7 %copy-start.21 = (f32[64,1,4,384]{3,0,2,1:T(8,128)S(1)}, f32[64,1,4,384]{3,0,2,1:T(8,128)}, u32[]{:S(2)}) copy-start(f32[64,1,4,384]{3,0,2,1:T(8,128)} %copy-done.20) | copy-start | bytes 1179652
  303.9 2.2 copy-start.9
  303.9 3.8 %copy-start.8 = (bf16[64,1,4,1024]{3,2,0,1:T(4,128)(2,1)S(1)}, bf16[64,1,4,1024]{3,2,0,1:T(4,128)(2,1)}, u32[]{:S(2)}) copy-start(bf16[64,1,4,1024]{3,2,0,1:T(4,128)(2,1)} %get-tuple-element.11) | copy-start | bytes 1572868
  303.9 5.4 %copy-start.1 = (bf16[1,4096,384]{2,1,0:T(8,128)(2,1)S(1)}, bf16[1,4096,384]{2,1,0:T(8,128)(2,1)}, u32[]{:S(2)}) copy-start(bf16[1,4096,384]{2,1,0:T(8,128)(2,1)} %param.10) | copy-start | bytes 9437188
Sparse Core Ops, SparseCore 0:
  166.6 50.2 reduce-scatter.2
  219.6 49.1 reduce-scatter.4

commit v8 on v3

--- a/solution.py
+++ b/solution.py
@@ -63,8 +63,8 @@
     return pl.pallas_call(
         _a2a_kernel,
         out_shape=jax.ShapeDtypeStruct(x.shape, x.dtype),
-        in_specs=[pl.BlockSpec(memory_space=pl.ANY)],
-        out_specs=pl.BlockSpec(memory_space=pl.ANY),
+        in_specs=[pl.BlockSpec(memory_space=pltpu.VMEM)],
+        out_specs=pl.BlockSpec(memory_space=pltpu.VMEM),
         scratch_shapes=[
             pltpu.SemaphoreType.DMA((n,)),
             pltpu.SemaphoreType.DMA((n,)),

time: 313 us -> 317 us (1.013)
  Pallas kernels: 139 us -> 147 us
  waiting for transfers between devices: 76.4 us -> 72.5 us
    pallas_call x4, Pallas kernels: 139 us -> 147 us  [expert_all_to_all(): pl.pallas_call(_a2a_kernel, out_shape=jax.ShapeDtypeStruct(x.shape, x.dty...]
  transfers between devices with their start and end apart: 4 -> 4, of which waited for: 4 -> 4; matrix products, arithmetic and copies ran while one was open for 19% -> 18% of each run, Pallas kernels for 22% -> 23%
where the time goes in v8:
time: 317 us; the launch traced here: 312 us
  Pallas kernels  147 us (46%)
  waiting for transfers between devices  72.5 us (23%)
  local copies, waits for them, and re-layouts  32.7 us (10%)
  matrix products  31.9 us (10%)
  between operations  14.5 us (5%)
  other arithmetic  12.7 us (4%)
    pallas_call x4, Pallas kernels, expert_all_to_all(): pl.pallas_call(_a2a_kernel, out_shape=jax.ShapeDtypeStruct(x.shape, x.dty...  147 us
    all_gather x2, waiting for transfers between devices, expert_chunk(): whole = lax.all_gather(arrived, 'tensor', axis=3, tiled=True)  44.5 us
    reduce_scatter x2, waiting for transfers between devices, expert_chunk(): sums = lax.psum_scatter(parts, 'tensor', scatter_dimension=3, tiled=True)  28 us
    unnamed x50, local copies, waits for them, and re-layouts  12.4 us
    another operation x2, local copies, waits for them, and re-layouts  11.1 us
    dot_general x2, matrix products, expert_chunk(): jnp.einsum('nesh,nesd->ehd', hidden, expert_scaled, preferred_element_typ...  7.68 us
    dot_general x2, matrix products, expert_chunk(): jnp.einsum('nesd,nesh->edh', expert_rows, grad_preact, preferred_element_...  7.2 us
    concatenate x2, other arithmetic, expert_chunk(): jnp.concatenate([out_part.astype(jnp.bfloat16), grad_part.astype(jnp.bflo...  7.08 us
  transfers between devices with their start and end apart: 4, of which 4 were waited for; matrix products, arithmetic and copies ran while one was open for 18% of the time, Pallas kernels for 23%

profile of v8, /device:TPU:7, one launch (start us, length us, event | category | flops | bytes accessed | tf_op | source)
XLA Modules:
  0.0 312.3 jit_solution(14809202109987345253)
XLA Ops:
  10.0 1.9 gather_fusion
  17.3 38.8 %slot_chunk1.2 = bf16[64,8,1024]{2,1,0:T(8,128)(2,1)} custom-call(bf16[64,8,1024]{2,1,0:T(8,128)(2,1)} %maximum_bitcast_fusion.1.x_ref), custom_call_target="tpu_custom_call" | custom-call | bytes 2097152 | tf_op jit(solution)/shard_map/slot_chunk1/pallas_call | solution.py:63
  56.2 2.7 maximum_bitcast_fusion.x_ref
  58.9 34.5 %slot_chunk0.2 = bf16[64,8,1024]{2,1,0:T(8,128)(2,1)} custom-call(bf16[64,8,1024]{2,1,0:T(8,128)(2,1)} %maximum_bitcast_fusion.x_ref), custom_call_target="tpu_custom_call" | custom-call | bytes 2097152 | tf_op jit(solution)/shard_map/slot_chunk0/pallas_call | solution.py:63
  93.9 11.9 %all-gather.7.cloned.1.call-done = bf16[64,8,4096]{2,1,0:T(8,128)(2,1)} async-done(((bf16[64,8,1024]{2,1,0:T(8,128)(2,1)}), bf16[64,8,4096]{2,1,0:T(8,128)(2,1)}) %all-gather.7.cloned.1.call-update) | async-done | bytes 4194320 | tf_op jit(solution)/shard_map/slot_chunk1/all_gather | solution.py:84
  105.9 5.6 %slice_bitcast_fusion.1 = (bf16[64,4,4096]{2,1,0:T(4,128)(2,1)S(1)}, bf16[64,4,4096]{2,1,0:T(4,128)(2,1)S(1)}) fusion(bf16[64,1,8,4096]{3,2,0,1:T(8,128)(2,1)} %bitcast.196), kind=kLoop, calls=%fused_computation.30 | loop fusion | bytes 8388608 | tf_op jit(solution)/shard_map/reshape.28
  111.5 1.8 fusion.33
  115.0 1.8 fusion.78
  122.6 3.4 %pad_maximum_fusion.1 = bf16[64,1,8,4096]{3,2,0,1:T(8,128)(2,1)} fusion(bf16[64,1,4,4096]{3,2,0,1:T(4,128)(2,1)S(1)} %bitcast.191, bf16[64,1,4,4096]{3,2,0,1:T(4,128)(2,1)S(1)} %bitcast.193), kind=kLoop, calls=%fused_computation.12 | loop fusion | flops 8388608 | bytes 8388608 | tf_op jit(solution)/shard_map/slot_chunk1/concatenate | solution.py:104
  126.3 32.6 %all-gather.5.cloned.1.call-done = bf16[64,8,4096]{2,1,0:T(8,128)(2,1)} async-done(((bf16[64,8,1024]{2,1,0:T(8,128)(2,1)}), bf16[64,8,4096]{2,1,0:T(8,128)(2,1)}) %all-gather.5.cloned.1.call-update) | async-done | bytes 4194320 | tf_op jit(solution)/shard_map/slot_chunk0/all_gather | solution.py:84
  158.9 5.5 %slice_bitcast_fusion.3 = (bf16[64,4,4096]{2,1,0:T(4,128)(2,1)S(1)}, bf16[64,4,4096]{2,1,0:T(4,128)(2,1)S(1)}) fusion(bf16[64,1,8,4096]{3,2,0,1:T(8,128)(2,1)} %bitcast.195), kind=kLoop, calls=%fused_computation.32 | loop fusion | bytes 8388608 | tf_op jit(solution)/shard_map/reshape.4
  164.5 1.8 fusion.28
  168.0 1.8 fusion.83
  175.6 3.6 %pad_maximum_fusion = bf16[64,1,8,4096]{3,2,0,1:T(8,128)(2,1)} fusion(bf16[64,1,4,4096]{3,2,0,1:T(4,128)(2,1)S(1)} %bitcast.192, bf16[64,1,4,4096]{3,2,0,1:T(4,128)(2,1)S(1)} %bitcast.194), kind=kLoop, calls=%fused_computation.11 | loop fusion | flops 8388608 | bytes 8388608 | tf_op jit(solution)/shard_map/slot_chunk0/concatenate | solution.py:104
  180.2 3.5 %fusion.23 = f32[4096,384,1]{1,0,2:T(8,128)S(1)} fusion(bf16[64,4,384]{2,0,1:T(8,128)(2,1)S(1)} %copy-done.12, bf16[64,4,4096]{2,1,0:T(4,128)(2,1)} %copy-done.8), kind=kOutput, calls=%fused_computation.40 | convolution fusion | flops 805306368 | bytes 8585216 | tf_op jit(solution)/shard_map/slot_chunk0/nesd,nesh->edh/dot_general | solution.py:100
  183.8 2.9 fusion.20
  186.7 3.7 %fusion.2 = bf16[1,4096,384]{2,1,0:T(8,128)(2,1)} fusion(bf16[64,4,384]{2,0,1:T(8,128)(2,1)S(1)} %fusion.78, f32[4096,384,1]{1,0,2:T(8,128)S(1)} %fusion.23, bf16[64,4,4096]{2,1,0:T(4,128)(2,1)S(1)} %copy-done.5), kind=kOutput, calls=%fused_computation.9 | convolution fusion | flops 808452096 | bytes 11730944 | tf_op jit(solution)/shard_map/slot_chunk1/nesd,nesh->edh/dot_general | solution.py:100
  190.4 4.8 %fusion.3 = bf16[1,384,4096]{2,1,0:T(8,128)(2,1)} fusion(f32[384,4096,1]{1,0,2:T(8,128)S(1)} %fusion.20, bf16[64,4,4096]{2,1,0:T(4,128)(2,1)S(1)} %copy-done.3, f32[64,1,4,384]{3,0,2,1:T(8,128)S(1)} %copy-done.19), kind=kOutput, calls=%fused_computation.10 | convolution fusion | flops 808943616 | bytes 11927552 | tf_op jit(solution)/shard_map/slot_chunk1/nesh,nesd->ehd/dot_general | solution.py:97
  195.2 16.1 %reduce-scatter.5.cloned.1.call-done = bf16[64,1,8,1024]{3,2,0,1:T(8,128)(2,1)} async-done(((bf16[64,1,8,4096]{3,2,0,1:T(8,128)(2,1)}), bf16[64,1,8,1024]{3,2,0,1:T(8,128)(2,1)}) %reduce-scatter.5.cloned.1.call-update) | async-done | bytes 1048592 | tf_op jit(solution)/shard_map/slot_chunk1/reduce_scatter | solution.py:107
  211.3 36.8 %slot_chunk1.3 = bf16[64,8,1024]{2,1,0:T(8,128)(2,1)} custom-call(bf16[64,8,1024]{2,1,0:T(8,128)(2,1)} %bitcast.199), custom_call_target="tpu_custom_call" | custom-call | bytes 2097152 | tf_op jit(solution)/shard_map/slot_chunk1/pallas_call | solution.py:63
  248.1 3.0 fusion.100
  251.2 11.9 %reduce-scatter.3.cloned.1.call-done = bf16[64,1,8,1024]{3,2,0,1:T(8,128)(2,1)} async-done(((bf16[64,1,8,4096]{3,2,0,1:T(8,128)(2,1)}), bf16[64,1,8,1024]{3,2,0,1:T(8,128)(2,1)}) %reduce-scatter.3.cloned.1.call-update) | async-done | bytes 1048592 | tf_op jit(solution)/shard_map/slot_chunk0/reduce_scatter | solution.py:107
  263.0 37.1 %slot_chunk0.3 = bf16[64,8,1024]{2,1,0:T(8,128)(2,1)} custom-call(bf16[64,8,1024]{2,1,0:T(8,128)(2,1)} %bitcast.200), custom_call_target="tpu_custom_call" | custom-call | bytes 2097152 | tf_op jit(solution)/shard_map/slot_chunk0/pallas_call | solution.py:63
  300.1 2.1 fusion.99
  (79 shorter events, 28.1 us)
Async XLA Ops:
  7.2 104.3 %copy-start = (bf16[1,4096,384]{2,1,0:T(8,128)(2,1)S(1)}, bf16[1,4096,384]{2,1,0:T(8,128)(2,1)}, u32[]{:S(2)}) copy-start(bf16[1,4096,384]{2,1,0:T(8,128)(2,1)} %param.10) | copy-start | bytes 9437188
  7.2 98.7 %all-gather.7.cloned.1.call-start = ((), (), s32[]{:S(2)}) async-start(), calls=%async_computation.5 | async-start | bytes 5242880 | tf_op jit(solution)/shard_map/slot_chunk1/all_gather | solution.py:84
  10.0 2.1 copy-start.15
  10.0 2.6 copy-start.13
  10.0 3.1 copy-start.14
  56.1 102.8 %all-gather.5.cloned.1.call-start = ((), (), s32[]{:S(2)}) async-start(), calls=%async_computation.4 | async-start | bytes 5242880 | tf_op jit(solution)/shard_map/slot_chunk0/all_gather | solution.py:84
  93.4 117.9 %reduce-scatter.5.cloned.1.call-start = ((), (), s32[]{:S(2)}) async-start(), calls=%async_computation.3 | async-start | bytes 5242880 | tf_op jit(solution)/shard_map/slot_chunk1/reduce_scatter | solution.py:107
  111.4 1.9 copy-start.4
  111.4 2.1 copy-start.2
  111.5 3.5 %copy-start.16 = (bf16[1,384,4096]{2,1,0:T(8,128)(2,1)S(1)}, bf16[1,384,4096]{2,1,0:T(8,128)(2,1)}, u32[]{:S(2)}) copy-start(bf16[1,384,4096]{2,1,0:T(8,128)(2,1)} %param.11) | copy-start | bytes 9437188
  113.3 6.4 %copy-start.18 = (f32[64,1,4,384]{3,0,2,1:T(8,128)}, f32[64,1,4,384]{3,0,2,1:T(8,128)S(1)}, u32[]{:S(2)}) copy-start(f32[64,1,4,384]{3,0,2,1:T(8,128)S(1)} %fusion.33) | copy-start | bytes 1179652
  126.1 136.9 %reduce-scatter.3.cloned.1.call-start = ((), (), s32[]{:S(2)}) async-start(), calls=%async_computation.2 | async-start | bytes 5242880 | tf_op jit(solution)/shard_map/slot_chunk0/reduce_scatter | solution.py:107
  164.4 1.9 copy-start.8
  164.4 2.1 copy-start.6
  164.4 3.5 %copy-start.17 = (bf16[1,384,4096]{2,1,0:T(8,128)(2,1)S(1)}, bf16[1,384,4096]{2,1,0:T(8,128)(2,1)}, u32[]{:S(2)}) copy-start(bf16[1,384,4096]{2,1,0:T(8,128)(2,1)} %param.11) | copy-start | bytes 9437188
  166.3 6.4 %copy-start.20 = (f32[64,1,4,384]{3,0,2,1:T(8,128)}, f32[64,1,4,384]{3,0,2,1:T(8,128)S(1)}, u32[]{:S(2)}) copy-start(f32[64,1,4,384]{3,0,2,1:T(8,128)S(1)} %fusion.28) | copy-start | bytes 1179652
  180.2 3.5 %copy-start.7 = (bf16[64,4,4096]{2,1,0:T(4,128)(2,1)S(1)}, bf16[64,4,4096]{2,1,0:T(4,128)(2,1)}, u32[]{:S(2)}) copy-start(bf16[64,4,4096]{2,1,0:T(4,128)(2,1)} %copy-done.6) | copy-start | bytes 6291460
  180.2 3.5 %copy-start.21 = (f32[64,1,4,384]{3,0,2,1:T(8,128)S(1)}, f32[64,1,4,384]{3,0,2,1:T(8,128)}, u32[]{:S(2)}) copy-start(f32[64,1,4,384]{3,0,2,1:T(8,128)} %copy-done.20) | copy-start | bytes 1179652
  183.8 2.9 copy-start.5
  186.7 3.7 %copy-start.3 = (bf16[64,4,4096]{2,1,0:T(4,128)(2,1)S(1)}, bf16[64,4,4096]{2,1,0:T(4,128)(2,1)}, u32[]{:S(2)}) copy-start(bf16[64,4,4096]{2,1,0:T(4,128)(2,1)} %copy-done.2) | copy-start | bytes 6291460
  186.7 3.7 %copy-start.19 = (f32[64,1,4,384]{3,0,2,1:T(8,128)S(1)}, f32[64,1,4,384]{3,0,2,1:T(8,128)}, u32[]{:S(2)}) copy-start(f32[64,1,4,384]{3,0,2,1:T(8,128)} %copy-done.18) | copy-start | bytes 1179652
  300.1 2.2 copy-start.10
  300.1 3.8 %copy-start.9 = (bf16[64,1,4,1024]{3,2,0,1:T(4,128)(2,1)S(1)}, bf16[64,1,4,1024]{3,2,0,1:T(4,128)(2,1)}, u32[]{:S(2)}) copy-start(bf16[64,1,4,1024]{3,2,0,1:T(4,128)(2,1)} %get-tuple-element.12) | copy-start | bytes 1572868
  300.1 5.4 %copy-start.1 = (bf16[1,4096,384]{2,1,0:T(8,128)(2,1)S(1)}, bf16[1,4096,384]{2,1,0:T(8,128)(2,1)}, u32[]{:S(2)}) copy-start(bf16[1,4096,384]{2,1,0:T(8,128)(2,1)} %param.10) | copy-start | bytes 9437188
  (2 other events, 2.2 us)
Sparse Core Ops, SparseCore 0:
  56.2 49.5 all-gather.6
  107.7 51.1 all-gather.4
  161.4 49.8 reduce-scatter.4
  213.9 49.1 reduce-scatter.2

commit v9 on v3

--- a/solution.py
+++ b/solution.py
@@ -122,7 +122,7 @@
     )
     per_token = jnp.sum(matches, axis=1)
     earlier = jnp.cumsum(per_token, axis=0) - per_token
-    destination = routing * capacity + jnp.take_along_axis(earlier, routing, axis=1)
+    destination = routing * capacity + jnp.sum(matches * earlier[:, None, :], axis=2)
     placed = (
         destination[:, :, None] == jnp.arange(buffer_rows, dtype=jnp.int32)[None, None, :]
     ).astype(jnp.float32)
@@ -152,12 +152,19 @@
         back_grad.append(b_grad)
         d_w_in = g_in if d_w_in is None else d_w_in + g_in
         d_w_out = g_out if d_w_out is None else d_w_out + g_out
-    back_out = jnp.concatenate(back_out, axis=2).reshape(buffer_rows, quarter).astype(jnp.float32)
-    back_grad = jnp.concatenate(back_grad, axis=2).reshape(buffer_rows, quarter).astype(jnp.float32)
-    mixed = jnp.einsum("tr,rd->td", weighting, back_out, precision=highest).astype(jnp.bfloat16)
-    d_tokens = jnp.einsum("tr,rd->td", membership, back_grad, precision=highest).astype(
-        jnp.bfloat16
-    )
+    back_out = jnp.concatenate(back_out, axis=2).reshape(buffer_rows, quarter)
+    back_grad = jnp.concatenate(back_grad, axis=2).reshape(buffer_rows, quarter)
+    gate_hi = weighting.astype(jnp.bfloat16)
+    rest = weighting - gate_hi.astype(jnp.float32)
+    gate_mid = rest.astype(jnp.bfloat16)
+    gate_lo = (rest - gate_mid.astype(jnp.float32)).astype(jnp.bfloat16)
+    mixed = sum(
+        jnp.einsum("tr,rd->td", part, back_out, preferred_element_type=jnp.float32)
+        for part in (gate_lo, gate_mid, gate_hi)
+    ).astype(jnp.bfloat16)
+    d_tokens = jnp.einsum(
+        "tr,rd->td", membership.astype(jnp.bfloat16), back_grad, preferred_element_type=jnp.float32
+    ).astype(jnp.bfloat16)
     return (mixed, d_tokens, d_w_in.astype(jnp.bfloat16), d_w_out.astype(jnp.bfloat16))
 
 

time: 313 us -> 314 us (level)
    unnamed x50 -> x46, local copies, waits for them, and re-layouts: 12.4 us -> 13.2 us
  transfers between devices with their start and end apart: 4 -> 4, of which waited for: 4 -> 4; matrix products, arithmetic and copies ran while one was open for 19% -> 18% of each run, Pallas kernels for 22% -> 22%
where the time goes in v9:
time: 314 us; the launch traced here: 309 us
  Pallas kernels  139 us (44%)
  waiting for transfers between devices  77.5 us (25%)
  matrix products  32.5 us (10%)
  local copies, waits for them, and re-layouts  31.2 us (10%)
  between operations  14.4 us (5%)
  other arithmetic  13.2 us (4%)
    pallas_call x4, Pallas kernels, expert_all_to_all(): pl.pallas_call(_a2a_kernel, out_shape=jax.ShapeDtypeStruct(x.shape, x.dty...  139 us
    all_gather x2, waiting for transfers between devices, expert_chunk(): whole = lax.all_gather(arrived, 'tensor', axis=3, tiled=True)  46.5 us
    reduce_scatter x2, waiting for transfers between devices, expert_chunk(): sums = lax.psum_scatter(parts, 'tensor', scatter_dimension=3, tiled=True)  30.9 us
    unnamed x46, local copies, waits for them, and re-layouts  13.2 us
    another operation x2, local copies, waits for them, and re-layouts  11 us
    dot_general x2, matrix products, expert_chunk(): jnp.einsum('nesh,nesd->ehd', hidden, expert_scaled, preferred_element_typ...  7.68 us
    concatenate x2, other arithmetic, expert_chunk(): jnp.concatenate([out_part.astype(jnp.bfloat16), grad_part.astype(jnp.bflo...  7.09 us
  transfers between devices with their start and end apart: 4, of which 4 were waited for; matrix products, arithmetic and copies ran while one was open for 18% of the time, Pallas kernels for 22%

profile of v9, /device:TPU:7, one launch (start us, length us, event | category | flops | bytes accessed | tf_op | source)
XLA Modules:
  0.0 309.1 jit_solution(726859301297536557)
XLA Ops:
  12.3 1.9 fusion.27
  17.3 36.8 %slot_chunk1.2 = bf16[64,8,1024]{2,1,0:T(8,128)(2,1)} custom-call(bf16[64,8,1024]{2,1,0:T(8,128)(2,1)} %maximum_bitcast_fusion.1.x_ref), custom_call_target="tpu_custom_call" | custom-call | bytes 2097152 | tf_op jit(solution)/shard_map/slot_chunk1/pallas_call | solution.py:63
  54.2 2.7 maximum_bitcast_fusion.x_ref
  56.9 32.6 %slot_chunk0.2 = bf16[64,8,1024]{2,1,0:T(8,128)(2,1)} custom-call(bf16[64,8,1024]{2,1,0:T(8,128)(2,1)} %maximum_bitcast_fusion.x_ref), custom_call_target="tpu_custom_call" | custom-call | bytes 2097152 | tf_op jit(solution)/shard_map/slot_chunk0/pallas_call | solution.py:63
  90.1 13.9 %all-gather.7.cloned.1.call-done = bf16[64,8,4096]{2,1,0:T(8,128)(2,1)} async-done(((bf16[64,8,1024]{2,1,0:T(8,128)(2,1)}), bf16[64,8,4096]{2,1,0:T(8,128)(2,1)}) %all-gather.7.cloned.1.call-update) | async-done | bytes 4194320 | tf_op jit(solution)/shard_map/slot_chunk1/all_gather | solution.py:84
  104.0 5.5 %slice_bitcast_fusion.1 = (bf16[64,4,4096]{2,1,0:T(4,128)(2,1)S(1)}, bf16[64,4,4096]{2,1,0:T(4,128)(2,1)S(1)}) fusion(bf16[64,1,8,4096]{3,2,0,1:T(8,128)(2,1)} %bitcast.194), kind=kLoop, calls=%fused_computation.29 | loop fusion | bytes 8388608 | tf_op jit(solution)/shard_map/reshape.25
  109.5 1.8 fusion.33
  113.0 1.8 fusion.78
  120.7 3.5 %pad_maximum_fusion.1 = bf16[64,1,8,4096]{3,2,0,1:T(8,128)(2,1)} fusion(bf16[64,1,4,4096]{3,2,0,1:T(4,128)(2,1)S(1)} %bitcast.189, bf16[64,1,4,4096]{3,2,0,1:T(4,128)(2,1)S(1)} %bitcast.191), kind=kLoop, calls=%fused_computation.11 | loop fusion | flops 8388608 | bytes 8388608 | tf_op jit(solution)/shard_map/slot_chunk1/concatenate | solution.py:104
  124.4 32.6 %all-gather.5.cloned.1.call-done = bf16[64,8,4096]{2,1,0:T(8,128)(2,1)} async-done(((bf16[64,8,1024]{2,1,0:T(8,128)(2,1)}), bf16[64,8,4096]{2,1,0:T(8,128)(2,1)}) %all-gather.5.cloned.1.call-update) | async-done | bytes 4194320 | tf_op jit(solution)/shard_map/slot_chunk0/all_gather | solution.py:84
  157.0 5.5 %slice_bitcast_fusion.3 = (bf16[64,4,4096]{2,1,0:T(4,128)(2,1)S(1)}, bf16[64,4,4096]{2,1,0:T(4,128)(2,1)S(1)}) fusion(bf16[64,1,8,4096]{3,2,0,1:T(8,128)(2,1)} %bitcast.193), kind=kLoop, calls=%fused_computation.31 | loop fusion | bytes 8388608 | tf_op jit(solution)/shard_map/reshape.1
  162.5 1.8 fusion.28
  166.0 1.8 fusion.83
  173.7 3.6 %pad_maximum_fusion = bf16[64,1,8,4096]{3,2,0,1:T(8,128)(2,1)} fusion(bf16[64,1,4,4096]{3,2,0,1:T(4,128)(2,1)S(1)} %bitcast.190, bf16[64,1,4,4096]{3,2,0,1:T(4,128)(2,1)S(1)} %bitcast.192), kind=kLoop, calls=%fused_computation.10 | loop fusion | flops 8388608 | bytes 8388608 | tf_op jit(solution)/shard_map/slot_chunk0/concatenate | solution.py:104
  179.0 1.8 fusion.23
  180.8 2.9 fusion.20
  183.7 3.7 %fusion.2 = bf16[1,4096,384]{2,1,0:T(8,128)(2,1)} fusion(bf16[64,4,384]{2,0,1:T(8,128)(2,1)S(1)} %fusion.78, f32[4096,384,1]{1,0,2:T(8,128)S(1)} %fusion.23, bf16[64,4,4096]{2,1,0:T(4,128)(2,1)S(1)} %copy-done.5), kind=kOutput, calls=%fused_computation.8 | convolution fusion | flops 808452096 | bytes 11730944 | tf_op jit(solution)/shard_map/slot_chunk1/nesd,nesh->edh/dot_general | solution.py:100
  187.4 4.8 %fusion.3 = bf16[1,384,4096]{2,1,0:T(8,128)(2,1)} fusion(f32[384,4096,1]{1,0,2:T(8,128)S(1)} %fusion.20, bf16[64,4,4096]{2,1,0:T(4,128)(2,1)S(1)} %copy-done.3, f32[64,1,4,384]{3,0,2,1:T(8,128)S(1)} %copy-done.17), kind=kOutput, calls=%fused_computation.9 | convolution fusion | flops 808943616 | bytes 11927552 | tf_op jit(solution)/shard_map/slot_chunk1/nesh,nesd->ehd/dot_general | solution.py:97
  192.2 17.2 %reduce-scatter.5.cloned.1.call-done = bf16[64,1,8,1024]{3,2,0,1:T(8,128)(2,1)} async-done(((bf16[64,1,8,4096]{3,2,0,1:T(8,128)(2,1)}), bf16[64,1,8,1024]{3,2,0,1:T(8,128)(2,1)}) %reduce-scatter.5.cloned.1.call-update) | async-done | bytes 1048592 | tf_op jit(solution)/shard_map/slot_chunk1/reduce_scatter | solution.py:107
  209.4 34.9 %slot_chunk1.3 = bf16[64,8,1024]{2,1,0:T(8,128)(2,1)} custom-call(bf16[64,8,1024]{2,1,0:T(8,128)(2,1)} %bitcast.197), custom_call_target="tpu_custom_call" | custom-call | bytes 2097152 | tf_op jit(solution)/shard_map/slot_chunk1/pallas_call | solution.py:63
  244.3 3.1 %fusion.106 = (bf16[64,1,4,1024]{3,2,0,1:T(4,128)(2,1)}, bf16[64,1,4,1024]{3,2,0,1:T(4,128)(2,1)}) fusion(bf16[64,1,8,1024]{3,2,0,1:T(8,128)(2,1)} %bitcast.195), kind=kLoop, calls=%fused_computation.95 | loop fusion | bytes 2097152 | tf_op jit(solution)/shard_map/slot_chunk1/slice | solution.py:109
  247.4 13.7 %reduce-scatter.3.cloned.1.call-done = bf16[64,1,8,1024]{3,2,0,1:T(8,128)(2,1)} async-done(((bf16[64,1,8,4096]{3,2,0,1:T(8,128)(2,1)}), bf16[64,1,8,1024]{3,2,0,1:T(8,128)(2,1)}) %reduce-scatter.3.cloned.1.call-update) | async-done | bytes 1048592 | tf_op jit(solution)/shard_map/slot_chunk0/reduce_scatter | solution.py:107
  261.1 35.1 %slot_chunk0.3 = bf16[64,8,1024]{2,1,0:T(8,128)(2,1)} custom-call(bf16[64,8,1024]{2,1,0:T(8,128)(2,1)} %bitcast.198), custom_call_target="tpu_custom_call" | custom-call | bytes 2097152 | tf_op jit(solution)/shard_map/slot_chunk0/pallas_call | solution.py:63
  296.3 2.1 fusion.105
  (73 shorter events, 29.7 us)
Async XLA Ops:
  7.2 102.3 %copy-start = (bf16[1,4096,384]{2,1,0:T(8,128)(2,1)S(1)}, bf16[1,4096,384]{2,1,0:T(8,128)(2,1)}, u32[]{:S(2)}) copy-start(bf16[1,4096,384]{2,1,0:T(8,128)(2,1)} %param.10) | copy-start | bytes 9437188
  7.2 96.8 %all-gather.7.cloned.1.call-start = ((), (), s32[]{:S(2)}) async-start(), calls=%async_computation.5 | async-start | bytes 5242880 | tf_op jit(solution)/shard_map/slot_chunk1/all_gather | solution.py:84
  54.1 102.8 %all-gather.5.cloned.1.call-start = ((), (), s32[]{:S(2)}) async-start(), calls=%async_computation.4 | async-start | bytes 5242880 | tf_op jit(solution)/shard_map/slot_chunk0/all_gather | solution.py:84
  89.5 119.9 %reduce-scatter.5.cloned.1.call-start = ((), (), s32[]{:S(2)}) async-start(), calls=%async_computation.3 | async-start | bytes 5242880 | tf_op jit(solution)/shard_map/slot_chunk1/reduce_scatter | solution.py:107
  109.5 1.9 copy-start.4
  109.5 2.1 copy-start.2
  109.5 3.5 %copy-start.14 = (bf16[1,384,4096]{2,1,0:T(8,128)(2,1)S(1)}, bf16[1,384,4096]{2,1,0:T(8,128)(2,1)}, u32[]{:S(2)}) copy-start(bf16[1,384,4096]{2,1,0:T(8,128)(2,1)} %param.11) | copy-start | bytes 9437188
  111.3 6.4 %copy-start.16 = (f32[64,1,4,384]{3,0,2,1:T(8,128)}, f32[64,1,4,384]{3,0,2,1:T(8,128)S(1)}, u32[]{:S(2)}) copy-start(f32[64,1,4,384]{3,0,2,1:T(8,128)S(1)} %fusion.33) | copy-start | bytes 1179652
  124.2 137.0 %reduce-scatter.3.cloned.1.call-start = ((), (), s32[]{:S(2)}) async-start(), calls=%async_computation.2 | async-start | bytes 5242880 | tf_op jit(solution)/shard_map/slot_chunk0/reduce_scatter | solution.py:107
  162.5 1.9 copy-start.8
  162.5 2.1 copy-start.6
  162.5 3.5 %copy-start.15 = (bf16[1,384,4096]{2,1,0:T(8,128)(2,1)S(1)}, bf16[1,384,4096]{2,1,0:T(8,128)(2,1)}, u32[]{:S(2)}) copy-start(bf16[1,384,4096]{2,1,0:T(8,128)(2,1)} %param.11) | copy-start | bytes 9437188
  164.3 6.4 %copy-start.18 = (f32[64,1,4,384]{3,0,2,1:T(8,128)}, f32[64,1,4,384]{3,0,2,1:T(8,128)S(1)}, u32[]{:S(2)}) copy-start(f32[64,1,4,384]{3,0,2,1:T(8,128)S(1)} %fusion.28) | copy-start | bytes 1179652
  167.8 1.3 copy-start.12
  177.3 1.6 copy-start.9
  177.3 1.6 copy-start.13
  179.0 1.8 copy-start.7
  179.0 1.8 copy-start.19
  180.8 2.9 copy-start.5
  183.7 3.7 %copy-start.3 = (bf16[64,4,4096]{2,1,0:T(4,128)(2,1)S(1)}, bf16[64,4,4096]{2,1,0:T(4,128)(2,1)}, u32[]{:S(2)}) copy-start(bf16[64,4,4096]{2,1,0:T(4,128)(2,1)} %copy-done.2) | copy-start | bytes 6291460
  183.7 3.7 %copy-start.17 = (f32[64,1,4,384]{3,0,2,1:T(8,128)S(1)}, f32[64,1,4,384]{3,0,2,1:T(8,128)}, u32[]{:S(2)}) copy-start(f32[64,1,4,384]{3,0,2,1:T(8,128)} %copy-done.16) | copy-start | bytes 1179652
  296.3 2.1 copy-start.11
  298.4 2.6 copy-start.10
  298.4 3.9 %copy-start.1 = (bf16[1,4096,384]{2,1,0:T(8,128)(2,1)S(1)}, bf16[1,4096,384]{2,1,0:T(8,128)(2,1)}, u32[]{:S(2)}) copy-start(bf16[1,4096,384]{2,1,0:T(8,128)(2,1)} %param.10) | copy-start | bytes 9437188
Sparse Core Ops, SparseCore 0:
  54.3 49.6 all-gather.6
  105.8 51.1 all-gather.4
  159.5 49.8 reduce-scatter.4
  212.0 49.1 reduce-scatter.2

commit v10 on v3

--- a/solution.py
+++ b/solution.py
@@ -27,7 +27,9 @@
     local = pltpu.make_async_copy(x_ref.at[me], o_ref.at[me], local_sem)
     local.start()
 
-    def push(k, carry):
+    def push(i, carry):
+        half = i // 2 + 1
+        k = half + (i % 2) * (n - 2 * half)
         peer = lax.rem(me + k, n)
         pltpu.make_async_remote_copy(
             src_ref=x_ref.at[peer],
@@ -39,7 +41,7 @@
         ).start()
         return carry
 
-    lax.fori_loop(1, n, push, 0)
+    lax.fori_loop(0, n - 1, push, 0)
 
     def settle(k, carry):
         peer = lax.rem(me + k, n)

time: 313 us -> 310 us (level)
  Pallas kernels: 139 us -> 132 us
    pallas_call x4, Pallas kernels: 139 us -> 132 us  [expert_all_to_all(): pl.pallas_call(_a2a_kernel, out_shape=jax.ShapeDtypeStruct(x.shape, x.dty...]
    reduce_scatter x2, waiting for transfers between devices: 29.9 us -> 33.1 us  [expert_chunk(): sums = lax.psum_scatter(parts, 'tensor', scatter_dimension=3, tiled=True)]
where the time goes in v10:
time: 310 us; the launch traced here: 304 us
  Pallas kernels  132 us (43%)
  waiting for transfers between devices  79.5 us (26%)
  local copies, waits for them, and re-layouts  32.7 us (11%)
  matrix products  31.9 us (10%)
  between operations  14.7 us (5%)
  other arithmetic  12.7 us (4%)
    pallas_call x4, Pallas kernels, expert_all_to_all(): pl.pallas_call(_a2a_kernel, out_shape=jax.ShapeDtypeStruct(x.shape, x.dty...  132 us
    all_gather x2, waiting for transfers between devices, expert_chunk(): whole = lax.all_gather(arrived, 'tensor', axis=3, tiled=True)  46.3 us
    reduce_scatter x2, waiting for transfers between devices, expert_chunk(): sums = lax.psum_scatter(parts, 'tensor', scatter_dimension=3, tiled=True)  33.1 us
    unnamed x50, local copies, waits for them, and re-layouts  12.4 us
    another operation x2, local copies, waits for them, and re-layouts  11.1 us
    dot_general x2, matrix products, expert_chunk(): jnp.einsum('nesh,nesd->ehd', hidden, expert_scaled, preferred_element_typ...  7.68 us
    dot_general x2, matrix products, expert_chunk(): jnp.einsum('nesd,nesh->edh', expert_rows, grad_preact, preferred_element_...  7.21 us
    concatenate x2, other arithmetic, expert_chunk(): jnp.concatenate([out_part.astype(jnp.bfloat16), grad_part.astype(jnp.bflo...  7.12 us
  transfers between devices with their start and end apart: 4, of which 4 were waited for; matrix products, arithmetic and copies ran while one was open for 19% of the time, Pallas kernels for 22%

profile of v10, /device:TPU:7, one launch (start us, length us, event | category | flops | bytes accessed | tf_op | source)
XLA Modules:
  0.0 304.5 jit_solution(1174380816607487305)
XLA Ops:
  10.0 1.9 gather_fusion
  17.3 33.2 %slot_chunk1.2 = bf16[64,8,1024]{2,1,0:T(8,128)(2,1)} custom-call(bf16[64,8,1024]{2,1,0:T(8,128)(2,1)} %maximum_bitcast_fusion.1.x_ref), custom_call_target="tpu_custom_call" | custom-call | bytes 2097152 | tf_op jit(solution)/shard_map/slot_chunk1/pallas_call | solution.py:65
  50.6 2.7 maximum_bitcast_fusion.x_ref
  53.2 35.6 %slot_chunk0.2 = bf16[64,8,1024]{2,1,0:T(8,128)(2,1)} custom-call(bf16[64,8,1024]{2,1,0:T(8,128)(2,1)} %maximum_bitcast_fusion.x_ref), custom_call_target="tpu_custom_call" | custom-call | bytes 2097152 | tf_op jit(solution)/shard_map/slot_chunk0/pallas_call | solution.py:65
  89.1 13.8 %all-gather.7.cloned.1.call-done = bf16[64,8,4096]{2,1,0:T(8,128)(2,1)} async-done(((bf16[64,8,1024]{2,1,0:T(8,128)(2,1)}), bf16[64,8,4096]{2,1,0:T(8,128)(2,1)}) %all-gather.7.cloned.1.call-update) | async-done | bytes 4194320 | tf_op jit(solution)/shard_map/slot_chunk1/all_gather | solution.py:86
  102.9 5.6 %slice_bitcast_fusion.1 = (bf16[64,4,4096]{2,1,0:T(4,128)(2,1)S(1)}, bf16[64,4,4096]{2,1,0:T(4,128)(2,1)S(1)}) fusion(bf16[64,1,8,4096]{3,2,0,1:T(8,128)(2,1)} %bitcast.196), kind=kLoop, calls=%fused_computation.30 | loop fusion | bytes 8388608 | tf_op jit(solution)/shard_map/reshape.28
  108.5 1.8 fusion.33
  112.0 1.8 fusion.78
  119.7 3.4 %pad_maximum_fusion.1 = bf16[64,1,8,4096]{3,2,0,1:T(8,128)(2,1)} fusion(bf16[64,1,4,4096]{3,2,0,1:T(4,128)(2,1)S(1)} %bitcast.191, bf16[64,1,4,4096]{3,2,0,1:T(4,128)(2,1)S(1)} %bitcast.193), kind=kLoop, calls=%fused_computation.12 | loop fusion | flops 8388608 | bytes 8388608 | tf_op jit(solution)/shard_map/slot_chunk1/concatenate | solution.py:106
  123.4 32.5 %all-gather.5.cloned.1.call-done = bf16[64,8,4096]{2,1,0:T(8,128)(2,1)} async-done(((bf16[64,8,1024]{2,1,0:T(8,128)(2,1)}), bf16[64,8,4096]{2,1,0:T(8,128)(2,1)}) %all-gather.5.cloned.1.call-update) | async-done | bytes 4194320 | tf_op jit(solution)/shard_map/slot_chunk0/all_gather | solution.py:86
  155.9 5.5 %slice_bitcast_fusion.3 = (bf16[64,4,4096]{2,1,0:T(4,128)(2,1)S(1)}, bf16[64,4,4096]{2,1,0:T(4,128)(2,1)S(1)}) fusion(bf16[64,1,8,4096]{3,2,0,1:T(8,128)(2,1)} %bitcast.195), kind=kLoop, calls=%fused_computation.32 | loop fusion | bytes 8388608 | tf_op jit(solution)/shard_map/reshape.4
  161.5 1.8 fusion.28
  165.0 1.8 fusion.83
  172.7 3.7 %pad_maximum_fusion = bf16[64,1,8,4096]{3,2,0,1:T(8,128)(2,1)} fusion(bf16[64,1,4,4096]{3,2,0,1:T(4,128)(2,1)S(1)} %bitcast.192, bf16[64,1,4,4096]{3,2,0,1:T(4,128)(2,1)S(1)} %bitcast.194), kind=kLoop, calls=%fused_computation.11 | loop fusion | flops 8388608 | bytes 8388608 | tf_op jit(solution)/shard_map/slot_chunk0/concatenate | solution.py:106
  177.3 3.5 %fusion.23 = f32[4096,384,1]{1,0,2:T(8,128)S(1)} fusion(bf16[64,4,384]{2,0,1:T(8,128)(2,1)S(1)} %copy-done.12, bf16[64,4,4096]{2,1,0:T(4,128)(2,1)} %copy-done.8), kind=kOutput, calls=%fused_computation.40 | convolution fusion | flops 805306368 | bytes 8585216 | tf_op jit(solution)/shard_map/slot_chunk0/nesd,nesh->edh/dot_general | solution.py:102
  180.8 2.9 fusion.20
  183.8 3.7 %fusion.2 = bf16[1,4096,384]{2,1,0:T(8,128)(2,1)} fusion(bf16[64,4,384]{2,0,1:T(8,128)(2,1)S(1)} %fusion.78, f32[4096,384,1]{1,0,2:T(8,128)S(1)} %fusion.23, bf16[64,4,4096]{2,1,0:T(4,128)(2,1)S(1)} %copy-done.5), kind=kOutput, calls=%fused_computation.9 | convolution fusion | flops 808452096 | bytes 11730944 | tf_op jit(solution)/shard_map/slot_chunk1/nesd,nesh->edh/dot_general | solution.py:102
  187.5 4.8 %fusion.3 = bf16[1,384,4096]{2,1,0:T(8,128)(2,1)} fusion(f32[384,4096,1]{1,0,2:T(8,128)S(1)} %fusion.20, bf16[64,4,4096]{2,1,0:T(4,128)(2,1)S(1)} %copy-done.3, f32[64,1,4,384]{3,0,2,1:T(8,128)S(1)} %copy-done.19), kind=kOutput, calls=%fused_computation.10 | convolution fusion | flops 808943616 | bytes 11927552 | tf_op jit(solution)/shard_map/slot_chunk1/nesh,nesd->ehd/dot_general | solution.py:99
  192.3 16.1 %reduce-scatter.5.cloned.1.call-done = bf16[64,1,8,1024]{3,2,0,1:T(8,128)(2,1)} async-done(((bf16[64,1,8,4096]{3,2,0,1:T(8,128)(2,1)}), bf16[64,1,8,1024]{3,2,0,1:T(8,128)(2,1)}) %reduce-scatter.5.cloned.1.call-update) | async-done | bytes 1048592 | tf_op jit(solution)/shard_map/slot_chunk1/reduce_scatter | solution.py:109
  208.3 31.7 %slot_chunk1.3 = bf16[64,8,1024]{2,1,0:T(8,128)(2,1)} custom-call(bf16[64,8,1024]{2,1,0:T(8,128)(2,1)} %bitcast.199), custom_call_target="tpu_custom_call" | custom-call | bytes 2097152 | tf_op jit(solution)/shard_map/slot_chunk1/pallas_call | solution.py:65
  240.0 3.0 fusion.100
  243.0 17.0 %reduce-scatter.3.cloned.1.call-done = bf16[64,1,8,1024]{3,2,0,1:T(8,128)(2,1)} async-done(((bf16[64,1,8,4096]{3,2,0,1:T(8,128)(2,1)}), bf16[64,1,8,1024]{3,2,0,1:T(8,128)(2,1)}) %reduce-scatter.3.cloned.1.call-update) | async-done | bytes 1048592 | tf_op jit(solution)/shard_map/slot_chunk0/reduce_scatter | solution.py:109
  260.0 32.0 %slot_chunk0.3 = bf16[64,8,1024]{2,1,0:T(8,128)(2,1)} custom-call(bf16[64,8,1024]{2,1,0:T(8,128)(2,1)} %bitcast.200), custom_call_target="tpu_custom_call" | custom-call | bytes 2097152 | tf_op jit(solution)/shard_map/slot_chunk0/pallas_call | solution.py:65
  292.1 2.1 fusion.99
  (79 shorter events, 27.8 us)
Async XLA Ops:
  7.2 101.3 %copy-start = (bf16[1,4096,384]{2,1,0:T(8,128)(2,1)S(1)}, bf16[1,4096,384]{2,1,0:T(8,128)(2,1)}, u32[]{:S(2)}) copy-start(bf16[1,4096,384]{2,1,0:T(8,128)(2,1)} %param.10) | copy-start | bytes 9437188
  7.2 95.7 %all-gather.7.cloned.1.call-start = ((), (), s32[]{:S(2)}) async-start(), calls=%async_computation.5 | async-start | bytes 5242880 | tf_op jit(solution)/shard_map/slot_chunk1/all_gather | solution.py:86
  10.0 2.1 copy-start.15
  10.0 2.6 copy-start.13
  10.0 3.1 %copy-start.14 = (bf16[32,1024]{1,0:T(8,128)(2,1)S(1)}, bf16[32,1024]{1,0:T(8,128)(2,1)}, u32[]{:S(2)}) copy-start(bf16[32,1024]{1,0:T(8,128)(2,1)} %param.7) | copy-start | bytes 196612
  50.5 105.4 %all-gather.5.cloned.1.call-start = ((), (), s32[]{:S(2)}) async-start(), calls=%async_computation.4 | async-start | bytes 5242880 | tf_op jit(solution)/shard_map/slot_chunk0/all_gather | solution.py:86
  88.8 119.5 %reduce-scatter.5.cloned.1.call-start = ((), (), s32[]{:S(2)}) async-start(), calls=%async_computation.3 | async-start | bytes 5242880 | tf_op jit(solution)/shard_map/slot_chunk1/reduce_scatter | solution.py:109
  108.5 1.9 copy-start.4
  108.5 2.1 copy-start.2
  108.5 3.5 %copy-start.16 = (bf16[1,384,4096]{2,1,0:T(8,128)(2,1)S(1)}, bf16[1,384,4096]{2,1,0:T(8,128)(2,1)}, u32[]{:S(2)}) copy-start(bf16[1,384,4096]{2,1,0:T(8,128)(2,1)} %param.11) | copy-start | bytes 9437188
  110.3 6.4 %copy-start.18 = (f32[64,1,4,384]{3,0,2,1:T(8,128)}, f32[64,1,4,384]{3,0,2,1:T(8,128)S(1)}, u32[]{:S(2)}) copy-start(f32[64,1,4,384]{3,0,2,1:T(8,128)S(1)} %fusion.33) | copy-start | bytes 1179652
  123.1 136.9 %reduce-scatter.3.cloned.1.call-start = ((), (), s32[]{:S(2)}) async-start(), calls=%async_computation.2 | async-start | bytes 5242880 | tf_op jit(solution)/shard_map/slot_chunk0/reduce_scatter | solution.py:109
  161.4 1.9 copy-start.8
  161.5 2.1 copy-start.6
  161.5 3.5 %copy-start.17 = (bf16[1,384,4096]{2,1,0:T(8,128)(2,1)S(1)}, bf16[1,384,4096]{2,1,0:T(8,128)(2,1)}, u32[]{:S(2)}) copy-start(bf16[1,384,4096]{2,1,0:T(8,128)(2,1)} %param.11) | copy-start | bytes 9437188
  163.3 6.4 %copy-start.20 = (f32[64,1,4,384]{3,0,2,1:T(8,128)}, f32[64,1,4,384]{3,0,2,1:T(8,128)S(1)}, u32[]{:S(2)}) copy-start(f32[64,1,4,384]{3,0,2,1:T(8,128)S(1)} %fusion.28) | copy-start | bytes 1179652
  177.3 3.5 %copy-start.7 = (bf16[64,4,4096]{2,1,0:T(4,128)(2,1)S(1)}, bf16[64,4,4096]{2,1,0:T(4,128)(2,1)}, u32[]{:S(2)}) copy-start(bf16[64,4,4096]{2,1,0:T(4,128)(2,1)} %copy-done.6) | copy-start | bytes 6291460
  177.3 3.5 %copy-start.21 = (f32[64,1,4,384]{3,0,2,1:T(8,128)S(1)}, f32[64,1,4,384]{3,0,2,1:T(8,128)}, u32[]{:S(2)}) copy-start(f32[64,1,4,384]{3,0,2,1:T(8,128)} %copy-done.20) | copy-start | bytes 1179652
  180.8 2.9 copy-start.5
  183.7 3.7 %copy-start.3 = (bf16[64,4,4096]{2,1,0:T(4,128)(2,1)S(1)}, bf16[64,4,4096]{2,1,0:T(4,128)(2,1)}, u32[]{:S(2)}) copy-start(bf16[64,4,4096]{2,1,0:T(4,128)(2,1)} %copy-done.2) | copy-start | bytes 6291460
  183.7 3.7 %copy-start.19 = (f32[64,1,4,384]{3,0,2,1:T(8,128)S(1)}, f32[64,1,4,384]{3,0,2,1:T(8,128)}, u32[]{:S(2)}) copy-start(f32[64,1,4,384]{3,0,2,1:T(8,128)} %copy-done.18) | copy-start | bytes 1179652
  292.0 2.2 copy-start.10
  292.0 3.8 %copy-start.9 = (bf16[64,1,4,1024]{3,2,0,1:T(4,128)(2,1)S(1)}, bf16[64,1,4,1024]{3,2,0,1:T(4,128)(2,1)}, u32[]{:S(2)}) copy-start(bf16[64,1,4,1024]{3,2,0,1:T(4,128)(2,1)} %get-tuple-element.12) | copy-start | bytes 1572868
  292.1 5.4 %copy-start.1 = (bf16[1,4096,384]{2,1,0:T(8,128)(2,1)S(1)}, bf16[1,4096,384]{2,1,0:T(8,128)(2,1)}, u32[]{:S(2)}) copy-start(bf16[1,4096,384]{2,1,0:T(8,128)(2,1)} %param.10) | copy-start | bytes 9437188
  (2 other events, 2.2 us)
Sparse Core Ops, SparseCore 0:
  50.6 52.2 all-gather.6
  104.7 51.1 all-gather.4
  158.4 49.8 reduce-scatter.4
  210.9 49.1 reduce-scatter.2

commit v11 on v10

--- a/solution.py
+++ b/solution.py
@@ -131,15 +131,13 @@
     membership = jnp.sum(placed, axis=1)
     weighting = jnp.sum(placed * gates[:, :, None], axis=1)
     quarter = tokens.shape[1]
-    rows = jnp.einsum(
-        "tr,td->rd",
-        membership.astype(jnp.bfloat16),
-        tokens,
-        preferred_element_type=jnp.float32,
+    both = jnp.einsum(
+        "ktr,ktd->krd",
+        jnp.stack([membership, weighting]),
+        jnp.stack([tokens, cotangent]).astype(jnp.float32),
+        precision=highest,
     ).astype(jnp.bfloat16)
-    scaled = jnp.einsum(
-        "tr,td->rd", weighting, cotangent.astype(jnp.float32), precision=highest
-    ).astype(jnp.bfloat16)
+    rows, scaled = both[0], both[1]
     rows = rows.reshape(devices, local_experts, capacity, quarter)
     scaled = scaled.reshape(devices, local_experts, capacity, quarter)
     step = capacity // CHUNKS

time: 310 us -> 311 us (level)
  the two profiles are of different devices: /device:TPU:7 before, /device:TPU:32 now
where the time goes in v11:
time: 311 us; the launch traced here: 307 us
  Pallas kernels  136 us (44%)
  waiting for transfers between devices  77.2 us (25%)
  local copies, waits for them, and re-layouts  32.9 us (11%)
  matrix products  32.3 us (10%)
  between operations  14.7 us (5%)
  other arithmetic  12.7 us (4%)
    pallas_call x4, Pallas kernels, expert_all_to_all(): pl.pallas_call(_a2a_kernel, out_shape=jax.ShapeDtypeStruct(x.shape, x.dty...  136 us
    all_gather x2, waiting for transfers between devices, expert_chunk(): whole = lax.all_gather(arrived, 'tensor', axis=3, tiled=True)  46.2 us
    reduce_scatter x2, waiting for transfers between devices, expert_chunk(): sums = lax.psum_scatter(parts, 'tensor', scatter_dimension=3, tiled=True)  30.9 us
    unnamed x50, local copies, waits for them, and re-layouts  12.4 us
    another operation x2, local copies, waits for them, and re-layouts  11.1 us
    dot_general x2, matrix products, expert_chunk(): jnp.einsum('nesh,nesd->ehd', hidden, expert_scaled, preferred_element_typ...  7.67 us
    dot_general x2, matrix products, expert_chunk(): jnp.einsum('nesd,nesh->edh', expert_rows, grad_preact, preferred_element_...  7.22 us
    concatenate x2, other arithmetic, expert_chunk(): jnp.concatenate([out_part.astype(jnp.bfloat16), grad_part.astype(jnp.bflo...  7.13 us
  transfers between devices with their start and end apart: 4, of which 4 were waited for; matrix products, arithmetic and copies ran while one was open for 19% of the time, Pallas kernels for 22%

profile of v11, /device:TPU:32, one launch (start us, length us, event | category | flops | bytes accessed | tf_op | source)
XLA Modules:
  0.0 306.7 jit_solution(13923520345012078015)
XLA Ops:
  10.0 1.9 gather_fusion
  12.7 1.8 convolution_convert_fusion.4
  17.8 35.8 %slot_chunk1.2 = bf16[64,8,1024]{2,1,0:T(8,128)(2,1)} custom-call(bf16[64,8,1024]{2,1,0:T(8,128)(2,1)} %maximum_bitcast_fusion.1.x_ref), custom_call_target="tpu_custom_call" | custom-call | bytes 2097152 | tf_op jit(solution)/shard_map/slot_chunk1/pallas_call | solution.py:65
  53.7 2.7 maximum_bitcast_fusion.x_ref
  56.4 32.8 %slot_chunk0.2 = bf16[64,8,1024]{2,1,0:T(8,128)(2,1)} custom-call(bf16[64,8,1024]{2,1,0:T(8,128)(2,1)} %maximum_bitcast_fusion.x_ref), custom_call_target="tpu_custom_call" | custom-call | bytes 2097152 | tf_op jit(solution)/shard_map/slot_chunk0/pallas_call | solution.py:65
  89.5 13.7 %all-gather.7.cloned.1.call-done = bf16[64,8,4096]{2,1,0:T(8,128)(2,1)} async-done(((bf16[64,8,1024]{2,1,0:T(8,128)(2,1)}), bf16[64,8,4096]{2,1,0:T(8,128)(2,1)}) %all-gather.7.cloned.1.call-update) | async-done | bytes 4194320 | tf_op jit(solution)/shard_map/slot_chunk1/all_gather | solution.py:86
  103.2 5.6 %slice_bitcast_fusion.1 = (bf16[64,4,4096]{2,1,0:T(4,128)(2,1)S(1)}, bf16[64,4,4096]{2,1,0:T(4,128)(2,1)S(1)}) fusion(bf16[64,1,8,4096]{3,2,0,1:T(8,128)(2,1)} %bitcast.197), kind=kLoop, calls=%fused_computation.30 | loop fusion | bytes 8388608 | tf_op jit(solution)/shard_map/reshape.30
  108.8 1.8 fusion.31
  119.9 3.4 %pad_maximum_fusion.1 = bf16[64,1,8,4096]{3,2,0,1:T(8,128)(2,1)} fusion(bf16[64,1,4,4096]{3,2,0,1:T(4,128)(2,1)S(1)} %bitcast.192, bf16[64,1,4,4096]{3,2,0,1:T(4,128)(2,1)S(1)} %bitcast.194), kind=kLoop, calls=%fused_computation.12 | loop fusion | flops 8388608 | bytes 8388608 | tf_op jit(solution)/shard_map/slot_chunk1/concatenate | solution.py:106
  123.6 32.5 %all-gather.5.cloned.1.call-done = bf16[64,8,4096]{2,1,0:T(8,128)(2,1)} async-done(((bf16[64,8,1024]{2,1,0:T(8,128)(2,1)}), bf16[64,8,4096]{2,1,0:T(8,128)(2,1)}) %all-gather.5.cloned.1.call-update) | async-done | bytes 4194320 | tf_op jit(solution)/shard_map/slot_chunk0/all_gather | solution.py:86
  156.2 5.5 %slice_bitcast_fusion.3 = (bf16[64,4,4096]{2,1,0:T(4,128)(2,1)S(1)}, bf16[64,4,4096]{2,1,0:T(4,128)(2,1)S(1)}) fusion(bf16[64,1,8,4096]{3,2,0,1:T(8,128)(2,1)} %bitcast.196), kind=kLoop, calls=%fused_computation.32 | loop fusion | bytes 8388608 | tf_op jit(solution)/shard_map/reshape.4
  161.7 1.8 fusion.26
  165.3 1.8 fusion.81
  172.9 3.7 %pad_maximum_fusion = bf16[64,1,8,4096]{3,2,0,1:T(8,128)(2,1)} fusion(bf16[64,1,4,4096]{3,2,0,1:T(4,128)(2,1)S(1)} %bitcast.193, bf16[64,1,4,4096]{3,2,0,1:T(4,128)(2,1)S(1)} %bitcast.195), kind=kLoop, calls=%fused_computation.11 | loop fusion | flops 8388608 | bytes 8388608 | tf_op jit(solution)/shard_map/slot_chunk0/concatenate | solution.py:106
  177.6 3.5 %fusion.23 = f32[4096,384,1]{1,0,2:T(8,128)S(1)} fusion(bf16[64,4,384]{2,0,1:T(8,128)(2,1)S(1)} %copy-done.12, bf16[64,4,4096]{2,1,0:T(4,128)(2,1)} %copy-done.8), kind=kOutput, calls=%fused_computation.41 | convolution fusion | flops 805306368 | bytes 8585216 | tf_op jit(solution)/shard_map/slot_chunk0/nesd,nesh->edh/dot_general | solution.py:102
  181.1 2.9 fusion.20
  184.1 3.7 %fusion.2 = bf16[1,4096,384]{2,1,0:T(8,128)(2,1)} fusion(bf16[64,4,384]{2,0,1:T(8,128)(2,1)S(1)} %fusion.76, f32[4096,384,1]{1,0,2:T(8,128)S(1)} %fusion.23, bf16[64,4,4096]{2,1,0:T(4,128)(2,1)S(1)} %copy-done.5), kind=kOutput, calls=%fused_computation.9 | convolution fusion | flops 808452096 | bytes 11730944 | tf_op jit(solution)/shard_map/slot_chunk1/nesd,nesh->edh/dot_general | solution.py:102
  187.8 4.8 %fusion.3 = bf16[1,384,4096]{2,1,0:T(8,128)(2,1)} fusion(f32[384,4096,1]{1,0,2:T(8,128)S(1)} %fusion.20, bf16[64,4,4096]{2,1,0:T(4,128)(2,1)S(1)} %copy-done.3, f32[64,1,4,384]{3,0,2,1:T(8,128)S(1)} %copy-done.19), kind=kOutput, calls=%fused_computation.10 | convolution fusion | flops 808943616 | bytes 11927552 | tf_op jit(solution)/shard_map/slot_chunk1/nesh,nesd->ehd/dot_general | solution.py:99
  192.6 15.9 %reduce-scatter.5.cloned.1.call-done = bf16[64,1,8,1024]{3,2,0,1:T(8,128)(2,1)} async-done(((bf16[64,1,8,4096]{3,2,0,1:T(8,128)(2,1)}), bf16[64,1,8,1024]{3,2,0,1:T(8,128)(2,1)}) %reduce-scatter.5.cloned.1.call-update) | async-done | bytes 1048592 | tf_op jit(solution)/shard_map/slot_chunk1/reduce_scatter | solution.py:109
  208.5 33.8 %slot_chunk1.3 = bf16[64,8,1024]{2,1,0:T(8,128)(2,1)} custom-call(bf16[64,8,1024]{2,1,0:T(8,128)(2,1)} %bitcast.200), custom_call_target="tpu_custom_call" | custom-call | bytes 2097152 | tf_op jit(solution)/shard_map/slot_chunk1/pallas_call | solution.py:65
  242.2 3.0 fusion.105
  245.2 15.0 %reduce-scatter.3.cloned.1.call-done = bf16[64,1,8,1024]{3,2,0,1:T(8,128)(2,1)} async-done(((bf16[64,1,8,4096]{3,2,0,1:T(8,128)(2,1)}), bf16[64,1,8,1024]{3,2,0,1:T(8,128)(2,1)}) %reduce-scatter.3.cloned.1.call-update) | async-done | bytes 1048592 | tf_op jit(solution)/shard_map/slot_chunk0/reduce_scatter | solution.py:109
  260.2 34.1 %slot_chunk0.3 = bf16[64,8,1024]{2,1,0:T(8,128)(2,1)} custom-call(bf16[64,8,1024]{2,1,0:T(8,128)(2,1)} %bitcast.201), custom_call_target="tpu_custom_call" | custom-call | bytes 2097152 | tf_op jit(solution)/shard_map/slot_chunk0/pallas_call | solution.py:65
  294.3 2.1 fusion.104
  (79 shorter events, 28.3 us)
Async XLA Ops:
  7.2 101.6 %copy-start = (bf16[1,4096,384]{2,1,0:T(8,128)(2,1)S(1)}, bf16[1,4096,384]{2,1,0:T(8,128)(2,1)}, u32[]{:S(2)}) copy-start(bf16[1,4096,384]{2,1,0:T(8,128)(2,1)} %param.10) | copy-start | bytes 9437188
  7.2 96.0 %all-gather.7.cloned.1.call-start = ((), (), s32[]{:S(2)}) async-start(), calls=%async_computation.5 | async-start | bytes 5242880 | tf_op jit(solution)/shard_map/slot_chunk1/all_gather | solution.py:86
  10.0 2.1 copy-start.15
  10.0 2.6 copy-start.13
  10.0 2.6 copy-start.14
  53.7 102.5 %all-gather.5.cloned.1.call-start = ((), (), s32[]{:S(2)}) async-start(), calls=%async_computation.4 | async-start | bytes 5242880 | tf_op jit(solution)/shard_map/slot_chunk0/all_gather | solution.py:86
  89.3 119.2 %reduce-scatter.5.cloned.1.call-start = ((), (), s32[]{:S(2)}) async-start(), calls=%async_computation.3 | async-start | bytes 5242880 | tf_op jit(solution)/shard_map/slot_chunk1/reduce_scatter | solution.py:109
  108.7 1.9 copy-start.4
  108.7 2.1 copy-start.2
  108.8 3.5 %copy-start.16 = (bf16[1,384,4096]{2,1,0:T(8,128)(2,1)S(1)}, bf16[1,384,4096]{2,1,0:T(8,128)(2,1)}, u32[]{:S(2)}) copy-start(bf16[1,384,4096]{2,1,0:T(8,128)(2,1)} %param.11) | copy-start | bytes 9437188
  110.6 6.4 %copy-start.18 = (f32[64,1,4,384]{3,0,2,1:T(8,128)}, f32[64,1,4,384]{3,0,2,1:T(8,128)S(1)}, u32[]{:S(2)}) copy-start(f32[64,1,4,384]{3,0,2,1:T(8,128)S(1)} %fusion.31) | copy-start | bytes 1179652
  123.4 136.8 %reduce-scatter.3.cloned.1.call-start = ((), (), s32[]{:S(2)}) async-start(), calls=%async_computation.2 | async-start | bytes 5242880 | tf_op jit(solution)/shard_map/slot_chunk0/reduce_scatter | solution.py:109
  161.7 1.9 copy-start.8
  161.7 2.1 copy-start.6
  161.7 3.5 %copy-start.17 = (bf16[1,384,4096]{2,1,0:T(8,128)(2,1)S(1)}, bf16[1,384,4096]{2,1,0:T(8,128)(2,1)}, u32[]{:S(2)}) copy-start(bf16[1,384,4096]{2,1,0:T(8,128)(2,1)} %param.11) | copy-start | bytes 9437188
  163.6 6.4 %copy-start.20 = (f32[64,1,4,384]{3,0,2,1:T(8,128)}, f32[64,1,4,384]{3,0,2,1:T(8,128)S(1)}, u32[]{:S(2)}) copy-start(f32[64,1,4,384]{3,0,2,1:T(8,128)S(1)} %fusion.26) | copy-start | bytes 1179652
  177.6 3.5 %copy-start.7 = (bf16[64,4,4096]{2,1,0:T(4,128)(2,1)S(1)}, bf16[64,4,4096]{2,1,0:T(4,128)(2,1)}, u32[]{:S(2)}) copy-start(bf16[64,4,4096]{2,1,0:T(4,128)(2,1)} %copy-done.6) | copy-start | bytes 6291460
  177.6 3.5 %copy-start.21 = (f32[64,1,4,384]{3,0,2,1:T(8,128)S(1)}, f32[64,1,4,384]{3,0,2,1:T(8,128)}, u32[]{:S(2)}) copy-start(f32[64,1,4,384]{3,0,2,1:T(8,128)} %copy-done.20) | copy-start | bytes 1179652
  181.1 2.9 copy-start.5
  184.0 3.7 %copy-start.3 = (bf16[64,4,4096]{2,1,0:T(4,128)(2,1)S(1)}, bf16[64,4,4096]{2,1,0:T(4,128)(2,1)}, u32[]{:S(2)}) copy-start(bf16[64,4,4096]{2,1,0:T(4,128)(2,1)} %copy-done.2) | copy-start | bytes 6291460
  184.0 3.7 %copy-start.19 = (f32[64,1,4,384]{3,0,2,1:T(8,128)S(1)}, f32[64,1,4,384]{3,0,2,1:T(8,128)}, u32[]{:S(2)}) copy-start(f32[64,1,4,384]{3,0,2,1:T(8,128)} %copy-done.18) | copy-start | bytes 1179652
  294.3 2.2 copy-start.10
  294.3 3.8 %copy-start.9 = (bf16[64,1,4,1024]{3,2,0,1:T(4,128)(2,1)S(1)}, bf16[64,1,4,1024]{3,2,0,1:T(4,128)(2,1)}, u32[]{:S(2)}) copy-start(bf16[64,1,4,1024]{3,2,0,1:T(4,128)(2,1)} %get-tuple-element.14) | copy-start | bytes 1572868
  294.3 5.4 %copy-start.1 = (bf16[1,4096,384]{2,1,0:T(8,128)(2,1)S(1)}, bf16[1,4096,384]{2,1,0:T(8,128)(2,1)}, u32[]{:S(2)}) copy-start(bf16[1,4096,384]{2,1,0:T(8,128)(2,1)} %param.10) | copy-start | bytes 9437188
  (2 other events, 2.2 us)
Sparse Core Ops, SparseCore 0:
  53.8 49.2 all-gather.6
  105.0 51.1 all-gather.4
  158.7 49.7 reduce-scatter.4
  211.0 49.1 reduce-scatter.2
